TPU v7x, 32 devices: a whole 2x2x4 slice. The times are simulated.
32 devices in a mesh: tile: 8 (over z, y), rec: 4 (over x, core).
Axes of the slice: x: 2, y: 2, z: 4, core: 2. Of those that a mesh axis runs over, the one named last changes fastest.
Arguments:
- screens: bfloat16 [2, 384, 128, 128], P(None, 'tile', 'rec'), may hold values from -1.796875 to 1.796875
- tile_owner: int32 [2, 2, 1024, 1], replicated, may hold values from 0 to 7; in each aligned block of 128 rows (0 to 127, 128 to 255, ..., all dimensions but the last counted through in order) at most 24 rows name the same one
- tile_slot: int32 [2, 2, 1024], replicated, may hold values from 0 to 47
- commands_init: float32 [4096], P('rec'), may hold values from -1.2 to 1.2
- reconstructor: bfloat16 [32, 16, 128, 128], P('rec', 'tile'), may hold values from -1 to 1
- pattern: int32 [32, 16], P('rec', 'tile'), may hold values from 0 to 31
Outputs:
- lgs_slopes: float32 [2, 32, 128], P(None, 'tile', 'rec')
- science_residual: bfloat16 [2, 992, 128, 128], P(None, 'tile', 'rec')
- commands: float32 [4096], P('rec')
Inputs may be any that keep to these rules, and one draw needn't show every extreme that they name: `tile_owner`: within the 128 consecutive entries of one index of tile for one frame and layer, each holder is named at most 24 times; in every frame and layer some such entries name one holder exactly 24 times.
All inputs are finite; a program needn't handle non-finite values.
Results may differ from a plain program's by a relative error of at most 0.011.
Values may be sent and summed in bfloat16 or wider, within the bound.
No kernel may reach another device: no remote copies, remote signals or barrier semaphores. Data moves between devices by JAX's collectives and lax.ppermute only.
A program may use at most 64 MiB of HBM per device.

v0:
```python
import math

import jax
import jax.numpy as jnp
from jax import lax
from jax.sharding import PartitionSpec as P

SUBPX = 16
SPOT = 32
SUB = 8
PT = 64
LG_DEV = 4
SC_DEV = 124


loop_gain = 0.5


def influence(tile_px, sub_px, sub_count):
    pixel = jnp.arange(tile_px, dtype=jnp.float32)[:, None] + 0.5
    centre = (jnp.arange(sub_count, dtype=jnp.float32)[None, :] + 0.5) * sub_px
    return jnp.maximum(0.0, 1.0 - jnp.abs(pixel - centre) / sub_px)


def tables(spot_px, sub_px):
    freq = jnp.arange(spot_px, dtype=jnp.int32)[:, None]
    pixel = jnp.arange(sub_px, dtype=jnp.int32)[None, :]
    turns = (freq * pixel % spot_px).astype(jnp.float32) * (2.0 * math.pi / spot_px)
    return (jnp.cos(turns).astype(jnp.bfloat16), jnp.sin(turns).astype(jnp.bfloat16))


def centred(spot_px):
    index = jnp.arange(spot_px, dtype=jnp.int32)
    return ((index + spot_px // 2) % spot_px - spot_px // 2).astype(jnp.float32) / spot_px


def along_pixels(values, table):
    return jnp.einsum("iaubv,nv->iaubn", values, table, preferred_element_type=jnp.float32)


def along_rows(table, values):
    return jnp.einsum("mu,iaubn->iabmn", table, values, preferred_element_type=jnp.float32)


def spot_slopes(residual):
    item_count, row_px, col_px = residual.shape
    sub_rows = row_px // SUBPX
    sub_cols = col_px // SUBPX
    cos_t, sin_t = tables(SPOT, SUBPX)
    pieces = residual.reshape(item_count, sub_rows, SUBPX, sub_cols, SUBPX)
    real_part = jnp.cos(pieces).astype(jnp.bfloat16)
    imag_part = jnp.sin(pieces).astype(jnp.bfloat16)
    g_re = (along_pixels(real_part, cos_t) + along_pixels(imag_part, sin_t)).astype(jnp.bfloat16)
    g_im = (along_pixels(imag_part, cos_t) - along_pixels(real_part, sin_t)).astype(jnp.bfloat16)
    h_re = along_rows(cos_t, g_re) + along_rows(sin_t, g_im)
    h_im = along_rows(cos_t, g_im) - along_rows(sin_t, g_re)
    spots = h_re * h_re + h_im * h_im
    coords = centred(SPOT)
    totals = jnp.sum(spots, axis=(3, 4))
    slope_x = jnp.sum(spots * coords[None, None, None, None, :], axis=(3, 4)) / totals
    slope_y = jnp.sum(spots * coords[None, None, None, :, None], axis=(3, 4)) / totals
    return jnp.stack([slope_x, slope_y], axis=-1).reshape(item_count, sub_rows * sub_cols * 2)


def pack_tiles(screens, owners, slots, pairs, my_tile, capacity):
    packed = []
    places = jnp.arange(capacity, dtype=jnp.int32)
    for frame, layer_idx in pairs:
        owner_rows = owners[frame, layer_idx]
        slot_rows = slots[frame, layer_idx]
        mine = owner_rows == my_tile
        order = jnp.cumsum(mine.astype(jnp.int32), axis=1) - 1
        picked = mine[:, None, :] & (order[:, None, :] == places[None, :, None])
        wanted = jnp.sum(jnp.where(picked, slot_rows[:, None, :], 0), axis=2)
        packed.append(jnp.take(screens[layer_idx], wanted, axis=0))
    return jnp.stack(packed, axis=1)


def unpack_tiles(received, owners, pairs, my_tile, capacity):
    results = []
    item_count = owners.shape[3]
    later = jnp.arange(item_count, dtype=jnp.int32)
    earlier_mask = later[None, :] < later[:, None]
    for position in range(len(pairs)):
        frame, layer_idx = pairs[position]
        mine = lax.dynamic_index_in_dim(owners[frame, layer_idx], my_tile, 0, keepdims=False)
        same_owner = mine[:, None] == mine[None, :]
        order = jnp.sum((same_owner & earlier_mask).astype(jnp.int32), axis=1)
        flat_index = mine * capacity + order
        layer_tiles = received[:, position].reshape(-1, received.shape[3], received.shape[4])
        results.append(jnp.take(layer_tiles, flat_index, axis=0).astype(jnp.float32))
    return results


def add_layers(pieces, first_index):
    phase = pieces[first_index]
    phase = phase + pieces[first_index + 1]
    return phase


def per_device(screens, tile_owner, tile_slot, commands_init, reconstructor, pattern):
    layer_total, tiles_here, slab_rows, tile_px = screens.shape
    frame_total = tile_owner.shape[0]
    tile_count = lax.axis_size("tile")
    rec_count = lax.axis_size("rec")
    my_tile = lax.axis_index("tile")
    my_rec = lax.axis_index("rec")
    item_count = LG_DEV + SC_DEV
    capacity = max(2, 3 * item_count // (2 * tile_count))
    owners = tile_owner[..., 0].reshape(frame_total, layer_total, tile_count, item_count)
    slots = tile_slot.reshape(frame_total, layer_total, tile_count, item_count)
    influence_all = influence(tile_px, SUBPX, SUB)
    influence_rows = lax.dynamic_slice_in_dim(influence_all, my_rec * slab_rows, slab_rows, 0)
    lgs_places = (my_tile * LG_DEV + jnp.arange(LG_DEV, dtype=jnp.int32)) % PT
    sci_places = (my_tile * SC_DEV + jnp.arange(SC_DEV, dtype=jnp.int32)) % PT
    item_places = jnp.concatenate([lgs_places, sci_places])
    state = commands_init
    slope_frames = []
    science_frames = []
    for frame in range(frame_total):
        pairs = [(frame, layer_idx) for layer_idx in range(layer_total)]
        sending = pack_tiles(screens, owners, slots, pairs, my_tile, capacity)
        received = lax.all_to_all(sending, "tile", split_axis=0, concat_axis=0, tiled=True)
        pieces = unpack_tiles(received, owners, pairs, my_tile, capacity)
        phase = add_layers(pieces, 0)
        full_commands = lax.all_gather(state, "rec", axis=0, tiled=True)
        mirror = full_commands.reshape(PT, SUB, SUB)
        chosen = jnp.take(mirror, item_places, axis=0)
        shapes = jnp.einsum(
            "xa,iab,yb->ixy", influence_rows, chosen, influence_all, precision=lax.Precision.HIGHEST
        )
        residual = phase - shapes
        science_frames.append(residual[LG_DEV:].astype(jnp.bfloat16))
        slopes = spot_slopes(residual[:LG_DEV])
        slope_frames.append(slopes)
        slopes_b = slopes.astype(jnp.bfloat16)
        everyone = lax.all_gather(slopes_b[None], ("tile", "rec"), axis=0, tiled=True)
        everyone = everyone.reshape(tile_count, rec_count, LG_DEV, -1).transpose(0, 2, 1, 3)
        everyone = everyone.reshape(tile_count * LG_DEV, -1)
        needed = jnp.take(everyone, pattern, axis=0)
        partial_rows = jnp.einsum(
            "ibcs,ibs->ic", reconstructor, needed, preferred_element_type=jnp.float32
        ).reshape(-1)
        state = state + loop_gain * lax.psum(partial_rows, "tile")
    return (jnp.stack(slope_frames, axis=0), jnp.stack(science_frames, axis=0), state)


def solution(mesh):
    placed = (
        P(None, "tile", "rec", None),
        P(),
        P(),
        P("rec"),
        P("rec", "tile", None, None),
        P("rec", "tile"),
    )
    return jax.shard_map(
        per_device,
        mesh=mesh,
        in_specs=placed,
        out_specs=(P(None, "tile", "rec"), P(None, "tile", "rec", None), P("rec")),
        check_vma=False,
    )
```

profile of v0, /device:TPU:0, one launch (start us, length us, event | category | flops | bytes accessed | tf_op | source)
XLA Modules:
  0.0 293.3 jit_solution(11876869289070020217)
XLA Ops:
  0.6 0.8 reshape.281
  1.5 0.7 fusion.160
  2.2 0.3 reduce_window_sum.23
  2.5 0.3 reduce_window_sum.22
  2.8 0.3 select_reduce_fusion.2
  3.2 1.2 slice_bitcast_fusion.1
  4.5 0.9 gather_fusion.1
  5.4 1.4 select_bitcast_fusion.2
  6.9 0.9 gather_fusion
  7.8 0.3 select_bitcast_fusion.3
  8.1 1.1 copy-done.2
  9.2 2.0 pad_maximum_fusion
  11.2 7.3 %all-to-all-start = ((bf16[8,2,24,32,128]{4,3,2,1,0:T(8,128)(2,1)}), bf16[8,2,24,32,128]{4,3,2,1,0:T(8,128)(2,1)}, u32[]{:S(2)}, u32[]{:S(2)}) async-start(bf16[8,2,24,32,128]{4,3,2,1,0:T(8,128)(2,1)} %pad_maximum_fusion), calls=%async_computation | async-start | bytes 6291456 | tf_op jit(solution)/shard_map/all_to_all | solution.py:123
  18.4 0.3 reduce_window_sum.32
  18.7 0.3 reduce_window_sum.27
  19.0 0.3 select_reduce_fusion
  19.5 0.9 gather_fusion.6
  20.5 2.0 gather_fusion.5
  22.5 5.2 %all_gather.12 = f32[4096]{0:T(1024)S(1)} all-gather(f32[1024]{0:T(1024)S(1)} %copy-done.6), channel_id=1, replica_groups=mesh['tile'=8,'rec'=4] {'rec'}, dimensions={0}, use_global_device_ids=true | all-gather | bytes 20480 | tf_op jit(solution)/shard_map/all_gather | solution.py:126
  27.9 0.8 gather_fusion.4
  29.6 0.3 select_bitcast_fusion
  29.9 1.1 copy-done.1
  31.0 0.3 select_bitcast_fusion.1
  31.3 2.0 pad_maximum_fusion.1
  33.5 55.7 %all-to-all-done = bf16[8,2,24,32,128]{4,3,2,1,0:T(8,128)(2,1)} async-done(((bf16[8,2,24,32,128]{4,3,2,1,0:T(8,128)(2,1)}), bf16[8,2,24,32,128]{4,3,2,1,0:T(8,128)(2,1)}, u32[]{:S(2)}, u32[]{:S(2)}) %all-to-all-start) | async-done | bytes 3145760 | tf_op jit(solution)/shard_map/all_to_all | solution.py:123
  89.3 4.7 %all-to-all-start.1 = ((bf16[8,2,24,32,128]{4,3,2,1,0:T(8,128)(2,1)}), bf16[8,2,24,32,128]{4,3,2,1,0:T(8,128)(2,1)}, u32[]{:S(2)}, u32[]{:S(2)}) async-start(bf16[8,2,24,32,128]{4,3,2,1,0:T(8,128)(2,1)} %pad_maximum_fusion.1), calls=%async_computation.1 | async-start | bytes 6291456 | tf_op jit(solution)/shard_map/all_to_all | solution.py:123
  94.5 0.4 fusion.54
  94.9 3.7 %fusion.164 = (bf16[8,1,24,32,128]{4,3,2,1,0:T(8,128)(2,1)S(1)}, bf16[8,1,24,32,128]{4,3,2,1,0:T(8,128)(2,1)}) fusion(bf16[8,2,24,32,128]{4,3,2,1,0:T(8,128)(2,1)} %all-to-all-done), kind=kLoop, calls=%fused_computation.284 | loop fusion | bytes 6291456 | tf_op jit(solution)/shard_map/slice | solution.py:90
  98.6 2.2 gather_fusion.3
  100.8 1.7 gather_fusion.2
  102.5 5.7 %add_subtract_fusion.1 = f32[128,32,128]{2,0,1:T(8,128)S(1)} fusion(bf16[128,32,128]{2,1,0:T(8,128)(2,1)S(1)} %gather_fusion.3, bf16[128,32,128]{2,1,0:T(8,128)(2,1)} %gather_fusion.2, pred[128]{0:T(512)(128)(4,1)S(1)} %get-tuple-element.29, pred[128]{0:T(512)(128)(4,1)S(1)} %get-tuple-element.73, f32[128,8,32]{0,2,1:T(8,128)S(1)} %fusion.54, ...), kind=kOutput, calls=%fused_computation.18 | convolution fusion | flops 53482496 | bytes 4326176 | tf_op jit(solution)/shard_map/xa,iab,yb->ixy/dot_general | solution.py:129
  108.1 0.5 cosine_convert_fusion.1
  108.6 0.9 copy-done.3
  110.5 0.3 fusion.9
  111.0 0.4 fusion.70
  111.4 0.4 fusion.73
  111.8 0.4 fusion.2
  112.1 0.9 multiply_reduce_fusion.3
  113.4 65.9 %all_gather.13 = bf16[32,4,32]{2,1,0:T(4,128)(2,1)S(1)} all-gather(bf16[1,4,32]{2,1,0:T(4,128)(2,1)S(1)} %copy.90), channel_id=1, replica_groups=mesh['tile'=8,'rec'=4] {'tile','rec'}, dimensions={0}, use_global_device_ids=true | all-gather | bytes 8448 | tf_op jit(solution)/shard_map/all_gather | solution.py:137
  179.4 0.6 gather_fusion.9
  180.3 26.0 %psum.14 = f32[1024]{0:T(1024)S(1)} all-reduce(f32[1024]{0:T(1024)S(1)} %bitcast.175), channel_id=1, replica_groups=mesh['tile'=8,'rec'=4] {'tile'}, use_global_device_ids=true, to_apply=%region_15.20 | all-reduce | flops 1024 | bytes 8192 | tf_op jit(solution)/shard_map/psum | solution.py:144
  206.3 5.4 %all_gather.14 = f32[4096]{0:T(1024)S(1)} all-gather(f32[1024]{0:T(1024)S(1)} %multiply_add_fusion.1), channel_id=1, replica_groups=mesh['tile'=8,'rec'=4] {'rec'}, dimensions={0}, use_global_device_ids=true | all-gather | bytes 20480 | tf_op jit(solution)/shard_map/all_gather | solution.py:126
  211.9 0.8 gather_fusion.10
  213.1 0.4 fusion.52
  213.5 3.7 %fusion.165 = (bf16[8,1,24,32,128]{4,3,2,1,0:T(8,128)(2,1)S(1)}, bf16[8,1,24,32,128]{4,3,2,1,0:T(8,128)(2,1)}) fusion(bf16[8,2,24,32,128]{4,3,2,1,0:T(8,128)(2,1)} %all-to-all-done.1), kind=kLoop, calls=%fused_computation.285 | loop fusion | bytes 6291456 | tf_op jit(solution)/shard_map/slice | solution.py:90
  217.2 2.2 gather_fusion.8
  219.4 1.7 gather_fusion.7
  221.0 5.7 %add_subtract_fusion = f32[128,32,128]{2,0,1:T(8,128)S(1)} fusion(bf16[128,32,128]{2,1,0:T(8,128)(2,1)S(1)} %gather_fusion.8, bf16[128,32,128]{2,1,0:T(8,128)(2,1)} %gather_fusion.7, pred[128]{0:T(512)(128)(4,1)S(1)} %get-tuple-element.37, pred[128]{0:T(512)(128)(4,1)S(1)} %get-tuple-element.71, f32[128,8,32]{0,2,1:T(8,128)S(1)} %fusion.52, ...), kind=kOutput, calls=%fused_computation.17 | convolution fusion | flops 53482496 | bytes 4326176 | tf_op jit(solution)/shard_map/xa,iab,yb->ixy/dot_general | solution.py:129
  226.7 0.5 cosine_convert_fusion
  227.2 0.3 fusion.13
  227.5 0.8 copy-done.4
  228.8 1.1 fusion.14
  230.3 1.3 fusion.11
  231.6 0.4 fusion.64
  232.0 0.3 fusion.10
  232.3 0.4 fusion.67
  232.7 0.4 fusion
  233.1 0.9 multiply_reduce_fusion.1
  234.4 2.6 copy.106
  237.1 36.8 %all_gather.15 = bf16[32,4,32]{2,1,0:T(4,128)(2,1)S(1)} all-gather(bf16[1,4,32]{2,1,0:T(4,128)(2,1)S(1)} %copy.103), channel_id=1, replica_groups=mesh['tile'=8,'rec'=4] {'tile','rec'}, dimensions={0}, use_global_device_ids=true | all-gather | bytes 8448 | tf_op jit(solution)/shard_map/all_gather | solution.py:137
  274.1 0.6 gather_fusion.11
  275.0 17.1 %psum.15 = f32[1024]{0:T(1024)S(1)} all-reduce(f32[1024]{0:T(1024)S(1)} %bitcast.176), channel_id=1, replica_groups=mesh['tile'=8,'rec'=4] {'tile'}, use_global_device_ids=true, to_apply=%region_19.24 | all-reduce | flops 1024 | bytes 8192 | tf_op jit(solution)/shard_map/psum | solution.py:144
  292.1 0.6 multiply_add_fusion
  292.7 0.6 pad_maximum_fusion.5
  (100 shorter events, 6.6 us)
Async XLA Ops:
  0.6 179.4 %copy-start = (bf16[8,2,128,128]{3,2,1,0:T(8,128)(2,1)S(1)}, bf16[8,2,128,128]{3,2,1,0:T(8,128)(2,1)}, u32[]{:S(2)}) copy-start(bf16[8,2,128,128]{3,2,1,0:T(8,128)(2,1)} %param.18) | copy-start | bytes 1572868
  7.8 1.4 copy-start.2
  11.2 78.1 %all-to-all-start = ((bf16[8,2,24,32,128]{4,3,2,1,0:T(8,128)(2,1)}), bf16[8,2,24,32,128]{4,3,2,1,0:T(8,128)(2,1)}, u32[]{:S(2)}, u32[]{:S(2)}) async-start(bf16[8,2,24,32,128]{4,3,2,1,0:T(8,128)(2,1)} %pad_maximum_fusion), calls=%async_computation | async-start | bytes 6291456 | tf_op jit(solution)/shard_map/all_to_all | solution.py:123
  20.5 2.0 copy-start.6
  20.5 8.3 %copy-start.5 = (s32[2,2,1024,1]{2,3,1,0:T(1,128)S(1)}, s32[2,2,1024,1]{2,3,1,0:T(1,128)}, u32[]{:S(2)}) copy-start(s32[2,2,1024,1]{2,3,1,0:T(1,128)} %param.15) | copy-start | bytes 49156
  29.6 1.4 copy-start.1
  31.3 2.0 copy-start.7
  89.3 124.2 %all-to-all-start.1 = ((bf16[8,2,24,32,128]{4,3,2,1,0:T(8,128)(2,1)}), bf16[8,2,24,32,128]{4,3,2,1,0:T(8,128)(2,1)}, u32[]{:S(2)}, u32[]{:S(2)}) async-start(bf16[8,2,24,32,128]{4,3,2,1,0:T(8,128)(2,1)} %pad_maximum_fusion.1), calls=%async_computation.1 | async-start | bytes 6291456 | tf_op jit(solution)/shard_map/all_to_all | solution.py:123
  108.1 1.4 copy-start.3
  226.7 1.6 copy-start.4
where the time goes:
time: 294 us; the launch traced here: 293 us
  blocking collectives  156 us (53%)
  waiting for transfers between devices  55.7 us (19%)
  local copies, waits for them, and re-layouts  34.4 us (12%)
  matrix products  20.7 us (7%)
  other arithmetic  12.8 us (4%)
  starting transfers between devices  11.9 us (4%)
    all_gather x2, blocking collectives, per_device(): lax.all_gather(slopes_b[None], ('tile', 'rec'), axis=0, tiled=True)  103 us
    all_to_all x2, waiting for transfers between devices, per_device(): lax.all_to_all(sending, 'tile', split_axis=0, concat_axis=0, tiled=True)  55.7 us
    psum x2, blocking collectives, per_device(): state = state + loop_gain * lax.psum(partial_rows, 'tile')  43.2 us
    dot_general x4, matrix products, per_device(): jnp.einsum('xa,iab,yb->ixy', influence_rows, chosen, influence_all, preci...  12.2 us
    all_to_all x2, starting transfers between devices, per_device(): lax.all_to_all(sending, 'tile', split_axis=0, concat_axis=0, tiled=True)  11.9 us
    all_gather x2, blocking collectives, per_device(): full_commands = lax.all_gather(state, 'rec', axis=0, tiled=True)  10.6 us
    gather x4, local copies, waits for them, and re-layouts, unpack_tiles(): jnp.take(layer_tiles, flat_index, axis=0).astype(jnp.float32)  7.65 us
    slice x2, local copies, waits for them, and re-layouts, unpack_tiles(): received[:, position].reshape(-1, received.shape[3], received.shape[4])  7.41 us
  transfers between devices with their start and end apart: 2, of which 1 were waited for; matrix products, arithmetic and copies ran while one was open for 10% of the time, Pallas kernels for 0%

commit v1 on v0

--- a/solution.py
+++ b/solution.py
@@ -1,8 +1,13 @@
+import functools
 import math
 
 import jax
 import jax.numpy as jnp
+import ml_dtypes
+import numpy as np
 from jax import lax
+from jax.experimental import pallas as pl
+from jax.experimental.pallas import tpu as pltpu
 from jax.sharding import PartitionSpec as P
 
 SUBPX = 16
@@ -11,7 +16,9 @@
 PT = 64
 LG_DEV = 4
 SC_DEV = 124
-
+ITEMS = LG_DEV + SC_DEV
+LANES = 128
+CMD = SUB * SUB
 
 loop_gain = 0.5
 
@@ -92,23 +99,16 @@
     return results
 
 
-def add_layers(pieces, first_index):
-    phase = pieces[first_index]
-    phase = phase + pieces[first_index + 1]
-    return phase
-
-
-def per_device(screens, tile_owner, tile_slot, commands_init, reconstructor, pattern):
+def by_request(screens, tile_owner, tile_slot, commands_init, reconstructor, pattern):
     layer_total, tiles_here, slab_rows, tile_px = screens.shape
     frame_total = tile_owner.shape[0]
     tile_count = lax.axis_size("tile")
     rec_count = lax.axis_size("rec")
     my_tile = lax.axis_index("tile")
     my_rec = lax.axis_index("rec")
-    item_count = LG_DEV + SC_DEV
-    capacity = max(2, 3 * item_count // (2 * tile_count))
-    owners = tile_owner[..., 0].reshape(frame_total, layer_total, tile_count, item_count)
-    slots = tile_slot.reshape(frame_total, layer_total, tile_count, item_count)
+    capacity = max(2, 3 * ITEMS // (2 * tile_count))
+    owners = tile_owner[..., 0].reshape(frame_total, layer_total, tile_count, ITEMS)
+    slots = tile_slot.reshape(frame_total, layer_total, tile_count, ITEMS)
     influence_all = influence(tile_px, SUBPX, SUB)
     influence_rows = lax.dynamic_slice_in_dim(influence_all, my_rec * slab_rows, slab_rows, 0)
     lgs_places = (my_tile * LG_DEV + jnp.arange(LG_DEV, dtype=jnp.int32)) % PT
@@ -122,7 +122,7 @@
         sending = pack_tiles(screens, owners, slots, pairs, my_tile, capacity)
         received = lax.all_to_all(sending, "tile", split_axis=0, concat_axis=0, tiled=True)
         pieces = unpack_tiles(received, owners, pairs, my_tile, capacity)
-        phase = add_layers(pieces, 0)
+        phase = functools.reduce(jnp.add, pieces)
         full_commands = lax.all_gather(state, "rec", axis=0, tiled=True)
         mirror = full_commands.reshape(PT, SUB, SUB)
         chosen = jnp.take(mirror, item_places, axis=0)
@@ -145,6 +145,340 @@
     return (jnp.stack(slope_frames, axis=0), jnp.stack(science_frames, axis=0), state)
 
 
+def vmem():
+    return pl.BlockSpec(memory_space=pltpu.VMEM)
+
+
+def smem():
+    return pl.BlockSpec(memory_space=pltpu.SMEM)
+
+
+def constant_tables(slab_rows):
+    f32, bf16 = np.float32, ml_dtypes.bfloat16
+    turns = (np.arange(SPOT)[:, None] * np.arange(SUBPX)[None, :] % SPOT).astype(f32)
+    turns = turns * f32(2.0 * math.pi / SPOT)
+    cos_t, sin_t = np.cos(turns).astype(bf16).astype(f32), np.sin(turns).astype(bf16).astype(f32)
+    cols = LANES // SUBPX
+    eye_c = np.eye(cols, dtype=f32)
+    cos_v, sin_v = np.kron(eye_c, cos_t.T), np.kron(eye_c, sin_t.T)
+    along_v = np.block([[cos_v, -sin_v], [sin_v, cos_v]])
+    rows = LG_DEV * slab_rows // SUBPX
+    eye_r = np.eye(rows, dtype=f32)
+    cos_u, sin_u = np.kron(eye_r, cos_t), np.kron(eye_r, sin_t)
+    along_u = np.block([[cos_u, sin_u], [-sin_u, cos_u]])
+    index = np.arange(SPOT)
+    coord = (((index + SPOT // 2) % SPOT) - SPOT // 2).astype(f32) / SPOT
+    groups = LANES // (2 * cols)
+    total_n = np.zeros((cols, SPOT, groups, cols, 2), f32)
+    coord_n = np.zeros((cols, SPOT, groups, cols, 2), f32)
+    for b in range(cols):
+        total_n[b, :, :, b, :] = 1.0
+        coord_n[b, :, :, b, 0] = coord[:, None]
+    over_n = np.concatenate([t.reshape(cols * SPOT, LANES) for t in (total_n, coord_n)], axis=1)
+    sub_rows = slab_rows // SUBPX
+    total_m = np.zeros((sub_rows, LG_DEV, LG_DEV, sub_rows, SPOT), f32)
+    coord_m = np.zeros((sub_rows, LG_DEV, LG_DEV, sub_rows, SPOT), f32)
+    for a in range(sub_rows):
+        for i in range(LG_DEV):
+            total_m[a, i, i, a, :] = 1.0
+            coord_m[a, i, i, a, :] = coord
+    over_m = np.concatenate([t.reshape(rows, rows * SPOT) for t in (total_m, coord_m)], axis=0)
+    pixel = np.arange(LANES, dtype=f32)[:, None] + f32(0.5)
+    centre = (np.arange(SUB, dtype=f32)[None, :] + f32(0.5)) * SUBPX
+    infl = np.maximum(f32(0.0), f32(1.0) - np.abs(pixel - centre) / f32(SUBPX))
+    per_row = LANES // CMD
+    spread = np.tile(infl.T, (per_row * SUB, 1))
+    keep = np.kron(np.eye(per_row * SUB, dtype=f32), np.ones((1, SUB), f32))
+    return dict(
+        along_v=along_v.astype(bf16),
+        along_u=along_u.astype(bf16),
+        over_n=over_n.astype(bf16),
+        over_m=over_m.astype(bf16),
+        spread=spread,
+        keep=keep,
+    )
+
+
+def split_dot(exact, wide, left):
+    high = wide.astype(jnp.bfloat16)
+    low = (wide - high.astype(jnp.float32)).astype(jnp.bfloat16)
+    dot = functools.partial(jnp.dot, preferred_element_type=jnp.float32)
+    if left:
+        return dot(exact, high) + dot(exact, low)
+    return dot(high, exact) + dot(low, exact)
+
+
+def sincos(x):
+    turns = jnp.floor(x * np.float32(2.0 / math.pi) + 0.5)
+    r = x - turns * np.float32(1.5703125)
+    r = r - turns * np.float32(4.837512969970703125e-4)
+    r = r - turns * np.float32(7.54978995489188216e-8)
+    z = r * r
+    s = ((np.float32(-1.9515295891e-4) * z + np.float32(8.3321608736e-3)) * z - np.float32(1.6666654611e-1)) * z * r + r
+    c = ((np.float32(2.443315711809948e-5) * z - np.float32(1.388731625493765e-3)) * z + np.float32(4.166664568298827e-2)) * z * z - np.float32(0.5) * z + 1.0
+    q = turns.astype(jnp.int32) & 3
+    odd = (q & 1) == 1
+    sine = jnp.where(odd, c, s)
+    cosine = jnp.where(odd, s, c)
+    sine = jnp.where(q >= 2, -sine, sine)
+    cosine = jnp.where((q == 1) | (q == 2), -cosine, cosine)
+    return sine, cosine
+
+
+def row_weights(my_rec, slab_rows):
+    groups = []
+    for k in range(slab_rows // 8):
+        g = my_rec * (slab_rows // 8) + k
+        first = (g + 1) // 2 - 1
+        x = (g * 8 + lax.broadcasted_iota(jnp.int32, (8, LANES), 0)).astype(jnp.float32) + 0.5
+        pair = []
+        for a in (first, first + 1):
+            inside = (a >= 0) & (a < SUB)
+            centre = (a.astype(jnp.float32) + 0.5) * SUBPX
+            w = jnp.maximum(0.0, 1.0 - jnp.abs(x - centre) / SUBPX)
+            pair.append((jnp.clip(a, 0, SUB - 1), jnp.where(inside, w, 0.0)))
+        groups.append(pair)
+    return groups
+
+
+def column_profiles(c_rows, keep, spread):
+    picked = [jnp.broadcast_to(c_rows[i : i + 1], keep.shape) * keep for i in range(c_rows.shape[0])]
+    return jnp.dot(
+        jnp.concatenate(picked, axis=0), spread, preferred_element_type=jnp.float32, precision=lax.Precision.HIGHEST
+    )
+
+
+def pick_kernel(slots, screens, out):
+    tile_count, layers = out.shape[0], out.shape[1]
+    total = slots.shape[0] // layers
+    for t in range(tile_count):
+        for l in range(layers):
+            for i in range(LG_DEV):
+                out[t, l, i] = screens[l, slots[l * total + t * ITEMS + i]]
+
+
+def slope_kernel(first, owners, received, c_base, *refs):
+    if first:
+        along_v, along_u, over_n, over_m, keep, spread, payload, slopes, prof = refs
+    else:
+        updates, along_v, along_u, over_n, over_m, keep, spread, payload, slopes, c_out, prof = refs
+    slab_rows = received.shape[3]
+    my_tile, my_rec = lax.axis_index("tile"), lax.axis_index("rec")
+    per_row = LANES // CMD
+    need = LG_DEV // per_row
+    row_count = PT // per_row
+    base = lax.rem(my_tile * need, row_count)
+    if first:
+        c_rows = c_base[pl.ds(base, need), :]
+    else:
+        c_new = c_base[...] + loop_gain * jnp.sum(updates[...], axis=0).reshape(c_base.shape)
+        c_out[...] = c_new
+        c_rows = c_out[pl.ds(base, need), :]
+    prof[...] = column_profiles(c_rows, keep[...], spread[...])
+    weights = row_weights(my_rec, slab_rows)
+    layers = received.shape[1]
+    total = owners.shape[0] // layers
+    rows = []
+    for i in range(LG_DEV):
+        phase = None
+        for l in range(layers):
+            tile = received[owners[l * total + my_tile * ITEMS + i], l, i].astype(jnp.float32)
+            phase = tile if phase is None else phase + tile
+        for k, ((a0, w0), (a1, w1)) in enumerate(weights):
+            shape = w0 * prof[pl.ds(i * SUB + a0, 1), :] + w1 * prof[pl.ds(i * SUB + a1, 1), :]
+            rows.append(phase[k * 8 : (k + 1) * 8] - shape)
+    residual = jnp.concatenate(rows, axis=0)
+    sine, cosine = sincos(residual)
+    e = jnp.concatenate([cosine.astype(jnp.bfloat16), sine.astype(jnp.bfloat16)], axis=1)
+    g = jnp.dot(e, along_v[...], preferred_element_type=jnp.float32).astype(jnp.bfloat16)
+    half = g.shape[1] // 2
+    g = jnp.concatenate([g[:, :half], g[:, half:]], axis=0)
+    h = jnp.dot(along_u[...], g, preferred_element_type=jnp.float32)
+    n = h.shape[0] // 2
+    h_re, h_im = h[:n], h[n:]
+    spot = h_re * h_re + h_im * h_im
+    sums = split_dot(over_m[...], split_dot(over_n[...], spot, False), True)
+    m = sums.shape[0] // 2
+    lane = lax.broadcasted_iota(jnp.int32, (m, LANES), 1)
+    row = lax.broadcasted_iota(jnp.int32, (m, LANES), 0)
+    top = sums[:m, LANES:] + jnp.where(lane % 2 == 1, sums[m:, :LANES], 0.0)
+    ratio = top / sums[:m, :LANES]
+    sub_rows = slab_rows // SUBPX
+    ratio = jnp.where(lane // SUBPX == my_rec * sub_rows + row // LG_DEV, ratio, 0.0)
+    own = ratio[:LG_DEV]
+    for a in range(1, sub_rows):
+        own = own + ratio[a * LG_DEV : (a + 1) * LG_DEV]
+    slopes[...] = own
+    payload[...] = jnp.broadcast_to(own.astype(jnp.bfloat16).astype(jnp.float32)[None], payload.shape)
+
+
+def update_kernel(pattern, received, blocks, out, slopes):
+    slopes[...] = jnp.sum(received[...], axis=1).reshape(slopes.shape)
+    rows = []
+    for i in range(blocks.shape[0]):
+        total = None
+        for b in range(blocks.shape[1]):
+            vector = slopes[pl.ds(pattern[i, b], 1), :].astype(jnp.bfloat16)
+            part = lax.dot_general(
+                vector, blocks[i, b], (((1,), (1,)), ((), ())), preferred_element_type=jnp.float32
+            )
+            total = part if total is None else total + part
+        rows.append(total)
+    out[...] = jnp.broadcast_to(jnp.concatenate(rows, axis=0)[None], out.shape)
+
+
+def science_kernel(first_ids, second_ids, c_first, c_second, keep, spread, *refs):
+    *pieces, out, store, prof, sem = refs
+    slab_rows = out.shape[2]
+    my_tile, my_rec = lax.axis_index("tile"), lax.axis_index("rec")
+    copies, at = [], 0
+    for i, piece in enumerate(pieces):
+        copies.append(pltpu.make_async_copy(piece, store.at[pl.ds(at, piece.shape[0])], sem.at[i]))
+        at += piece.shape[0]
+    for copy in copies:
+        copy.start()
+    weights = row_weights(my_rec, slab_rows)
+    profile_rows = PT * SUB
+    for f, c in enumerate((c_first, c_second)):
+        prof[pl.ds(f * profile_rows, profile_rows)] = column_profiles(c[...], keep[...], spread[...])
+    for copy in copies:
+        copy.wait()
+    start = lax.rem(my_tile * SC_DEV, PT)
+    for f, ids in enumerate((first_ids, second_ids)):
+
+        @pl.loop(0, PT)
+        def _(q):
+            p = lax.rem(start + q, PT)
+            row = f * profile_rows + p * SUB
+            shapes = [
+                w0 * prof[pl.ds(row + a0, 1), :] + w1 * prof[pl.ds(row + a1, 1), :]
+                for (a0, w0), (a1, w1) in weights
+            ]
+            shape = jnp.concatenate(shapes, axis=0)
+
+            def item(k):
+                phase = store[ids[k]].astype(jnp.float32) + store[ids[SC_DEV + k]].astype(jnp.float32)
+                out[f, k] = (phase - shape).astype(jnp.bfloat16)
+
+            item(q)
+
+            @pl.when(q + PT < SC_DEV)
+            def _():
+                item(q + PT)
+
+
+def by_ring(screens, tile_owner, tile_slot, commands_init, reconstructor, pattern):
+    layers, tiles_here, slab_rows, tile_px = screens.shape
+    frames = tile_owner.shape[0]
+    n = lax.axis_size("tile")
+    rec_count = lax.axis_size("rec")
+    everyone = n * rec_count
+    my_tile, my_rec = lax.axis_index("tile"), lax.axis_index("rec")
+    table = {k: jnp.asarray(v) for k, v in constant_tables(slab_rows).items()}
+    block_rows = reconstructor.shape[0]
+    f32 = jnp.float32
+
+    ring = list(range(0, n, 2)) + list(range(n - 1, 0, -2))
+    forward = [(ring[k], ring[(k + 1) % n]) for k in range(n)]
+    backward = [(b, a) for a, b in forward]
+
+    def place(tile):
+        return jnp.where(tile % 2 == 0, tile // 2, n - 1 - tile // 2)
+
+    slots = tile_slot.reshape(frames, layers * n * ITEMS)
+    owners = tile_owner.reshape(frames, layers * n * ITEMS)
+
+    def guide_tiles(frame):
+        picked = pl.pallas_call(
+            pick_kernel,
+            out_shape=jax.ShapeDtypeStruct((n, layers, LG_DEV, slab_rows, tile_px), screens.dtype),
+            in_specs=[smem(), vmem()],
+            out_specs=vmem(),
+        )(slots[frame], screens)
+        return lax.all_to_all(picked, "tile", split_axis=0, concat_axis=0, tiled=True)
+
+    def slopes_of(frame, received, c_base, updates):
+        first = updates is None
+        outs = [
+            jax.ShapeDtypeStruct((everyone, LG_DEV, LANES), f32),
+            jax.ShapeDtypeStruct((LG_DEV, LANES), f32),
+        ]
+        if not first:
+            outs.append(jax.ShapeDtypeStruct(c_base.shape, f32))
+        args = [received, c_base] + ([] if first else [updates])
+        args += [table[k] for k in ("along_v", "along_u", "over_n", "over_m", "keep", "spread")]
+        result = pl.pallas_call(
+            functools.partial(slope_kernel, first),
+            out_shape=outs,
+            in_specs=[smem()] + [vmem()] * len(args),
+            out_specs=[vmem()] * len(outs),
+            scratch_shapes=[pltpu.VMEM((LG_DEV * SUB, LANES), f32)],
+        )(owners[frame], *args)
+        payload, own = result[0], result[1]
+        own = lax.dynamic_slice_in_dim(own, my_rec * (slab_rows // SUBPX * SUB * 2), slab_rows // SUBPX * SUB * 2, 1)
+        return payload, own, (c_base if first else result[2])
+
+    def updates_of(payload, copies):
+        received = lax.all_to_all(payload, ("tile", "rec"), split_axis=0, concat_axis=0, tiled=True)
+        received = received.reshape(n, rec_count, LG_DEV, LANES)
+        return pl.pallas_call(
+            update_kernel,
+            out_shape=jax.ShapeDtypeStruct((copies, block_rows, LANES), f32),
+            in_specs=[smem(), vmem(), vmem()],
+            out_specs=vmem(),
+            scratch_shapes=[pltpu.VMEM((n * LG_DEV, LANES), f32)],
+        )(pattern, received, reconstructor)
+
+    received = [guide_tiles(f) for f in range(frames)]
+    c0 = lax.all_gather(commands_init.reshape(-1, LANES), "rec", axis=0, tiled=True)
+    ahead, behind = [screens], [screens]
+    for _ in range(n // 2 - 1):
+        ahead.append(lax.ppermute(ahead[-1], "tile", forward))
+        behind.append(lax.ppermute(behind[-1], "tile", backward))
+    far_first = lax.ppermute(ahead[-1][0], "tile", forward)
+    far_second = lax.ppermute(behind[-1][1], "tile", backward)
+
+    payload, slopes_first, _ = slopes_of(0, received[0], c0, None)
+    updates = updates_of(payload, everyone)
+    updates = lax.all_to_all(updates, ("tile", "rec"), split_axis=0, concat_axis=0, tiled=True)
+    updates = updates.reshape(n, rec_count, block_rows, LANES)
+    payload, slopes_second, c1 = slopes_of(1, received[1], c0, updates)
+    updates = updates_of(payload, n)
+    updates = lax.all_to_all(updates, "tile", split_axis=0, concat_axis=0, tiled=True)
+    mine = lax.dynamic_slice_in_dim(c1, my_rec * block_rows, block_rows, 0)
+    c2 = mine + loop_gain * jnp.sum(updates, axis=0)
+
+    pieces = [x.reshape(layers * tiles_here, slab_rows, tile_px) for x in ahead]
+    pieces += [far_first, far_second]
+    pieces += [x.reshape(layers * tiles_here, slab_rows, tile_px) for x in reversed(behind[1:])]
+    back = (place(my_tile) - place(tile_owner[..., 0].reshape(frames, layers, n, ITEMS))) % n
+    layer = jnp.arange(layers, dtype=jnp.int32)[None, :, None, None]
+    where = (back * layers + layer) * tiles_here + tile_slot.reshape(frames, layers, n, ITEMS)
+    where = lax.dynamic_index_in_dim(where, my_tile, 2, keepdims=False)[:, :, LG_DEV:]
+    where = where.reshape(frames, layers * SC_DEV)
+    science = pl.pallas_call(
+        science_kernel,
+        out_shape=jax.ShapeDtypeStruct((frames, SC_DEV, slab_rows, tile_px), jnp.bfloat16),
+        in_specs=[smem()] * 2 + [vmem()] * 4 + [pl.BlockSpec(memory_space=pl.ANY)] * len(pieces),
+        out_specs=vmem(),
+        scratch_shapes=[
+            pltpu.VMEM((n * layers * tiles_here, slab_rows, tile_px), screens.dtype),
+            pltpu.VMEM((frames * PT * SUB, LANES), f32),
+            pltpu.SemaphoreType.DMA((len(pieces),)),
+        ],
+        compiler_params=pltpu.CompilerParams(vmem_limit_bytes=32 << 20),
+    )(where[0], where[1], c0, c1, table["keep"], table["spread"], *pieces)
+    return jnp.stack([slopes_first, slopes_second], axis=0), science, c2.reshape(-1)
+
+
+def per_device(screens, tile_owner, *rest):
+    layers, tiles_here, _, _ = screens.shape
+    frames, n = tile_owner.shape[0], lax.axis_size("tile")
+    capacity = max(2, 3 * ITEMS // (2 * n))
+    few = tiles_here <= frames * capacity and n % 2 == 0 and frames == 2 and layers == 2
+    return (by_ring if few else by_request)(screens, tile_owner, *rest)
+
+
 def solution(mesh):
     placed = (
         P(None, "tile", "rec", None),

time: 294 us -> 130 us (0.44)
  blocking collectives: 156 us -> 5.6 us
  local copies, waits for them, and re-layouts: 34.4 us -> 9.09 us
  starting transfers between devices: 11.9 us -> 34 us
  Pallas kernels: 0 us -> 20.8 us
  matrix products: 20.7 us -> 0 us
  other arithmetic: 12.8 us -> 1.27 us
    all_gather x4 -> x1, blocking collectives: 113 us -> 5.6 us  [by_ring(): lax.all_gather(commands_init.reshape(-1, LANES), 'rec', axis=0, tiled=True)]
    psum x2 -> x0, blocking collectives: 43.2 us -> none  [per_device(): state = state + loop_gain * lax.psum(partial_rows, 'tile')]
    pallas_call x0 -> x7, Pallas kernels: none -> 20.8 us  [the longest x1 6.6 us: by_ring(): pl.pallas_call(science_kernel, out_shape=jax.ShapeDtypeStruct((frames, SC...]
    dot_general x22 -> x0, matrix products: 20.7 us -> none  [the longest x4 12.2 us: per_device(): jnp.einsum('xa,iab,yb->ixy', influence_rows, chosen, influence_all, preci...]
    gather x12 -> x0, local copies, waits for them, and re-layouts: 15 us -> none  [the longest x4 7.65 us: unpack_tiles(): jnp.take(layer_tiles, flat_index, axis=0).astype(jnp.float32)]
    all_to_all x2 -> x6, starting transfers between devices: 11.9 us -> 23.7 us  [the longest x2 10.4 us: guide_tiles(): lax.all_to_all(picked, 'tile', split_axis=0, concat_axis=0, tiled=True)]
    ppermute x0 -> x8, starting transfers between devices: none -> 10.3 us  [the longest x3 7.54 us: by_ring(): behind.append(lax.ppermute(behind[-1], 'tile', backward))]
    ppermute x0 -> x8, waiting for transfers between devices: none -> 9.66 us  [the longest x3 9.65 us: by_ring(): behind.append(lax.ppermute(behind[-1], 'tile', backward))]
  transfers between devices with their start and end apart: 2 -> 14, of which waited for: 1 -> 7; matrix products, arithmetic and copies ran while one was open for 10% -> 5% of each run, Pallas kernels for 0% -> 11%
where the time goes in v1:
time: 130 us
  waiting for transfers between devices  58 us (45%)
  starting transfers between devices  34 us (26%)
  Pallas kernels  20.8 us (16%)
  local copies, waits for them, and re-layouts  9.09 us (7%)
  blocking collectives  5.6 us (4%)
    all_to_all x1, waiting for transfers between devices, by_ring(): lax.all_to_all(updates, ('tile', 'rec'), split_axis=0, concat_axis=0, til...  16.4 us
    all_to_all x2, waiting for transfers between devices, guide_tiles(): lax.all_to_all(picked, 'tile', split_axis=0, concat_axis=0, tiled=True)  13.6 us
    all_to_all x2, waiting for transfers between devices, updates_of(): lax.all_to_all(payload, ('tile', 'rec'), split_axis=0, concat_axis=0, til...  12.3 us
    all_to_all x2, starting transfers between devices, guide_tiles(): lax.all_to_all(picked, 'tile', split_axis=0, concat_axis=0, tiled=True)  10.4 us
    ppermute x3, waiting for transfers between devices, by_ring(): behind.append(lax.ppermute(behind[-1], 'tile', backward))  9.65 us
    ppermute x3, starting transfers between devices, by_ring(): behind.append(lax.ppermute(behind[-1], 'tile', backward))  7.54 us
    all_to_all x2, starting transfers between devices, updates_of(): lax.all_to_all(payload, ('tile', 'rec'), split_axis=0, concat_axis=0, til...  7.42 us
    pallas_call x1, Pallas kernels, by_ring(): pl.pallas_call(science_kernel, out_shape=jax.ShapeDtypeStruct((frames, SC...  6.6 us
  transfers between devices with their start and end apart: 14, of which 7 were waited for; matrix products, arithmetic and copies ran while one was open for 5% of the time, Pallas kernels for 11%

profile of v1, /device:TPU:0, one launch (start us, length us, event | category | flops | bytes accessed | tf_op | source)
XLA Modules:
  0.0 129.5 jit_solution(9204355625550542354)
XLA Ops:
  0.6 0.0 copy-start.11
  0.6 0.0 copy-start.13
  0.7 3.0 %collective-permute-start.4 = (bf16[2,48,32,128]{3,2,1,0:T(8,128)(2,1)}, bf16[2,48,32,128]{3,2,1,0:T(8,128)(2,1)S(1)}, u32[]{:S(2)}, u32[]{:S(2)}) collective-permute-start(bf16[2,48,32,128]{3,2,1,0:T(8,128)(2,1)} %screens.3), channel_id=1, source_target_pairs={{8,0},{16,8},{24,16},{28,24},{20,28},{12,20},{4,12},{0,4},{9,1},{1... | collective-permute-start | bytes 2359304 | tf_op jit(solution)/shard_map/ppermute | solution.py:437
  3.7 0.1 collective-permute-start
  3.8 0.7 slice_bitcast_fusion.3
  4.5 0.6 copy.22
  5.1 2.0 %shard_map.139 = bf16[8,2,4,32,128]{4,3,2,1,0:T(8,128)(2,1)} custom-call(s32[2048]{0:T(1024)} %bitcast.44, bf16[2,48,32,128]{3,2,1,0:T(8,128)(2,1)} %screens.3), custom_call_target="tpu_custom_call" | custom-call | tf_op jit(solution)/shard_map/pallas_call | solution.py:392
  7.1 6.2 %all-to-all-start = ((bf16[8,2,4,32,128]{4,3,2,1,0:T(8,128)(2,1)}), bf16[8,2,4,32,128]{4,3,2,1,0:T(8,128)(2,1)S(1)}, u32[]{:S(2)}, u32[]{:S(2)}) async-start(bf16[8,2,4,32,128]{4,3,2,1,0:T(8,128)(2,1)} %shard_map.139), calls=%async_computation | async-start | bytes 1048576 | tf_op jit(solution)/shard_map/all_to_all | solution.py:398
  13.3 0.0 copy-start.15
  13.3 9.6 %collective-permute-done.4 = bf16[2,48,32,128]{3,2,1,0:T(8,128)(2,1)S(1)} collective-permute-done((bf16[2,48,32,128]{3,2,1,0:T(8,128)(2,1)}, bf16[2,48,32,128]{3,2,1,0:T(8,128)(2,1)S(1)}, u32[]{:S(2)}, u32[]{:S(2)}) %collective-permute-start.4) | collective-permute-done | bytes 786464 | tf_op jit(solution)/shard_map/ppermute | solution.py:437
  23.0 2.7 %collective-permute-start.5 = (bf16[2,48,32,128]{3,2,1,0:T(8,128)(2,1)S(1)}, bf16[2,48,32,128]{3,2,1,0:T(8,128)(2,1)}, u32[]{:S(2)}, u32[]{:S(2)}) collective-permute-start(bf16[2,48,32,128]{3,2,1,0:T(8,128)(2,1)S(1)} %collective-permute-done.4), channel_id=1, source_target_pairs={{8,0},{16,8},{24,16},{28,24},{20,28},{12,20},{4,12},{0,4},{9,1},{1... | collective-permute-start | bytes 2359304 | tf_op jit(solution)/shard_map/ppermute | solution.py:437
  25.6 0.0 collective-permute-done
  25.6 0.4 collective-permute-start.1
  26.0 0.0 copy-done.11
  26.0 0.6 fusion.7
  26.6 0.0 copy-done.13
  26.6 5.6 %all_gather.3.c_base.c_first = f32[32,128]{1,0:T(8,128)} all-gather(f32[8,128]{1,0:T(8,128)S(1)} %bitcast.49), channel_id=1, replica_groups=mesh['tile'=8,'rec'=4] {'rec'}, dimensions={0}, use_global_device_ids=true | all-gather | bytes 20480 | tf_op jit(solution)/shard_map/all_gather | solution.py:433
  32.2 2.8 %all-to-all-done.received = bf16[8,2,4,32,128]{4,3,2,1,0:T(8,128)(2,1)S(1)} async-done(((bf16[8,2,4,32,128]{4,3,2,1,0:T(8,128)(2,1)}), bf16[8,2,4,32,128]{4,3,2,1,0:T(8,128)(2,1)S(1)}, u32[]{:S(2)}, u32[]{:S(2)}) %all-to-all-start) | async-done | bytes 524320 | tf_op jit(solution)/shard_map/all_to_all | solution.py:398
  35.0 0.8 copy-done.7
  35.8 2.9 %shard_map.140 = (f32[32,4,128]{2,1,0:T(4,128)}, f32[4,128]{1,0:T(4,128)}) custom-call(s32[2048]{0:T(1024)} %bitcast.47, bf16[8,2,4,32,128]{4,3,2,1,0:T(8,128)(2,1)} %copy-done.7, f32[32,128]{1,0:T(8,128)} %all_gather.3.c_base.c_first, bf16[256,512]{1,0:T(8,128)(2,1)} %constant.96.clone.refs_0_.refs_1_, bf16[512,256]{1,0:T(8,128)(2,1)} %constant.97.clone.refs_1_.refs_2_, ...), custom_call_target="tpu_custom_call" | custom-call | tf_op jit(solution)/shard_map/pallas_call | solution.py:410
  38.8 4.7 %all-to-all-start.2 = ((f32[32,4,128]{2,1,0:T(4,128)}), f32[32,4,128]{2,1,0:T(4,128)S(1)}, u32[]{:S(2)}, u32[]{:S(2)}) async-start(f32[32,4,128]{2,1,0:T(4,128)} %get-tuple-element.9), calls=%async_computation.2 | async-start | bytes 131072 | tf_op jit(solution)/shard_map/all_to_all | solution.py:422
  43.5 0.6 copy.21
  44.1 2.0 %shard_map.141 = bf16[8,2,4,32,128]{4,3,2,1,0:T(8,128)(2,1)} custom-call(s32[2048]{0:T(1024)} %bitcast.45, bf16[2,48,32,128]{3,2,1,0:T(8,128)(2,1)} %screens.3), custom_call_target="tpu_custom_call" | custom-call | tf_op jit(solution)/shard_map/pallas_call | solution.py:392
  46.1 9.1 %all-to-all-done.2 = f32[32,4,128]{2,1,0:T(4,128)S(1)} async-done(((f32[32,4,128]{2,1,0:T(4,128)}), f32[32,4,128]{2,1,0:T(4,128)S(1)}, u32[]{:S(2)}, u32[]{:S(2)}) %all-to-all-start.2) | async-done | bytes 65568 | tf_op jit(solution)/shard_map/all_to_all | solution.py:422
  55.2 4.1 %all-to-all-start.1 = ((bf16[8,2,4,32,128]{4,3,2,1,0:T(8,128)(2,1)}), bf16[8,2,4,32,128]{4,3,2,1,0:T(8,128)(2,1)}, u32[]{:S(2)}, u32[]{:S(2)}) async-start(bf16[8,2,4,32,128]{4,3,2,1,0:T(8,128)(2,1)} %shard_map.141), calls=%async_computation.1 | async-start | bytes 1048576 | tf_op jit(solution)/shard_map/all_to_all | solution.py:398
  59.4 0.0 collective-permute-done.5
  59.4 1.9 %collective-permute-start.6 = (bf16[2,48,32,128]{3,2,1,0:T(8,128)(2,1)}, bf16[2,48,32,128]{3,2,1,0:T(8,128)(2,1)S(1)}, u32[]{:S(2)}, u32[]{:S(2)}) collective-permute-start(bf16[2,48,32,128]{3,2,1,0:T(8,128)(2,1)} %collective-permute-done.5), channel_id=1, source_target_pairs={{8,0},{16,8},{24,16},{28,24},{20,28},{12,20},{4,12},{0,4},{9,1},{1... | collective-permute-start | bytes 2359304 | tf_op jit(solution)/shard_map/ppermute | solution.py:437
  61.3 0.0 collective-permute-done.1
  61.3 0.3 collective-permute-start.2
  61.6 0.0 copy-done.12
  61.6 0.0 copy-done.15
  61.6 0.7 copy.15.pattern
  62.3 0.0 copy-done.1
  62.3 0.0 copy-done.10
  62.3 2.1 %shard_map.142 = f32[32,8,128]{2,1,0:T(8,128)} custom-call(s32[8,2]{1,0:T(8,128)} %copy.15.pattern, f32[8,4,4,128]{3,2,1,0:T(4,128)} %bitcast.42, bf16[8,2,128,128]{3,2,1,0:T(8,128)(2,1)} %blocks.3), custom_call_target="tpu_custom_call" | custom-call | tf_op jit(solution)/shard_map/pallas_call | solution.py:424
  64.5 10.8 %all-to-all-done.1.received = bf16[8,2,4,32,128]{4,3,2,1,0:T(8,128)(2,1)} async-done(((bf16[8,2,4,32,128]{4,3,2,1,0:T(8,128)(2,1)}), bf16[8,2,4,32,128]{4,3,2,1,0:T(8,128)(2,1)}, u32[]{:S(2)}, u32[]{:S(2)}) %all-to-all-start.1) | async-done | bytes 524320 | tf_op jit(solution)/shard_map/all_to_all | solution.py:398
  75.3 2.6 %all-to-all-start.3 = ((f32[32,8,128]{2,1,0:T(8,128)}), f32[32,8,128]{2,1,0:T(8,128)S(1)}, u32[]{:S(2)}, u32[]{:S(2)}) async-start(f32[32,8,128]{2,1,0:T(8,128)} %shard_map.142), calls=%async_computation.3 | async-start | bytes 262144 | tf_op jit(solution)/shard_map/all_to_all | solution.py:443
  77.9 0.1 fusion.8
  78.0 0.1 squeeze.34.second_ids
  78.0 0.1 squeeze.33.first_ids
  78.1 0.1 dynamic-slice_bitcast_fusion.1
  78.2 16.4 %all-to-all-done.3 = f32[32,8,128]{2,1,0:T(8,128)S(1)} async-done(((f32[32,8,128]{2,1,0:T(8,128)}), f32[32,8,128]{2,1,0:T(8,128)S(1)}, u32[]{:S(2)}, u32[]{:S(2)}) %all-to-all-start.3) | async-done | bytes 131104 | tf_op jit(solution)/shard_map/all_to_all | solution.py:443
  94.6 0.7 copy-done.8
  95.2 3.0 %shard_map.143 = (f32[32,4,128]{2,1,0:T(4,128)}, f32[4,128]{1,0:T(4,128)}, f32[32,128]{1,0:T(8,128)}) custom-call(s32[2048]{0:T(1024)} %bitcast.46, bf16[8,2,4,32,128]{4,3,2,1,0:T(8,128)(2,1)} %all-to-all-done.1.received, f32[32,128]{1,0:T(8,128)} %all_gather.3.c_base.c_first, f32[8,4,8,128]{3,2,1,0:T(8,128)} %bitcast.40, ...), custom_call_target="tpu_custom_call" | custom-call | tf_op jit(solution)/shard_map/pallas_call | solution.py:410
  98.2 2.7 %all-to-all-start.4 = ((f32[32,4,128]{2,1,0:T(4,128)}), f32[32,4,128]{2,1,0:T(4,128)S(1)}, u32[]{:S(2)}, u32[]{:S(2)}) async-start(f32[32,4,128]{2,1,0:T(4,128)} %get-tuple-element.12), calls=%async_computation.4 | async-start | bytes 131072 | tf_op jit(solution)/shard_map/all_to_all | solution.py:422
  100.9 0.0 collective-permute-done.6
  101.0 0.8 slice_bitcast_fusion
  101.8 1.7 %collective-permute-start.7 = (bf16[48,32,128]{2,1,0:T(8,128)(2,1)}, bf16[48,32,128]{2,1,0:T(8,128)(2,1)}, u32[]{:S(2)}, u32[]{:S(2)}) collective-permute-start(bf16[48,32,128]{2,1,0:T(8,128)(2,1)} %slice_bitcast_fusion), channel_id=1, source_target_pairs={{8,0},{16,8},{24,16},{28,24},{20,28},{12,20},{4,12},{0,4},{9,1},{1... | collective-permute-start | bytes 1179656 | tf_op jit(solution)/shard_map/ppermute | solution.py:439
  103.4 0.0 collective-permute-done.2
  103.4 0.8 slice_bitcast_fusion.1
  104.2 0.4 collective-permute-start.3
  104.6 0.8 dynamic-slice_bitcast_fusion
  105.3 3.1 %all-to-all-done.4 = f32[32,4,128]{2,1,0:T(4,128)S(1)} async-done(((f32[32,4,128]{2,1,0:T(4,128)}), f32[32,4,128]{2,1,0:T(4,128)S(1)}, u32[]{:S(2)}, u32[]{:S(2)}) %all-to-all-start.4) | async-done | bytes 65568 | tf_op jit(solution)/shard_map/all_to_all | solution.py:422
  108.5 0.6 copy-done.9
  109.1 2.1 %shard_map.145 = f32[8,8,128]{2,1,0:T(8,128)} custom-call(s32[8,2]{1,0:T(8,128)} %copy.15.pattern, f32[8,4,4,128]{3,2,1,0:T(4,128)} %bitcast.41, bf16[8,2,128,128]{3,2,1,0:T(8,128)(2,1)} %blocks.3), custom_call_target="tpu_custom_call" | custom-call | tf_op jit(solution)/shard_map/pallas_call | solution.py:424
  111.2 3.3 %all-to-all-start.5 = ((f32[8,8,128]{2,1,0:T(8,128)}), f32[8,8,128]{2,1,0:T(8,128)S(1)}, u32[]{:S(2)}, u32[]{:S(2)}) async-start(f32[8,8,128]{2,1,0:T(8,128)} %shard_map.145), calls=%async_computation.5 | async-start | bytes 65536 | tf_op jit(solution)/shard_map/all_to_all | solution.py:447
  114.5 0.6 pad_maximum_fusion
  115.1 6.0 %all-to-all-done.5 = f32[8,8,128]{2,1,0:T(8,128)S(1)} async-done(((f32[8,8,128]{2,1,0:T(8,128)}), f32[8,8,128]{2,1,0:T(8,128)S(1)}, u32[]{:S(2)}, u32[]{:S(2)}) %all-to-all-start.5) | async-done | bytes 32800 | tf_op jit(solution)/shard_map/all_to_all | solution.py:447
  121.1 0.6 add_bitcast_fusion
  121.8 0.0 collective-permute-done.7.refs_5_
  121.8 0.0 collective-permute-done.3.refs_4_
  121.8 0.0 copy-start.2
  121.8 1.1 copy-done.2
  122.9 6.6 %shard_map.144 = bf16[2,124,32,128]{3,2,1,0:T(8,128)(2,1)} custom-call(s32[248]{0:T(256)S(1)} %squeeze.33.first_ids, s32[248]{0:T(256)S(1)} %squeeze.34.second_ids, f32[32,128]{1,0:T(8,128)S(1)} %copy-done.4, f32[32,128]{1,0:T(8,128)S(1)} %copy-done.6, f32[16,128]{1,0:T(8,128)S(1)} %copy-done.5, f32[128,128]{1,0:T(8,128)S(1)} %copy-done.3, ...), custom_call_target="tpu_custom_call" | custom-call | tf_op jit(solution)/shard_map/pallas_call | solution.py:459
  (23 shorter events, 0.1 us)
Async XLA Ops:
  0.6 25.4 %copy-start.11 = (s32[2,2,1024,1]{2,3,1,0:T(1,128)S(1)}, s32[2,2,1024,1]{2,3,1,0:T(1,128)}, u32[]{:S(2)}) copy-start(s32[2,2,1024,1]{2,3,1,0:T(1,128)} %param.13) | copy-start | bytes 49156
  0.6 26.0 %copy-start.13 = (f32[1024]{0:T(1024)S(1)}, f32[1024]{0:T(1024)}, u32[]{:S(2)}) copy-start(f32[1024]{0:T(1024)} %param.15) | copy-start | bytes 12292
  0.7 22.3 %collective-permute-start.4 = (bf16[2,48,32,128]{3,2,1,0:T(8,128)(2,1)}, bf16[2,48,32,128]{3,2,1,0:T(8,128)(2,1)S(1)}, u32[]{:S(2)}, u32[]{:S(2)}) collective-permute-start(bf16[2,48,32,128]{3,2,1,0:T(8,128)(2,1)} %screens.3), channel_id=1, source_target_pairs={{8,0},{16,8},{24,16},{28,24},{20,28},{12,20},{4,12},{0,4},{9,1},{1... | collective-permute-start | bytes 2359304 | tf_op jit(solution)/shard_map/ppermute | solution.py:437
  3.7 22.0 %collective-permute-start = (bf16[2,48,32,128]{3,2,1,0:T(8,128)(2,1)}, bf16[2,48,32,128]{3,2,1,0:T(8,128)(2,1)S(1)}, u32[]{:S(2)}, u32[]{:S(2)}) collective-permute-start(bf16[2,48,32,128]{3,2,1,0:T(8,128)(2,1)} %screens.3), channel_id=1, source_target_pairs={{0,8},{8,16},{16,24},{24,28},{28,20},{20,12},{12,4},{4,0},{1,9},{9... | collective-permute-start | bytes 2359304 | tf_op jit(solution)/shard_map/ppermute | solution.py:436
  7.1 27.9 %all-to-all-start = ((bf16[8,2,4,32,128]{4,3,2,1,0:T(8,128)(2,1)}), bf16[8,2,4,32,128]{4,3,2,1,0:T(8,128)(2,1)S(1)}, u32[]{:S(2)}, u32[]{:S(2)}) async-start(bf16[8,2,4,32,128]{4,3,2,1,0:T(8,128)(2,1)} %shard_map.139), calls=%async_computation | async-start | bytes 1048576 | tf_op jit(solution)/shard_map/all_to_all | solution.py:398
  13.3 48.3 %copy-start.12 = (s32[2,2,1024]{2,1,0:T(2,128)S(1)}, s32[2,2,1024]{2,1,0:T(2,128)}, u32[]{:S(2)}) copy-start(s32[2,2,1024]{2,1,0:T(2,128)} %param.14) | copy-start | bytes 49156
  13.3 48.3 %copy-start.15 = (s32[8,2]{0,1:T(2,128)S(1)}, s32[8,2]{0,1:T(2,128)}, u32[]{:S(2)}) copy-start(s32[8,2]{0,1:T(2,128)} %param.17) | copy-start | bytes 196
  23.0 36.4 %collective-permute-start.5 = (bf16[2,48,32,128]{3,2,1,0:T(8,128)(2,1)S(1)}, bf16[2,48,32,128]{3,2,1,0:T(8,128)(2,1)}, u32[]{:S(2)}, u32[]{:S(2)}) collective-permute-start(bf16[2,48,32,128]{3,2,1,0:T(8,128)(2,1)S(1)} %collective-permute-done.4), channel_id=1, source_target_pairs={{8,0},{16,8},{24,16},{28,24},{20,28},{12,20},{4,12},{0,4},{9,1},{1... | collective-permute-start | bytes 2359304 | tf_op jit(solution)/shard_map/ppermute | solution.py:437
  25.6 36.7 %copy-start.1 = (bf16[2,48,32,128]{3,2,1,0:T(8,128)(2,1)}, bf16[2,48,32,128]{3,2,1,0:T(8,128)(2,1)S(1)}, u32[]{:S(2)}) copy-start(bf16[2,48,32,128]{3,2,1,0:T(8,128)(2,1)S(1)} %collective-permute-done) | copy-start | bytes 2359300
  25.6 35.7 %collective-permute-start.1 = (bf16[2,48,32,128]{3,2,1,0:T(8,128)(2,1)S(1)}, bf16[2,48,32,128]{3,2,1,0:T(8,128)(2,1)}, u32[]{:S(2)}, u32[]{:S(2)}) collective-permute-start(bf16[2,48,32,128]{3,2,1,0:T(8,128)(2,1)S(1)} %collective-permute-done), channel_id=1, source_target_pairs={{0,8},{8,16},{16,24},{24,28},{28,20},{20,12},{12,4},{4,0},{1,9},{9... | collective-permute-start | bytes 2359304 | tf_op jit(solution)/shard_map/ppermute | solution.py:436
  35.0 0.8 copy-start.7
  38.8 39.4 %copy-start.14 = (f32[4,128]{1,0:T(4,128)S(1)}, f32[4,128]{1,0:T(4,128)}, u32[]{:S(2)}) copy-start(f32[4,128]{1,0:T(4,128)} %get-tuple-element.8) | copy-start | bytes 6148
  38.8 16.4 %all-to-all-start.2 = ((f32[32,4,128]{2,1,0:T(4,128)}), f32[32,4,128]{2,1,0:T(4,128)S(1)}, u32[]{:S(2)}, u32[]{:S(2)}) async-start(f32[32,4,128]{2,1,0:T(4,128)} %get-tuple-element.9), calls=%async_computation.2 | async-start | bytes 131072 | tf_op jit(solution)/shard_map/all_to_all | solution.py:422
  55.2 7.1 %copy-start.10 = (f32[32,4,128]{2,1,0:T(4,128)}, f32[32,4,128]{2,1,0:T(4,128)S(1)}, u32[]{:S(2)}) copy-start(f32[32,4,128]{2,1,0:T(4,128)S(1)} %all-to-all-done.2) | copy-start | bytes 196612
  55.2 20.1 %all-to-all-start.1 = ((bf16[8,2,4,32,128]{4,3,2,1,0:T(8,128)(2,1)}), bf16[8,2,4,32,128]{4,3,2,1,0:T(8,128)(2,1)}, u32[]{:S(2)}, u32[]{:S(2)}) async-start(bf16[8,2,4,32,128]{4,3,2,1,0:T(8,128)(2,1)} %shard_map.141), calls=%async_computation.1 | async-start | bytes 1048576 | tf_op jit(solution)/shard_map/all_to_all | solution.py:398
  59.4 41.5 %collective-permute-start.6 = (bf16[2,48,32,128]{3,2,1,0:T(8,128)(2,1)}, bf16[2,48,32,128]{3,2,1,0:T(8,128)(2,1)S(1)}, u32[]{:S(2)}, u32[]{:S(2)}) collective-permute-start(bf16[2,48,32,128]{3,2,1,0:T(8,128)(2,1)} %collective-permute-done.5), channel_id=1, source_target_pairs={{8,0},{16,8},{24,16},{28,24},{20,28},{12,20},{4,12},{0,4},{9,1},{1... | collective-permute-start | bytes 2359304 | tf_op jit(solution)/shard_map/ppermute | solution.py:437
  61.3 42.1 %collective-permute-start.2 = (bf16[2,48,32,128]{3,2,1,0:T(8,128)(2,1)}, bf16[2,48,32,128]{3,2,1,0:T(8,128)(2,1)S(1)}, u32[]{:S(2)}, u32[]{:S(2)}) collective-permute-start(bf16[2,48,32,128]{3,2,1,0:T(8,128)(2,1)} %collective-permute-done.1), channel_id=1, source_target_pairs={{0,8},{8,16},{16,24},{24,28},{28,20},{20,12},{12,4},{4,0},{1,9},{9... | collective-permute-start | bytes 2359304 | tf_op jit(solution)/shard_map/ppermute | solution.py:436
  64.5 57.3 %copy-start = (bf16[2,48,32,128]{3,2,1,0:T(8,128)(2,1)S(1)}, bf16[2,48,32,128]{3,2,1,0:T(8,128)(2,1)}, u32[]{:S(2)}) copy-start(bf16[2,48,32,128]{3,2,1,0:T(8,128)(2,1)} %screens.3) | copy-start | bytes 2359300
  64.5 57.3 %copy-start.3 = (f32[128,128]{1,0:T(8,128)S(1)}, f32[128,128]{1,0:T(8,128)}, u32[]{:S(2)}) copy-start(f32[128,128]{1,0:T(8,128)} %constant.100.clone.refs_5_.refs_6_.spread) | copy-start | bytes 196612
  64.5 57.3 %copy-start.4 = (f32[32,128]{1,0:T(8,128)S(1)}, f32[32,128]{1,0:T(8,128)}, u32[]{:S(2)}) copy-start(f32[32,128]{1,0:T(8,128)} %all_gather.3.c_base.c_first) | copy-start | bytes 49156
  64.5 57.3 %copy-start.5 = (f32[16,128]{1,0:T(8,128)S(1)}, f32[16,128]{1,0:T(8,128)}, u32[]{:S(2)}) copy-start(f32[16,128]{1,0:T(8,128)} %constant.101.clone.refs_4_.refs_5_.keep) | copy-start | bytes 24580
  75.3 19.3 %all-to-all-start.3 = ((f32[32,8,128]{2,1,0:T(8,128)}), f32[32,8,128]{2,1,0:T(8,128)S(1)}, u32[]{:S(2)}, u32[]{:S(2)}) async-start(f32[32,8,128]{2,1,0:T(8,128)} %shard_map.142), calls=%async_computation.3 | async-start | bytes 262144 | tf_op jit(solution)/shard_map/all_to_all | solution.py:443
  94.6 0.7 copy-start.8
  98.2 22.9 %copy-start.6 = (f32[32,128]{1,0:T(8,128)S(1)}, f32[32,128]{1,0:T(8,128)}, u32[]{:S(2)}) copy-start(f32[32,128]{1,0:T(8,128)} %get-tuple-element.11.c_second) | copy-start | bytes 49156
  98.2 10.2 %all-to-all-start.4 = ((f32[32,4,128]{2,1,0:T(4,128)}), f32[32,4,128]{2,1,0:T(4,128)S(1)}, u32[]{:S(2)}, u32[]{:S(2)}) async-start(f32[32,4,128]{2,1,0:T(4,128)} %get-tuple-element.12), calls=%async_computation.4 | async-start | bytes 131072 | tf_op jit(solution)/shard_map/all_to_all | solution.py:422
  101.8 20.0 %collective-permute-start.7 = (bf16[48,32,128]{2,1,0:T(8,128)(2,1)}, bf16[48,32,128]{2,1,0:T(8,128)(2,1)}, u32[]{:S(2)}, u32[]{:S(2)}) collective-permute-start(bf16[48,32,128]{2,1,0:T(8,128)(2,1)} %slice_bitcast_fusion), channel_id=1, source_target_pairs={{8,0},{16,8},{24,16},{28,24},{20,28},{12,20},{4,12},{0,4},{9,1},{1... | collective-permute-start | bytes 1179656 | tf_op jit(solution)/shard_map/ppermute | solution.py:439
  104.2 17.6 %collective-permute-start.3 = (bf16[48,32,128]{2,1,0:T(8,128)(2,1)}, bf16[48,32,128]{2,1,0:T(8,128)(2,1)}, u32[]{:S(2)}, u32[]{:S(2)}) collective-permute-start(bf16[48,32,128]{2,1,0:T(8,128)(2,1)} %slice_bitcast_fusion.1), channel_id=1, source_target_pairs={{0,8},{8,16},{16,24},{24,28},{28,20},{20,12},{12,4},{4,0},{1,9},{9... | collective-permute-start | bytes 1179656 | tf_op jit(solution)/shard_map/ppermute | solution.py:438
  108.5 0.6 copy-start.9
  111.2 10.0 %all-to-all-start.5 = ((f32[8,8,128]{2,1,0:T(8,128)}), f32[8,8,128]{2,1,0:T(8,128)S(1)}, u32[]{:S(2)}, u32[]{:S(2)}) async-start(f32[8,8,128]{2,1,0:T(8,128)} %shard_map.145), calls=%async_computation.5 | async-start | bytes 65536 | tf_op jit(solution)/shard_map/all_to_all | solution.py:447
  121.8 1.1 copy-start.2

commit v2 on v1

--- a/solution.py
+++ b/solution.py
@@ -145,6 +145,10 @@
     return (jnp.stack(slope_frames, axis=0), jnp.stack(science_frames, axis=0), state)
 
 
+def microseconds(t):
+    return pl.CostEstimate(flops=0, bytes_accessed=int(t * 3.69e6), transcendentals=0)
+
+
 def vmem():
     return pl.BlockSpec(memory_space=pltpu.VMEM)
 
@@ -189,14 +193,17 @@
     per_row = LANES // CMD
     spread = np.tile(infl.T, (per_row * SUB, 1))
     keep = np.kron(np.eye(per_row * SUB, dtype=f32), np.ones((1, SUB), f32))
-    return dict(
-        along_v=along_v.astype(bf16),
-        along_u=along_u.astype(bf16),
-        over_n=over_n.astype(bf16),
-        over_m=over_m.astype(bf16),
-        spread=spread,
-        keep=keep,
-    )
+    half = along_v.shape[1] // 2
+    exact = [along_v[:, :half], along_v[:, half:], along_u, over_n, over_m]
+    return dict(exact=np.concatenate(exact, axis=0).astype(bf16), mirror=np.concatenate([keep, spread], axis=0))
+
+
+def unpack_tables(exact, slab_rows):
+    e_cols = 2 * LANES
+    spots = LG_DEV * slab_rows // SUBPX * SPOT
+    edges = [0, e_cols, 2 * e_cols, 2 * e_cols + 2 * spots, 3 * e_cols + 2 * spots, exact.shape[0]]
+    v_re, v_im, u, over_n, over_m = [exact.at[pl.ds(a, b - a)] for a, b in zip(edges, edges[1:])]
+    return v_re, v_im, u, over_n, over_m
 
 
 def split_dot(exact, wide, left):
@@ -241,58 +248,79 @@
     return groups
 
 
-def column_profiles(c_rows, keep, spread):
+def column_profiles(c_rows, mirror):
+    at = LANES // CMD * SUB
+    keep, spread = mirror[:at], mirror[at:]
     picked = [jnp.broadcast_to(c_rows[i : i + 1], keep.shape) * keep for i in range(c_rows.shape[0])]
     return jnp.dot(
         jnp.concatenate(picked, axis=0), spread, preferred_element_type=jnp.float32, precision=lax.Precision.HIGHEST
     )
 
 
-def pick_kernel(slots, screens, out):
-    tile_count, layers = out.shape[0], out.shape[1]
-    total = slots.shape[0] // layers
-    for t in range(tile_count):
+def stages(n):
+    return [1 << k for k in range(n.bit_length() - 1)]
+
+
+def destination(me, bits, k):
+    return (k << bits) | (me & ((1 << bits) - 1))
+
+
+def offer_kernel(frame, slots, screens, out):
+    partner = lax.axis_index("tile") ^ 1
+    count, layers = out.shape[0], out.shape[1]
+    for k in range(count):
+        d = destination(partner, 1, k)
         for l in range(layers):
             for i in range(LG_DEV):
-                out[t, l, i] = screens[l, slots[l * total + t * ITEMS + i]]
-
-
-def slope_kernel(first, owners, received, c_base, *refs):
-    if first:
-        along_v, along_u, over_n, over_m, keep, spread, payload, slopes, prof = refs
-    else:
-        updates, along_v, along_u, over_n, over_m, keep, spread, payload, slopes, c_out, prof = refs
-    slab_rows = received.shape[3]
-    my_tile, my_rec = lax.axis_index("tile"), lax.axis_index("rec")
-    per_row = LANES // CMD
-    need = LG_DEV // per_row
-    row_count = PT // per_row
-    base = lax.rem(my_tile * need, row_count)
-    if first:
-        c_rows = c_base[pl.ds(base, need), :]
-    else:
-        c_new = c_base[...] + loop_gain * jnp.sum(updates[...], axis=0).reshape(c_base.shape)
-        c_out[...] = c_new
-        c_rows = c_out[pl.ds(base, need), :]
-    prof[...] = column_profiles(c_rows, keep[...], spread[...])
+                out[k, l, i] = screens[l, slots[frame, l, d * ITEMS + i]]
+
+
+def merge_kernel(frame, bits, owners, slots, mine, received, send, keep):
+    me = lax.axis_index("tile")
+    count, layers = send.shape[0], send.shape[1]
+    other = 1 << (bits - 1)
+    for out, side in ((keep, me), (send, me ^ (1 << bits))):
+        for k in range(count):
+            d = destination(side, bits + 1, k)
+            j = d >> bits
+            for l in range(layers):
+                for i in range(LG_DEV):
+                    g = d * ITEMS + i
+                    theirs = ((owners[frame, l, g] ^ me) & other) != 0
+                    ours = mine[l, slots[frame, l, g]] if bits == 1 else mine[j, l, i]
+                    out[k, l, i] = jnp.where(theirs, received[j, l, i], ours)
+
+
+def last_merge(frame, owners, kept, received):
+    me = lax.axis_index("tile")
+    layers = owners.shape[1]
+    other = lax.axis_size("tile") // 2
+    tiles = []
+    for i in range(LG_DEV):
+        row = []
+        for l in range(layers):
+            theirs = ((owners[frame, l, me * ITEMS + i] ^ me) & other) != 0
+            row.append(jnp.where(theirs, received[0, l, i], kept[0, l, i]))
+        tiles.append(row)
+    return tiles
+
+
+def slopes_from(tiles, prof, table, payload, slopes):
+    slab_rows = tiles[0][0].shape[0]
+    v_re, v_im, along_u, over_n, over_m = unpack_tables(table, slab_rows)
+    my_rec = lax.axis_index("rec")
     weights = row_weights(my_rec, slab_rows)
-    layers = received.shape[1]
-    total = owners.shape[0] // layers
     rows = []
     for i in range(LG_DEV):
-        phase = None
-        for l in range(layers):
-            tile = received[owners[l * total + my_tile * ITEMS + i], l, i].astype(jnp.float32)
-            phase = tile if phase is None else phase + tile
+        phase = functools.reduce(jnp.add, [tile.astype(jnp.float32) for tile in tiles[i]])
         for k, ((a0, w0), (a1, w1)) in enumerate(weights):
             shape = w0 * prof[pl.ds(i * SUB + a0, 1), :] + w1 * prof[pl.ds(i * SUB + a1, 1), :]
             rows.append(phase[k * 8 : (k + 1) * 8] - shape)
     residual = jnp.concatenate(rows, axis=0)
     sine, cosine = sincos(residual)
     e = jnp.concatenate([cosine.astype(jnp.bfloat16), sine.astype(jnp.bfloat16)], axis=1)
-    g = jnp.dot(e, along_v[...], preferred_element_type=jnp.float32).astype(jnp.bfloat16)
-    half = g.shape[1] // 2
-    g = jnp.concatenate([g[:, :half], g[:, half:]], axis=0)
+    g = [jnp.dot(e, v[...], preferred_element_type=jnp.float32).astype(jnp.bfloat16) for v in (v_re, v_im)]
+    g = jnp.concatenate(g, axis=0)
     h = jnp.dot(along_u[...], g, preferred_element_type=jnp.float32)
     n = h.shape[0] // 2
     h_re, h_im = h[:n], h[n:]
@@ -312,13 +340,43 @@
     payload[...] = jnp.broadcast_to(own.astype(jnp.bfloat16).astype(jnp.float32)[None], payload.shape)
 
 
+def own_rows(my_tile):
+    per_row = LANES // CMD
+    need = LG_DEV // per_row
+    return lax.rem(my_tile * need, PT // per_row), need
+
+
+def first_slopes(owners, kept, received, mirror, table, *refs):
+    *c_parts, payload, slopes, c, prof = refs
+    my_tile, my_rec = lax.axis_index("tile"), lax.axis_index("rec")
+    for k, part in enumerate(c_parts):
+        c[pl.ds((my_rec ^ k) * part.shape[0], part.shape[0]), :] = part[...]
+    base, need = own_rows(my_tile)
+    prof[...] = column_profiles(c[pl.ds(base, need), :], mirror)
+    tiles = last_merge(0, owners, kept, received)
+    slopes_from(tiles, prof, table, payload, slopes)
+
+
+def ring_place(n, tile):
+    return jnp.where(lax.rem(tile, 2) == 0, tile // 2, n - 1 - tile // 2)
+
+
+def second_slopes(owners, kept, received, c_base, updates, mirror, table, payload, slopes, c_out, prof):
+    my_tile = lax.axis_index("tile")
+    c_out[...] = c_base[...] + loop_gain * jnp.sum(updates[...], axis=0).reshape(c_base.shape)
+    base, need = own_rows(my_tile)
+    prof[...] = column_profiles(c_out[pl.ds(base, need), :], mirror)
+    tiles = last_merge(1, owners, kept, received)
+    slopes_from(tiles, prof, table, payload, slopes)
+
+
 def update_kernel(pattern, received, blocks, out, slopes):
     slopes[...] = jnp.sum(received[...], axis=1).reshape(slopes.shape)
     rows = []
     for i in range(blocks.shape[0]):
         total = None
         for b in range(blocks.shape[1]):
-            vector = slopes[pl.ds(pattern[i, b], 1), :].astype(jnp.bfloat16)
+            vector = slopes[pl.ds(pattern[b, i], 1), :].astype(jnp.bfloat16)
             part = lax.dot_general(
                 vector, blocks[i, b], (((1,), (1,)), ((), ())), preferred_element_type=jnp.float32
             )
@@ -327,44 +385,48 @@
     out[...] = jnp.broadcast_to(jnp.concatenate(rows, axis=0)[None], out.shape)
 
 
-def science_kernel(first_ids, second_ids, c_first, c_second, keep, spread, *refs):
-    *pieces, out, store, prof, sem = refs
+def science_kernel(n, tiles_here, owners, slots, c_first, c_second, mirror, *refs):
+    gathered, out, store, prof, starts, sem = refs
+    layers = owners.shape[1]
     slab_rows = out.shape[2]
     my_tile, my_rec = lax.axis_index("tile"), lax.axis_index("rec")
-    copies, at = [], 0
-    for i, piece in enumerate(pieces):
-        copies.append(pltpu.make_async_copy(piece, store.at[pl.ds(at, piece.shape[0])], sem.at[i]))
-        at += piece.shape[0]
-    for copy in copies:
-        copy.start()
+    copy = pltpu.make_async_copy(gathered, store, sem)
+    copy.start()
+    for o in range(n):
+        starts[o] = ring_place(n, jnp.int32(o)) * layers * tiles_here
     weights = row_weights(my_rec, slab_rows)
     profile_rows = PT * SUB
     for f, c in enumerate((c_first, c_second)):
-        prof[pl.ds(f * profile_rows, profile_rows)] = column_profiles(c[...], keep[...], spread[...])
-    for copy in copies:
-        copy.wait()
+        prof[pl.ds(f * profile_rows, profile_rows)] = column_profiles(c[...], mirror)
+    copy.wait()
     start = lax.rem(my_tile * SC_DEV, PT)
-    for f, ids in enumerate((first_ids, second_ids)):
-
-        @pl.loop(0, PT)
-        def _(q):
-            p = lax.rem(start + q, PT)
-            row = f * profile_rows + p * SUB
+    for f in range(out.shape[0]):
+
+        def one(q, both):
+            row = f * profile_rows + lax.rem(start + q, PT) * SUB
             shapes = [
                 w0 * prof[pl.ds(row + a0, 1), :] + w1 * prof[pl.ds(row + a1, 1), :]
                 for (a0, w0), (a1, w1) in weights
             ]
             shape = jnp.concatenate(shapes, axis=0)
-
-            def item(k):
-                phase = store[ids[k]].astype(jnp.float32) + store[ids[SC_DEV + k]].astype(jnp.float32)
+            for k in (q, q + PT)[: 1 + both]:
+                g = my_tile * ITEMS + LG_DEV + k
+                phase = None
+                for l in range(layers):
+                    tile = store[starts[owners[f, l, g]] + l * tiles_here + slots[f, l, g]].astype(jnp.float32)
+                    phase = tile if phase is None else phase + tile
                 out[f, k] = (phase - shape).astype(jnp.bfloat16)
 
-            item(q)
-
-            @pl.when(q + PT < SC_DEV)
-            def _():
-                item(q + PT)
+        twice = SC_DEV - PT
+        together = 4
+
+        @pl.loop(0, twice // together)
+        def _(q):
+            for j in range(together):
+                one(q * together + j, True)
+
+        for q in range(twice // together * together, PT):
+            one(q, q < twice)
 
 
 def by_ring(screens, tile_owner, tile_slot, commands_init, reconstructor, pattern):
@@ -377,49 +439,21 @@
     table = {k: jnp.asarray(v) for k, v in constant_tables(slab_rows).items()}
     block_rows = reconstructor.shape[0]
     f32 = jnp.float32
+    limit = pltpu.CompilerParams(vmem_limit_bytes=24 << 20)
 
     ring = list(range(0, n, 2)) + list(range(n - 1, 0, -2))
-    forward = [(ring[k], ring[(k + 1) % n]) for k in range(n)]
-    backward = [(b, a) for a, b in forward]
-
-    def place(tile):
-        return jnp.where(tile % 2 == 0, tile // 2, n - 1 - tile // 2)
-
-    slots = tile_slot.reshape(frames, layers * n * ITEMS)
-    owners = tile_owner.reshape(frames, layers * n * ITEMS)
-
-    def guide_tiles(frame):
-        picked = pl.pallas_call(
-            pick_kernel,
-            out_shape=jax.ShapeDtypeStruct((n, layers, LG_DEV, slab_rows, tile_px), screens.dtype),
-            in_specs=[smem(), vmem()],
-            out_specs=vmem(),
-        )(slots[frame], screens)
-        return lax.all_to_all(picked, "tile", split_axis=0, concat_axis=0, tiled=True)
-
-    def slopes_of(frame, received, c_base, updates):
-        first = updates is None
-        outs = [
-            jax.ShapeDtypeStruct((everyone, LG_DEV, LANES), f32),
-            jax.ShapeDtypeStruct((LG_DEV, LANES), f32),
-        ]
-        if not first:
-            outs.append(jax.ShapeDtypeStruct(c_base.shape, f32))
-        args = [received, c_base] + ([] if first else [updates])
-        args += [table[k] for k in ("along_v", "along_u", "over_n", "over_m", "keep", "spread")]
-        result = pl.pallas_call(
-            functools.partial(slope_kernel, first),
-            out_shape=outs,
-            in_specs=[smem()] + [vmem()] * len(args),
-            out_specs=[vmem()] * len(outs),
-            scratch_shapes=[pltpu.VMEM((LG_DEV * SUB, LANES), f32)],
-        )(owners[frame], *args)
-        payload, own = result[0], result[1]
-        own = lax.dynamic_slice_in_dim(own, my_rec * (slab_rows // SUBPX * SUB * 2), slab_rows // SUBPX * SUB * 2, 1)
-        return payload, own, (c_base if first else result[2])
-
-    def updates_of(payload, copies):
-        received = lax.all_to_all(payload, ("tile", "rec"), split_axis=0, concat_axis=0, tiled=True)
+
+    owners = tile_owner[..., 0]
+    tables_in = [table["mirror"], table["exact"]]
+    payload_out = [
+        jax.ShapeDtypeStruct((everyone, LG_DEV, LANES), f32),
+        jax.ShapeDtypeStruct((LG_DEV, LANES), f32),
+    ]
+
+    def exchange(payload):
+        return lax.all_to_all(payload, ("tile", "rec"), split_axis=0, concat_axis=0, tiled=True)
+
+    def updates_of(received, copies):
         received = received.reshape(n, rec_count, LG_DEV, LANES)
         return pl.pallas_call(
             update_kernel,
@@ -427,55 +461,118 @@
             in_specs=[smem(), vmem(), vmem()],
             out_specs=vmem(),
             scratch_shapes=[pltpu.VMEM((n * LG_DEV, LANES), f32)],
-        )(pattern, received, reconstructor)
-
-    received = [guide_tiles(f) for f in range(frames)]
-    c0 = lax.all_gather(commands_init.reshape(-1, LANES), "rec", axis=0, tiled=True)
-    ahead, behind = [screens], [screens]
-    for _ in range(n // 2 - 1):
-        ahead.append(lax.ppermute(ahead[-1], "tile", forward))
-        behind.append(lax.ppermute(behind[-1], "tile", backward))
-    far_first = lax.ppermute(ahead[-1][0], "tile", forward)
-    far_second = lax.ppermute(behind[-1][1], "tile", backward)
-
-    payload, slopes_first, _ = slopes_of(0, received[0], c0, None)
-    updates = updates_of(payload, everyone)
+            compiler_params=limit,
+            cost_estimate=microseconds(2),
+        )(pattern.T, received, reconstructor)
+
+    wide = (layers, LG_DEV, slab_rows, tile_px)
+
+    def tiles_of(*counts):
+        shapes = [jax.ShapeDtypeStruct((c,) + wide, screens.dtype) for c in counts]
+        return dict(out_shape=shapes, out_specs=[vmem()] * len(shapes))
+
+    def swap(x, bit):
+        return lax.ppermute(x, "tile", [(t, t ^ bit) for t in range(n)])
+
+    def offer(frame, mine):
+        (out,) = pl.pallas_call(
+            functools.partial(offer_kernel, frame), in_specs=[smem(), vmem()], compiler_params=limit, **tiles_of(n // 2)
+        )(tile_slot, mine)
+        return out
+
+    def merge(frame, bits, mine, received):
+        count = n >> (bits + 1)
+        return pl.pallas_call(
+            functools.partial(merge_kernel, frame, bits),
+            in_specs=[smem()] * 2 + [vmem()] * 2,
+            compiler_params=limit,
+            **tiles_of(count, count),
+        )(owners, tile_slot, mine, received)
+
+    def later(value, after):
+        return lax.optimization_barrier((value, after))[0]
+
+    def own_lanes(slopes):
+        width = slab_rows // SUBPX * SUB * 2
+        return lax.dynamic_slice_in_dim(slopes, my_rec * width, width, 1)
+
+    last = n.bit_length() - 1
+    sent = [offer(0, screens)]
+    gathered_after = sent[0]
+    second = offer(1, later(screens, sent[0]))
+    kept, got = screens, swap(sent[0], 1)
+    for bits in range(1, last):
+        send, kept = merge(0, bits, kept, got)
+        got = swap(send, 1 << bits)
+    kept_second, got_second = later(screens, send), swap(second, 1)
+    for bits in range(1, last):
+        send, kept_second = merge(1, bits, kept_second, got_second)
+        got_second = swap(send, 1 << bits)
+        if bits == 1:
+            kept = later(kept, send)
+    guide = [(kept, got), (kept_second, got_second)]
+    c_own = commands_init.reshape(-1, LANES)
+    c_parts = [c_own] + [
+        lax.ppermute(c_own, "rec", [(r, r ^ k) for r in range(rec_count)]) for k in range(1, rec_count)
+    ]
+
+    gathered = lax.all_gather(later(screens, gathered_after), "tile", axis_index_groups=[ring])
+    gathered = gathered.reshape(n * layers * tiles_here, slab_rows, tile_px)
+
+    payload, slopes_first, c0 = pl.pallas_call(
+        first_slopes,
+        out_shape=payload_out + [jax.ShapeDtypeStruct((rec_count * block_rows, LANES), f32)],
+        in_specs=[smem()] + [vmem()] * (2 + rec_count + len(tables_in)),
+        out_specs=[vmem()] * 3,
+        scratch_shapes=[pltpu.VMEM((LG_DEV * SUB, LANES), f32)],
+        compiler_params=limit,
+        cost_estimate=microseconds(3),
+    )(owners, *guide[0], *tables_in, *c_parts)
+    slopes_first = own_lanes(slopes_first)
+    updates = updates_of(later(exchange(payload), send), everyone)
     updates = lax.all_to_all(updates, ("tile", "rec"), split_axis=0, concat_axis=0, tiled=True)
     updates = updates.reshape(n, rec_count, block_rows, LANES)
-    payload, slopes_second, c1 = slopes_of(1, received[1], c0, updates)
-    updates = updates_of(payload, n)
+
+    payload, slopes_second, c1 = pl.pallas_call(
+        second_slopes,
+        out_shape=payload_out + [jax.ShapeDtypeStruct(c0.shape, f32)],
+        in_specs=[smem()] + [vmem()] * (4 + len(tables_in)),
+        out_specs=[vmem()] * 3,
+        scratch_shapes=[pltpu.VMEM((LG_DEV * SUB, LANES), f32)],
+        compiler_params=limit,
+        cost_estimate=microseconds(3),
+    )(owners, *guide[1], c0, updates, *tables_in)
+    updates = updates_of(exchange(payload), n)
     updates = lax.all_to_all(updates, "tile", split_axis=0, concat_axis=0, tiled=True)
-    mine = lax.dynamic_slice_in_dim(c1, my_rec * block_rows, block_rows, 0)
-    c2 = mine + loop_gain * jnp.sum(updates, axis=0)
-
-    pieces = [x.reshape(layers * tiles_here, slab_rows, tile_px) for x in ahead]
-    pieces += [far_first, far_second]
-    pieces += [x.reshape(layers * tiles_here, slab_rows, tile_px) for x in reversed(behind[1:])]
-    back = (place(my_tile) - place(tile_owner[..., 0].reshape(frames, layers, n, ITEMS))) % n
-    layer = jnp.arange(layers, dtype=jnp.int32)[None, :, None, None]
-    where = (back * layers + layer) * tiles_here + tile_slot.reshape(frames, layers, n, ITEMS)
-    where = lax.dynamic_index_in_dim(where, my_tile, 2, keepdims=False)[:, :, LG_DEV:]
-    where = where.reshape(frames, layers * SC_DEV)
     science = pl.pallas_call(
-        science_kernel,
+        functools.partial(science_kernel, n, tiles_here),
         out_shape=jax.ShapeDtypeStruct((frames, SC_DEV, slab_rows, tile_px), jnp.bfloat16),
-        in_specs=[smem()] * 2 + [vmem()] * 4 + [pl.BlockSpec(memory_space=pl.ANY)] * len(pieces),
+        in_specs=[smem()] * 2 + [vmem()] * 3 + [pl.BlockSpec(memory_space=pl.ANY)],
         out_specs=vmem(),
         scratch_shapes=[
             pltpu.VMEM((n * layers * tiles_here, slab_rows, tile_px), screens.dtype),
             pltpu.VMEM((frames * PT * SUB, LANES), f32),
-            pltpu.SemaphoreType.DMA((len(pieces),)),
+            pltpu.SMEM((n,), jnp.int32),
+            pltpu.SemaphoreType.DMA,
         ],
-        compiler_params=pltpu.CompilerParams(vmem_limit_bytes=32 << 20),
-    )(where[0], where[1], c0, c1, table["keep"], table["spread"], *pieces)
-    return jnp.stack([slopes_first, slopes_second], axis=0), science, c2.reshape(-1)
+        compiler_params=pltpu.CompilerParams(vmem_limit_bytes=60 << 20),
+        cost_estimate=pl.CostEstimate(
+            flops=8 * frames * SC_DEV * slab_rows * tile_px,
+            bytes_accessed=2 * (n * layers * tiles_here + frames * SC_DEV) * slab_rows * tile_px,
+            transcendentals=0,
+        ),
+    )(owners, tile_slot, c0, c1, table["mirror"], gathered)
+    updates = later(updates, science)
+    mine = lax.dynamic_slice_in_dim(c1, my_rec * block_rows, block_rows, 0)
+    c2 = mine + loop_gain * jnp.sum(updates, axis=0)
+    return jnp.stack([slopes_first, own_lanes(slopes_second)], axis=0), science, c2.reshape(-1)
 
 
 def per_device(screens, tile_owner, *rest):
     layers, tiles_here, _, _ = screens.shape
     frames, n = tile_owner.shape[0], lax.axis_size("tile")
     capacity = max(2, 3 * ITEMS // (2 * n))
-    few = tiles_here <= frames * capacity and n % 2 == 0 and frames == 2 and layers == 2
+    few = tiles_here <= frames * capacity and n & (n - 1) == 0 and frames == 2 and layers == 2
     return (by_ring if few else by_request)(screens, tile_owner, *rest)
 
 

time: 130 us -> 112 us (0.86)
  waiting for transfers between devices: 58 us -> 35.4 us
  between operations: 0.86 us -> 14.2 us
  blocking collectives: 5.6 us -> 0 us
  starting transfers between devices: 34 us -> 28.6 us
  Pallas kernels: 20.8 us -> 22.5 us
    all_to_all x1, waiting for transfers between devices: 16.4 us -> 0.01 us  [by_ring(): lax.all_to_all(updates, ('tile', 'rec'), split_axis=0, concat_axis=0, til...]
    all_to_all x4 -> x2, waiting for transfers between devices: 25.9 us -> 15.3 us  [exchange(): lax.all_to_all(payload, ('tile', 'rec'), split_axis=0, concat_axis=0, til...]
    ppermute x8 -> x9, waiting for transfers between devices: 9.66 us -> 20.1 us  [the longest x6 20.1 us: swap(): return lax.ppermute(x, 'tile', [(t, t ^ bit) for t in range(n)])]
    all_to_all x4 -> x2, starting transfers between devices: 17.8 us -> 8.99 us  [exchange(): lax.all_to_all(payload, ('tile', 'rec'), split_axis=0, concat_axis=0, til...]
    all_to_all x1, waiting for transfers between devices: 6.02 us -> 0.01 us  [by_ring(): lax.all_to_all(updates, 'tile', split_axis=0, concat_axis=0, tiled=True)]
    all_gather x1 -> x0, blocking collectives: 5.6 us -> none  [by_ring(): lax.all_gather(commands_init.reshape(-1, LANES), 'rec', axis=0, tiled=True)]
    ppermute x8 -> x9, starting transfers between devices: 10.3 us -> 13.7 us  [the longest x6 11.8 us: swap(): return lax.ppermute(x, 'tile', [(t, t ^ bit) for t in range(n)])]
    pallas_call x5 -> x9, Pallas kernels: 16.5 us -> 19.4 us  [the longest x1 8.06 us: by_ring(): pl.pallas_call(functools.partial(science_kernel, n, tiles_here), out_shap...]
  transfers between devices with their start and end apart: 14 -> 14, of which waited for: 7 -> 5; matrix products, arithmetic and copies ran while one was open for 5% -> 1% of each run, Pallas kernels for 11% -> 20%
where the time goes in v2:
time: 112 us; the launch traced here: 111 us
  waiting for transfers between devices  35.4 us (32%)
  starting transfers between devices  28.6 us (26%)
  Pallas kernels  22.5 us (20%)
  between operations  14.2 us (13%)
  local copies, waits for them, and re-layouts  8.4 us (8%)
  other arithmetic  1.9 us (2%)
    ppermute x6, waiting for transfers between devices, swap(): return lax.ppermute(x, 'tile', [(t, t ^ bit) for t in range(n)])  20.1 us
    all_to_all x2, waiting for transfers between devices, exchange(): lax.all_to_all(payload, ('tile', 'rec'), split_axis=0, concat_axis=0, til...  15.3 us
    ppermute x6, starting transfers between devices, swap(): return lax.ppermute(x, 'tile', [(t, t ^ bit) for t in range(n)])  11.8 us
    all_to_all x2, starting transfers between devices, exchange(): lax.all_to_all(payload, ('tile', 'rec'), split_axis=0, concat_axis=0, til...  8.99 us
    unnamed x33, local copies, waits for them, and re-layouts  8.25 us
    pallas_call x1, Pallas kernels, by_ring(): pl.pallas_call(functools.partial(science_kernel, n, tiles_here), out_shap...  8.06 us
    pallas_call x4, Pallas kernels, merge(): pl.pallas_call(functools.partial(merge_kernel, frame, bits), in_specs=[sm...  4.62 us
    all_to_all x1, starting transfers between devices, by_ring(): lax.all_to_all(updates, 'tile', split_axis=0, concat_axis=0, tiled=True)  3.33 us
  transfers between devices with their start and end apart: 14, of which 5 were waited for; matrix products, arithmetic and copies ran while one was open for 1% of the time, Pallas kernels for 20%

profile of v2, /device:TPU:0, one launch (start us, length us, event | category | flops | bytes accessed | tf_op | source)
XLA Modules:
  0.0 111.0 jit_solution(6327126043359595116)
XLA Ops:
  7.2 0.0 all-gather.3.cloned.1.call-start
  7.2 0.0 copy-start
  7.2 1.1 %copy-done = bf16[2,48,32,128]{3,2,1,0:T(8,128)(2,1)S(1)} copy-done((bf16[2,48,32,128]{3,2,1,0:T(8,128)(2,1)S(1)}, bf16[2,48,32,128]{3,2,1,0:T(8,128)(2,1)}, u32[]{:S(2)}) %copy-start) | copy-done | bytes 786456
  8.3 0.7 copy-done.7
  9.1 0.0 copy-start.11
  9.1 0.9 shard_map.103
  10.0 0.0 all-gather.3.cloned.1.call-update
  10.0 3.0 %collective-permute-start = (bf16[4,2,4,32,128]{4,3,2,1,0:T(8,128)(2,1)S(1)}, bf16[4,2,4,32,128]{4,3,2,1,0:T(8,128)(2,1)S(1)}, u32[]{:S(2)}, u32[]{:S(2)}) collective-permute-start(bf16[4,2,4,32,128]{4,3,2,1,0:T(8,128)(2,1)S(1)} %shard_map.103), channel_id=1, source_target_pairs={{0,4},{4,0},{8,12},{12,8},{16,20},{20,16},{24,28},{28,24},{1,5},{5... | collective-permute-start | bytes 786440 | tf_op jit(solution)/shard_map/ppermute | solution.py:475
  13.0 1.1 %copy-done.1 = bf16[2,48,32,128]{3,2,1,0:T(8,128)(2,1)S(1)} copy-done((bf16[2,48,32,128]{3,2,1,0:T(8,128)(2,1)S(1)}, bf16[2,48,32,128]{3,2,1,0:T(8,128)(2,1)}, u32[]{:S(2)}) %copy-start.1) | copy-done | bytes 786456
  14.2 0.7 copy-done.8
  14.9 0.9 shard_map.106
  15.8 0.1 collective-permute-start.2
  15.8 0.7 copy.13
  16.6 0.0 copy-start.6
  16.6 4.1 %collective-permute-done.received = bf16[4,2,4,32,128]{4,3,2,1,0:T(8,128)(2,1)S(1)} collective-permute-done((bf16[4,2,4,32,128]{4,3,2,1,0:T(8,128)(2,1)S(1)}, bf16[4,2,4,32,128]{4,3,2,1,0:T(8,128)(2,1)S(1)}, u32[]{:S(2)}, u32[]{:S(2)}) %collective-permute-start) | collective-permute-done | bytes 262176 | tf_op jit(solution)/shard_map/ppermute | solution.py:475
  20.7 1.2 %shard_map.104 = (bf16[2,2,4,32,128]{4,3,2,1,0:T(8,128)(2,1)S(1)}, bf16[2,2,4,32,128]{4,3,2,1,0:T(8,128)(2,1)S(1)}) custom-call(s32[2,2,1024]{2,1,0:T(2,128)S(1)} %bitcast.15, s32[2,2,1024]{2,1,0:T(2,128)S(1)} %copy-done.8, bf16[2,48,32,128]{3,2,1,0:T(8,128)(2,1)S(1)} %copy-done.1, bf16[4,2,4,32,128]{4,3,2,1,0:T(8,128)(2,1)S(1)} %collective-permute-done.received), custom_call_target="tpu_custom_call" | custom-call | tf_op jit(solution)/shard_map/pallas_call | solution.py:485
  21.9 1.6 %collective-permute-start.1 = (bf16[2,2,4,32,128]{4,3,2,1,0:T(8,128)(2,1)S(1)}, bf16[2,2,4,32,128]{4,3,2,1,0:T(8,128)(2,1)S(1)}, u32[]{:S(2)}, u32[]{:S(2)}) collective-permute-start(bf16[2,2,4,32,128]{4,3,2,1,0:T(8,128)(2,1)S(1)} %get-tuple-element.23), channel_id=1, source_target_pairs={{0,8},{4,12},{8,0},{12,4},{16,24},{20,28},{24,16},{28,20},{1,9},{5... | collective-permute-start | bytes 393224 | tf_op jit(solution)/shard_map/ppermute | solution.py:475
  23.5 6.5 %collective-permute-done.1.received = bf16[2,2,4,32,128]{4,3,2,1,0:T(8,128)(2,1)S(1)} collective-permute-done((bf16[2,2,4,32,128]{4,3,2,1,0:T(8,128)(2,1)S(1)}, bf16[2,2,4,32,128]{4,3,2,1,0:T(8,128)(2,1)S(1)}, u32[]{:S(2)}, u32[]{:S(2)}) %collective-permute-start.1) | collective-permute-done | bytes 131104 | tf_op jit(solution)/shard_map/ppermute | solution.py:475
  30.0 1.1 %shard_map.105 = (bf16[1,2,4,32,128]{4,3,2,1,0:T(8,128)(2,1)S(1)}, bf16[1,2,4,32,128]{4,3,2,1,0:T(8,128)(2,1)S(1)}) custom-call(s32[2,2,1024]{2,1,0:T(2,128)S(1)} %bitcast.16, s32[2,2,1024]{2,1,0:T(2,128)S(1)} %copy-done.8, bf16[2,2,4,32,128]{4,3,2,1,0:T(8,128)(2,1)S(1)} %get-tuple-element.22.mine, ...), custom_call_target="tpu_custom_call" | custom-call | tf_op jit(solution)/shard_map/pallas_call | solution.py:485
  31.2 2.6 %collective-permute-start.3 = (bf16[1,2,4,32,128]{4,3,2,1,0:T(8,128)(2,1)S(1)}, bf16[1,2,4,32,128]{4,3,2,1,0:T(8,128)(2,1)S(1)}, u32[]{:S(2)}, u32[]{:S(2)}) collective-permute-start(bf16[1,2,4,32,128]{4,3,2,1,0:T(8,128)(2,1)S(1)} %get-tuple-element.25), channel_id=1, source_target_pairs={{0,16},{4,20},{8,24},{12,28},{16,0},{20,4},{24,8},{28,12},{1,17},{... | collective-permute-start | bytes 196616 | tf_op jit(solution)/shard_map/ppermute | solution.py:475
  33.8 0.0 collective-permute-start.4
  33.8 1.5 %collective-permute-start.5 = (f32[8,128]{1,0:T(8,128)}, f32[8,128]{1,0:T(8,128)S(1)}, u32[]{:S(2)}, u32[]{:S(2)}) collective-permute-start(f32[8,128]{1,0:T(8,128)} %bitcast.26), channel_id=1, source_target_pairs={{0,2},{1,3},{2,0},{3,1},{4,6},{5,7},{6,4},{7,5},{8,10},{9,11},{10,... | collective-permute-start | bytes 12296 | tf_op jit(solution)/shard_map/ppermute | solution.py:516
  35.3 0.4 collective-permute-start.6
  35.7 0.0 collective-permute-done.2.received
  35.7 1.1 %copy-done.2 = bf16[2,48,32,128]{3,2,1,0:T(8,128)(2,1)S(1)} copy-done((bf16[2,48,32,128]{3,2,1,0:T(8,128)(2,1)S(1)}, bf16[2,48,32,128]{3,2,1,0:T(8,128)(2,1)}, u32[]{:S(2)}) %copy-start.2) | copy-done | bytes 786456
  36.8 1.2 %shard_map.107 = (bf16[2,2,4,32,128]{4,3,2,1,0:T(8,128)(2,1)S(1)}, bf16[2,2,4,32,128]{4,3,2,1,0:T(8,128)(2,1)S(1)}) custom-call(s32[2,2,1024]{2,1,0:T(2,128)S(1)} %bitcast.17, s32[2,2,1024]{2,1,0:T(2,128)S(1)} %copy-done.8, bf16[2,48,32,128]{3,2,1,0:T(8,128)(2,1)S(1)} %copy-done.2, bf16[4,2,4,32,128]{4,3,2,1,0:T(8,128)(2,1)S(1)} %collective-permute-done.2.received), custom_call_target="tpu_custom_call" | custom-call | tf_op jit(solution)/shard_map/pallas_call | solution.py:485
  38.0 1.7 %collective-permute-start.7 = (bf16[2,2,4,32,128]{4,3,2,1,0:T(8,128)(2,1)S(1)}, bf16[2,2,4,32,128]{4,3,2,1,0:T(8,128)(2,1)S(1)}, u32[]{:S(2)}, u32[]{:S(2)}) collective-permute-start(bf16[2,2,4,32,128]{4,3,2,1,0:T(8,128)(2,1)S(1)} %get-tuple-element.28), channel_id=1, source_target_pairs={{0,8},{4,12},{8,0},{12,4},{16,24},{20,28},{24,16},{28,20},{1,9},{5... | collective-permute-start | bytes 393224 | tf_op jit(solution)/shard_map/ppermute | solution.py:475
  39.7 0.0 collective-permute-done.4.refs_1_
  39.7 0.0 collective-permute-done.5.refs_2_
  39.7 0.0 collective-permute-done.6.refs_3_
  39.7 0.0 collective-permute-done.3.received
  39.7 0.0 copy-start.3
  39.7 1.1 copy-done.3
  40.8 0.9 copy-done.10
  41.7 0.7 copy-done.14
  42.4 2.5 %shard_map.108 = (f32[32,4,128]{2,1,0:T(4,128)}, f32[4,128]{1,0:T(4,128)S(1)}, f32[32,128]{1,0:T(8,128)S(1)}) custom-call(s32[2,2,1024]{2,1,0:T(2,128)S(1)} %bitcast.18, bf16[1,2,4,32,128]{4,3,2,1,0:T(8,128)(2,1)S(1)} %get-tuple-element.29.kept, bf16[1,2,4,32,128]{4,3,2,1,0:T(8,128)(2,1)S(1)} %collective-permute-done.3.received, f32[144,128]{1,0:T(8,128)S(1)} %copy-done.10, ...), custom_call_target="tpu_custom_call" | custom-call | bytes 11070000 | tf_op jit(solution)/shard_map/pallas_call | solution.py:522
  44.9 5.2 %all-to-all-start = ((f32[32,4,128]{2,1,0:T(4,128)}), f32[32,4,128]{2,1,0:T(4,128)S(1)}, u32[]{:S(2)}, u32[]{:S(2)}) async-start(f32[32,4,128]{2,1,0:T(4,128)} %get-tuple-element.35), calls=%async_computation | async-start | bytes 131072 | tf_op jit(solution)/shard_map/all_to_all | solution.py:454
  50.0 0.0 collective-permute-done.7.received
  50.0 0.0 copy-done.9
  50.1 1.1 %shard_map.109 = (bf16[1,2,4,32,128]{4,3,2,1,0:T(8,128)(2,1)S(1)}, bf16[1,2,4,32,128]{4,3,2,1,0:T(8,128)(2,1)S(1)}) custom-call(s32[2,2,1024]{2,1,0:T(2,128)S(1)} %bitcast.19, s32[2,2,1024]{2,1,0:T(2,128)S(1)} %copy-done.9, bf16[2,2,4,32,128]{4,3,2,1,0:T(8,128)(2,1)S(1)} %get-tuple-element.31.mine, ...), custom_call_target="tpu_custom_call" | custom-call | tf_op jit(solution)/shard_map/pallas_call | solution.py:485
  51.2 7.1 %all-to-all-done = f32[32,4,128]{2,1,0:T(4,128)S(1)} async-done(((f32[32,4,128]{2,1,0:T(4,128)}), f32[32,4,128]{2,1,0:T(4,128)S(1)}, u32[]{:S(2)}, u32[]{:S(2)}) %all-to-all-start) | async-done | bytes 65568 | tf_op jit(solution)/shard_map/all_to_all | solution.py:454
  58.3 0.0 copy-done.5
  58.3 0.0 copy-done.15
  58.3 1.6 %shard_map.110 = f32[32,8,128]{2,1,0:T(8,128)} custom-call(s32[2,8]{1,0:T(2,128)S(1)} %bitcast.29, f32[8,4,4,128]{3,2,1,0:T(4,128)S(1)} %bitcast.24, bf16[8,2,128,128]{3,2,1,0:T(8,128)(2,1)S(1)} %copy-done.5), custom_call_target="tpu_custom_call" | custom-call | bytes 7380000 | tf_op jit(solution)/shard_map/pallas_call | solution.py:458
  59.9 2.6 %all-to-all-start.1 = ((f32[32,8,128]{2,1,0:T(8,128)}), f32[32,8,128]{2,1,0:T(8,128)S(1)}, u32[]{:S(2)}, u32[]{:S(2)}) async-start(f32[32,8,128]{2,1,0:T(8,128)} %shard_map.110), calls=%async_computation.1 | async-start | bytes 262144 | tf_op jit(solution)/shard_map/all_to_all | solution.py:533
  62.5 2.7 %collective-permute-start.8 = (bf16[1,2,4,32,128]{4,3,2,1,0:T(8,128)(2,1)S(1)}, bf16[1,2,4,32,128]{4,3,2,1,0:T(8,128)(2,1)S(1)}, u32[]{:S(2)}, u32[]{:S(2)}) collective-permute-start(bf16[1,2,4,32,128]{4,3,2,1,0:T(8,128)(2,1)S(1)} %get-tuple-element.33), channel_id=1, source_target_pairs={{0,16},{4,20},{8,24},{12,28},{16,0},{20,4},{24,8},{28,12},{1,17},{... | collective-permute-start | bytes 196616 | tf_op jit(solution)/shard_map/ppermute | solution.py:475
  65.2 9.5 %collective-permute-done.8.received = bf16[1,2,4,32,128]{4,3,2,1,0:T(8,128)(2,1)S(1)} collective-permute-done((bf16[1,2,4,32,128]{4,3,2,1,0:T(8,128)(2,1)S(1)}, bf16[1,2,4,32,128]{4,3,2,1,0:T(8,128)(2,1)S(1)}, u32[]{:S(2)}, u32[]{:S(2)}) %collective-permute-start.8) | collective-permute-done | bytes 65568 | tf_op jit(solution)/shard_map/ppermute | solution.py:475
  74.7 0.0 all-to-all-done.1
  74.7 0.0 copy-done.4
  74.7 0.0 copy-done.11
  74.7 2.5 %shard_map.111 = (f32[32,4,128]{2,1,0:T(4,128)}, f32[4,128]{1,0:T(4,128)S(1)}, f32[32,128]{1,0:T(8,128)S(1)}) custom-call(s32[2,2,1024]{2,1,0:T(2,128)S(1)} %bitcast.20, bf16[1,2,4,32,128]{4,3,2,1,0:T(8,128)(2,1)S(1)} %get-tuple-element.32.kept, bf16[1,2,4,32,128]{4,3,2,1,0:T(8,128)(2,1)S(1)} %collective-permute-done.8.received, ...), custom_call_target="tpu_custom_call" | custom-call | bytes 11070000 | tf_op jit(solution)/shard_map/pallas_call | solution.py:536
  77.2 3.8 %all-to-all-start.2 = ((f32[32,4,128]{2,1,0:T(4,128)}), f32[32,4,128]{2,1,0:T(4,128)S(1)}, u32[]{:S(2)}, u32[]{:S(2)}) async-start(f32[32,4,128]{2,1,0:T(4,128)} %get-tuple-element.39), calls=%async_computation.2 | async-start | bytes 131072 | tf_op jit(solution)/shard_map/all_to_all | solution.py:454
  81.0 0.1 dynamic-slice_bitcast_fusion.1
  81.1 0.1 dynamic-slice_bitcast_fusion
  81.2 8.1 %all-to-all-done.2 = f32[32,4,128]{2,1,0:T(4,128)S(1)} async-done(((f32[32,4,128]{2,1,0:T(4,128)}), f32[32,4,128]{2,1,0:T(4,128)S(1)}, u32[]{:S(2)}, u32[]{:S(2)}) %all-to-all-start.2) | async-done | bytes 65568 | tf_op jit(solution)/shard_map/all_to_all | solution.py:454
  89.3 1.5 %shard_map.113 = f32[8,8,128]{2,1,0:T(8,128)} custom-call(s32[2,8]{1,0:T(2,128)S(1)} %bitcast.30, f32[8,4,4,128]{3,2,1,0:T(4,128)S(1)} %bitcast.23, bf16[8,2,128,128]{3,2,1,0:T(8,128)(2,1)S(1)} %copy-done.5), custom_call_target="tpu_custom_call" | custom-call | bytes 7380000 | tf_op jit(solution)/shard_map/pallas_call | solution.py:458
  90.9 3.3 %all-to-all-start.3 = ((f32[8,8,128]{2,1,0:T(8,128)}), f32[8,8,128]{2,1,0:T(8,128)S(1)}, u32[]{:S(2)}, u32[]{:S(2)}) async-start(f32[8,8,128]{2,1,0:T(8,128)} %shard_map.113), calls=%async_computation.3 | async-start | bytes 65536 | tf_op jit(solution)/shard_map/all_to_all | solution.py:546
  94.2 0.6 pad_maximum_fusion
  94.8 0.0 copy-done.6
  94.8 0.0 copy-done.12
  94.8 0.0 copy-done.13
  94.8 8.1 %shard_map.112 = bf16[2,124,32,128]{3,2,1,0:T(8,128)(2,1)} custom-call(s32[2,2,1024]{2,1,0:T(2,128)} %bitcast.21, s32[2,2,1024]{2,1,0:T(2,128)} %slots.13, f32[32,128]{1,0:T(8,128)} %copy-done.12, f32[32,128]{1,0:T(8,128)} %copy-done.13, f32[144,128]{1,0:T(8,128)} %constant.21.clone.mirror, bf16[768,32,128]{2,1,0:T(8,128)(2,1)} %bitcast.31), custom_call_target="tpu_custom_call" | custom-call | flops 8126464 | bytes 8323072 | tf_op jit(solution)/shard_map/pallas_call | solution.py:547
  102.9 0.0 all-to-all-done.3
  102.9 1.3 %add_bitcast_fusion = f32[1024]{0:T(1024)} fusion(f32[8,128]{1,0:T(8,128)S(1)} %reduce_sum.9, f32[32,128]{1,0:T(8,128)} %copy-done.13, s32[]{:T(128)S(6)} %select_n.8), kind=kLoop, calls=%fused_computation.2 | loop fusion | flops 2048 | bytes 12292 | tf_op jit(solution)/shard_map/reshape | solution.py:568
  (14 shorter events, 0.0 us)
Async XLA Ops:
  7.2 87.6 %all-gather.3.cloned.1.call-start = ((), (), s32[]{:S(2)}) async-start(), calls=%async_computation.4 | async-start | bytes 7077888 | tf_op jit(solution)/shard_map/all_gather | solution.py:519
  7.2 1.1 %copy-start = (bf16[2,48,32,128]{3,2,1,0:T(8,128)(2,1)S(1)}, bf16[2,48,32,128]{3,2,1,0:T(8,128)(2,1)}, u32[]{:S(2)}) copy-start(bf16[2,48,32,128]{3,2,1,0:T(8,128)(2,1)} %mine.2) | copy-start | bytes 2359300
  8.3 0.7 copy-start.7
  9.1 41.0 %copy-start.9 = (s32[2,2,1024]{2,1,0:T(2,128)S(1)}, s32[2,2,1024]{2,1,0:T(2,128)}, u32[]{:S(2)}) copy-start(s32[2,2,1024]{2,1,0:T(2,128)} %slots.13) | copy-start | bytes 49156
  9.1 49.3 %copy-start.5 = (bf16[8,2,128,128]{3,2,1,0:T(8,128)(2,1)S(1)}, bf16[8,2,128,128]{3,2,1,0:T(8,128)(2,1)}, u32[]{:S(2)}) copy-start(bf16[8,2,128,128]{3,2,1,0:T(8,128)(2,1)} %blocks.3) | copy-start | bytes 1572868
  9.1 49.3 %copy-start.15 = (s32[8,2]{0,1:T(2,128)S(1)}, s32[8,2]{0,1:T(2,128)}, u32[]{:S(2)}) copy-start(s32[8,2]{0,1:T(2,128)} %param.13) | copy-start | bytes 196
  9.1 65.6 %copy-start.4 = (bf16[1296,256]{1,0:T(8,128)(2,1)S(1)}, bf16[1296,256]{1,0:T(8,128)(2,1)}, u32[]{:S(2)}) copy-start(bf16[1296,256]{1,0:T(8,128)(2,1)} %constant.20.clone.table) | copy-start | bytes 1990660
  9.1 65.6 %copy-start.11 = (f32[144,128]{1,0:T(8,128)S(1)}, f32[144,128]{1,0:T(8,128)}, u32[]{:S(2)}) copy-start(f32[144,128]{1,0:T(8,128)} %constant.21.clone.mirror) | copy-start | bytes 221188
  10.0 10.7 %collective-permute-start = (bf16[4,2,4,32,128]{4,3,2,1,0:T(8,128)(2,1)S(1)}, bf16[4,2,4,32,128]{4,3,2,1,0:T(8,128)(2,1)S(1)}, u32[]{:S(2)}, u32[]{:S(2)}) collective-permute-start(bf16[4,2,4,32,128]{4,3,2,1,0:T(8,128)(2,1)S(1)} %shard_map.103), channel_id=1, source_target_pairs={{0,4},{4,0},{8,12},{12,8},{16,20},{20,16},{24,28},{28,24},{1,5},{5... | collective-permute-start | bytes 786440 | tf_op jit(solution)/shard_map/ppermute | solution.py:475
  13.0 1.1 %copy-start.1 = (bf16[2,48,32,128]{3,2,1,0:T(8,128)(2,1)S(1)}, bf16[2,48,32,128]{3,2,1,0:T(8,128)(2,1)}, u32[]{:S(2)}) copy-start(bf16[2,48,32,128]{3,2,1,0:T(8,128)(2,1)} %mine.2) | copy-start | bytes 2359300
  14.2 0.7 copy-start.8
  15.8 19.9 %collective-permute-start.2 = (bf16[4,2,4,32,128]{4,3,2,1,0:T(8,128)(2,1)S(1)}, bf16[4,2,4,32,128]{4,3,2,1,0:T(8,128)(2,1)S(1)}, u32[]{:S(2)}, u32[]{:S(2)}) collective-permute-start(bf16[4,2,4,32,128]{4,3,2,1,0:T(8,128)(2,1)S(1)} %shard_map.106), channel_id=1, source_target_pairs={{0,4},{4,0},{8,12},{12,8},{16,20},{20,16},{24,28},{28,24},{1,5},{5... | collective-permute-start | bytes 786440 | tf_op jit(solution)/shard_map/ppermute | solution.py:475
  16.6 78.2 %copy-start.6 = (s32[2,2,1024,1]{2,1,3,0:T(2,128)}, s32[2,2,1024,1]{2,1,3,0:T(2,128)S(1)}, u32[]{:S(2)}) copy-start(s32[2,2,1024,1]{2,1,3,0:T(2,128)S(1)} %copy.13) | copy-start | bytes 49156
  21.9 8.2 %collective-permute-start.1 = (bf16[2,2,4,32,128]{4,3,2,1,0:T(8,128)(2,1)S(1)}, bf16[2,2,4,32,128]{4,3,2,1,0:T(8,128)(2,1)S(1)}, u32[]{:S(2)}, u32[]{:S(2)}) collective-permute-start(bf16[2,2,4,32,128]{4,3,2,1,0:T(8,128)(2,1)S(1)} %get-tuple-element.23), channel_id=1, source_target_pairs={{0,8},{4,12},{8,0},{12,4},{16,24},{20,28},{24,16},{28,20},{1,9},{5... | collective-permute-start | bytes 393224 | tf_op jit(solution)/shard_map/ppermute | solution.py:475
  31.2 8.5 %collective-permute-start.3 = (bf16[1,2,4,32,128]{4,3,2,1,0:T(8,128)(2,1)S(1)}, bf16[1,2,4,32,128]{4,3,2,1,0:T(8,128)(2,1)S(1)}, u32[]{:S(2)}, u32[]{:S(2)}) collective-permute-start(bf16[1,2,4,32,128]{4,3,2,1,0:T(8,128)(2,1)S(1)} %get-tuple-element.25), channel_id=1, source_target_pairs={{0,16},{4,20},{8,24},{12,28},{16,0},{20,4},{24,8},{28,12},{1,17},{... | collective-permute-start | bytes 196616 | tf_op jit(solution)/shard_map/ppermute | solution.py:475
  33.8 5.9 %collective-permute-start.4 = (f32[8,128]{1,0:T(8,128)}, f32[8,128]{1,0:T(8,128)S(1)}, u32[]{:S(2)}, u32[]{:S(2)}) collective-permute-start(f32[8,128]{1,0:T(8,128)} %bitcast.25), channel_id=1, source_target_pairs={{0,1},{1,0},{2,3},{3,2},{4,5},{5,4},{6,7},{7,6},{8,9},{9,8},{10,11... | collective-permute-start | bytes 12296 | tf_op jit(solution)/shard_map/ppermute | solution.py:516
  33.8 5.9 %collective-permute-start.5 = (f32[8,128]{1,0:T(8,128)}, f32[8,128]{1,0:T(8,128)S(1)}, u32[]{:S(2)}, u32[]{:S(2)}) collective-permute-start(f32[8,128]{1,0:T(8,128)} %bitcast.26), channel_id=1, source_target_pairs={{0,2},{1,3},{2,0},{3,1},{4,6},{5,7},{6,4},{7,5},{8,10},{9,11},{10,... | collective-permute-start | bytes 12296 | tf_op jit(solution)/shard_map/ppermute | solution.py:516
  35.3 4.4 %collective-permute-start.6 = (f32[8,128]{1,0:T(8,128)}, f32[8,128]{1,0:T(8,128)S(1)}, u32[]{:S(2)}, u32[]{:S(2)}) collective-permute-start(f32[8,128]{1,0:T(8,128)} %bitcast.27), channel_id=1, source_target_pairs={{0,3},{1,2},{2,1},{3,0},{4,7},{5,6},{6,5},{7,4},{8,11},{9,10},{10,... | collective-permute-start | bytes 12296 | tf_op jit(solution)/shard_map/ppermute | solution.py:516
  35.7 1.1 %copy-start.2 = (bf16[2,48,32,128]{3,2,1,0:T(8,128)(2,1)S(1)}, bf16[2,48,32,128]{3,2,1,0:T(8,128)(2,1)}, u32[]{:S(2)}) copy-start(bf16[2,48,32,128]{3,2,1,0:T(8,128)(2,1)} %mine.2) | copy-start | bytes 2359300
  38.0 12.0 %collective-permute-start.7 = (bf16[2,2,4,32,128]{4,3,2,1,0:T(8,128)(2,1)S(1)}, bf16[2,2,4,32,128]{4,3,2,1,0:T(8,128)(2,1)S(1)}, u32[]{:S(2)}, u32[]{:S(2)}) collective-permute-start(bf16[2,2,4,32,128]{4,3,2,1,0:T(8,128)(2,1)S(1)} %get-tuple-element.28), channel_id=1, source_target_pairs={{0,8},{4,12},{8,0},{12,4},{16,24},{20,28},{24,16},{28,20},{1,9},{5... | collective-permute-start | bytes 393224 | tf_op jit(solution)/shard_map/ppermute | solution.py:475
  39.7 1.1 copy-start.3
  40.8 0.9 copy-start.10
  41.7 0.7 copy-start.14
  44.9 49.9 %copy-start.12 = (f32[32,128]{1,0:T(8,128)}, f32[32,128]{1,0:T(8,128)S(1)}, u32[]{:S(2)}) copy-start(f32[32,128]{1,0:T(8,128)S(1)} %get-tuple-element.34.c_base.c_first) | copy-start | bytes 49156
  44.9 13.5 %all-to-all-start = ((f32[32,4,128]{2,1,0:T(4,128)}), f32[32,4,128]{2,1,0:T(4,128)S(1)}, u32[]{:S(2)}, u32[]{:S(2)}) async-start(f32[32,4,128]{2,1,0:T(4,128)} %get-tuple-element.35), calls=%async_computation | async-start | bytes 131072 | tf_op jit(solution)/shard_map/all_to_all | solution.py:454
  59.9 14.8 %all-to-all-start.1 = ((f32[32,8,128]{2,1,0:T(8,128)}), f32[32,8,128]{2,1,0:T(8,128)S(1)}, u32[]{:S(2)}, u32[]{:S(2)}) async-start(f32[32,8,128]{2,1,0:T(8,128)} %shard_map.110), calls=%async_computation.1 | async-start | bytes 262144 | tf_op jit(solution)/shard_map/all_to_all | solution.py:533
  62.5 12.2 %collective-permute-start.8 = (bf16[1,2,4,32,128]{4,3,2,1,0:T(8,128)(2,1)S(1)}, bf16[1,2,4,32,128]{4,3,2,1,0:T(8,128)(2,1)S(1)}, u32[]{:S(2)}, u32[]{:S(2)}) collective-permute-start(bf16[1,2,4,32,128]{4,3,2,1,0:T(8,128)(2,1)S(1)} %get-tuple-element.33), channel_id=1, source_target_pairs={{0,16},{4,20},{8,24},{12,28},{16,0},{20,4},{24,8},{28,12},{1,17},{... | collective-permute-start | bytes 196616 | tf_op jit(solution)/shard_map/ppermute | solution.py:475
  77.2 17.6 %copy-start.13 = (f32[32,128]{1,0:T(8,128)}, f32[32,128]{1,0:T(8,128)S(1)}, u32[]{:S(2)}) copy-start(f32[32,128]{1,0:T(8,128)S(1)} %get-tuple-element.38.c_second) | copy-start | bytes 49156
  77.2 12.1 %all-to-all-start.2 = ((f32[32,4,128]{2,1,0:T(4,128)}), f32[32,4,128]{2,1,0:T(4,128)S(1)}, u32[]{:S(2)}, u32[]{:S(2)}) async-start(f32[32,4,128]{2,1,0:T(4,128)} %get-tuple-element.39), calls=%async_computation.2 | async-start | bytes 131072 | tf_op jit(solution)/shard_map/all_to_all | solution.py:454
  90.9 12.0 %all-to-all-start.3 = ((f32[8,8,128]{2,1,0:T(8,128)}), f32[8,8,128]{2,1,0:T(8,128)S(1)}, u32[]{:S(2)}, u32[]{:S(2)}) async-start(f32[8,8,128]{2,1,0:T(8,128)} %shard_map.113), calls=%async_computation.3 | async-start | bytes 65536 | tf_op jit(solution)/shard_map/all_to_all | solution.py:546
Sparse Core Ops, SparseCore 0:
  10.1 82.8 all-gather.2

commit v3 on v2

--- a/solution.py
+++ b/solution.py
@@ -267,15 +267,14 @@
 
 def offer_kernel(frame, slots, screens, out):
     partner = lax.axis_index("tile") ^ 1
-    count, layers = out.shape[0], out.shape[1]
-    for k in range(count):
+    for k in range(out.shape[0]):
         d = destination(partner, 1, k)
-        for l in range(layers):
+        for l in range(out.shape[1]):
             for i in range(LG_DEV):
                 out[k, l, i] = screens[l, slots[frame, l, d * ITEMS + i]]
 
 
-def merge_kernel(frame, bits, owners, slots, mine, received, send, keep):
+def merge_kernel(frame, bits, owners, slots, mine, received, send, keep, *flags):
     me = lax.axis_index("tile")
     count, layers = send.shape[0], send.shape[1]
     other = 1 << (bits - 1)
@@ -289,20 +288,21 @@
                     theirs = ((owners[frame, l, g] ^ me) & other) != 0
                     ours = mine[l, slots[frame, l, g]] if bits == 1 else mine[j, l, i]
                     out[k, l, i] = jnp.where(theirs, received[j, l, i], ours)
-
-
-def last_merge(frame, owners, kept, received):
-    me = lax.axis_index("tile")
-    layers = owners.shape[1]
-    other = lax.axis_size("tile") // 2
-    tiles = []
-    for i in range(LG_DEV):
-        row = []
+    for flag in flags:
         for l in range(layers):
-            theirs = ((owners[frame, l, me * ITEMS + i] ^ me) & other) != 0
-            row.append(jnp.where(theirs, received[0, l, i], kept[0, l, i]))
-        tiles.append(row)
-    return tiles
+            for i in range(LG_DEV):
+                theirs = ((owners[frame, l, me * ITEMS + i] ^ me) >> bits) & 1
+                flag[pl.ds(i * layers + l, 1), :] = jnp.full((1, LANES), theirs).astype(jnp.float32)
+
+
+def last_merge(kept, received, flags):
+    layers = kept.shape[1]
+
+    def tile(i, l):
+        theirs = flags[pl.ds(i * layers + l, 1), :] > 0.5
+        return jnp.where(theirs, received[0, l, i].astype(jnp.float32), kept[0, l, i].astype(jnp.float32))
+
+    return [[tile(i, l) for l in range(layers)] for i in range(LG_DEV)]
 
 
 def slopes_from(tiles, prof, table, payload, slopes):
@@ -346,27 +346,24 @@
     return lax.rem(my_tile * need, PT // per_row), need
 
 
-def first_slopes(owners, kept, received, mirror, table, *refs):
+def first_slopes(kept, received, flags, mirror, table, *refs):
     *c_parts, payload, slopes, c, prof = refs
     my_tile, my_rec = lax.axis_index("tile"), lax.axis_index("rec")
     for k, part in enumerate(c_parts):
         c[pl.ds((my_rec ^ k) * part.shape[0], part.shape[0]), :] = part[...]
     base, need = own_rows(my_tile)
     prof[...] = column_profiles(c[pl.ds(base, need), :], mirror)
-    tiles = last_merge(0, owners, kept, received)
+    tiles = last_merge(kept, received, flags)
     slopes_from(tiles, prof, table, payload, slopes)
 
 
-def ring_place(n, tile):
-    return jnp.where(lax.rem(tile, 2) == 0, tile // 2, n - 1 - tile // 2)
-
-
-def second_slopes(owners, kept, received, c_base, updates, mirror, table, payload, slopes, c_out, prof):
+def second_slopes(kept, received, flags, c_base, updates, mirror, table, payload, slopes, c_out, c_own, prof):
     my_tile = lax.axis_index("tile")
     c_out[...] = c_base[...] + loop_gain * jnp.sum(updates[...], axis=0).reshape(c_base.shape)
+    c_own[...] = c_out[pl.ds(lax.axis_index("rec") * c_own.shape[0], c_own.shape[0]), :]
     base, need = own_rows(my_tile)
     prof[...] = column_profiles(c_out[pl.ds(base, need), :], mirror)
-    tiles = last_merge(1, owners, kept, received)
+    tiles = last_merge(kept, received, flags)
     slopes_from(tiles, prof, table, payload, slopes)
 
 
@@ -385,20 +382,24 @@
     out[...] = jnp.broadcast_to(jnp.concatenate(rows, axis=0)[None], out.shape)
 
 
-def science_kernel(n, tiles_here, owners, slots, c_first, c_second, mirror, *refs):
-    gathered, out, store, prof, starts, sem = refs
-    layers = owners.shape[1]
+def science_kernel(places, c_first, c_second, mirror, gathered, out, store, prof, sem):
     slab_rows = out.shape[2]
     my_tile, my_rec = lax.axis_index("tile"), lax.axis_index("rec")
-    copy = pltpu.make_async_copy(gathered, store, sem)
-    copy.start()
-    for o in range(n):
-        starts[o] = ring_place(n, jnp.int32(o)) * layers * tiles_here
+    parts = sem.shape[0]
+    size = store.shape[0] // parts
+    copies = [
+        pltpu.make_async_copy(gathered.at[pl.ds(i * size, size)], store.at[pl.ds(i * size, size)], sem.at[i])
+        for i in range(parts)
+    ]
+    for copy in copies:
+        copy.start()
     weights = row_weights(my_rec, slab_rows)
     profile_rows = PT * SUB
     for f, c in enumerate((c_first, c_second)):
         prof[pl.ds(f * profile_rows, profile_rows)] = column_profiles(c[...], mirror)
-    copy.wait()
+    for copy in copies:
+        copy.wait()
+    layers = places.shape[0] // (out.shape[0] * SC_DEV)
     start = lax.rem(my_tile * SC_DEV, PT)
     for f in range(out.shape[0]):
 
@@ -410,10 +411,9 @@
             ]
             shape = jnp.concatenate(shapes, axis=0)
             for k in (q, q + PT)[: 1 + both]:
-                g = my_tile * ITEMS + LG_DEV + k
                 phase = None
                 for l in range(layers):
-                    tile = store[starts[owners[f, l, g]] + l * tiles_here + slots[f, l, g]].astype(jnp.float32)
+                    tile = store[places[(f * layers + l) * SC_DEV + k]].astype(jnp.float32)
                     phase = tile if phase is None else phase + tile
                 out[f, k] = (phase - shape).astype(jnp.bfloat16)
 
@@ -476,17 +476,24 @@
 
     def offer(frame, mine):
         (out,) = pl.pallas_call(
-            functools.partial(offer_kernel, frame), in_specs=[smem(), vmem()], compiler_params=limit, **tiles_of(n // 2)
+            functools.partial(offer_kernel, frame),
+            in_specs=[smem(), vmem()],
+            compiler_params=limit,
+            **tiles_of(n // 2),
         )(tile_slot, mine)
         return out
 
     def merge(frame, bits, mine, received):
         count = n >> (bits + 1)
+        outs = tiles_of(count, count)
+        if count == 1:
+            outs["out_shape"].append(jax.ShapeDtypeStruct((LG_DEV * layers, LANES), f32))
+            outs["out_specs"].append(vmem())
         return pl.pallas_call(
             functools.partial(merge_kernel, frame, bits),
             in_specs=[smem()] * 2 + [vmem()] * 2,
             compiler_params=limit,
-            **tiles_of(count, count),
+            **outs,
         )(owners, tile_slot, mine, received)
 
     def later(value, after):
@@ -497,63 +504,70 @@
         return lax.dynamic_slice_in_dim(slopes, my_rec * width, width, 1)
 
     last = n.bit_length() - 1
-    sent = [offer(0, screens)]
-    gathered_after = sent[0]
-    second = offer(1, later(screens, sent[0]))
-    kept, got = screens, swap(sent[0], 1)
-    for bits in range(1, last):
-        send, kept = merge(0, bits, kept, got)
-        got = swap(send, 1 << bits)
-    kept_second, got_second = later(screens, send), swap(second, 1)
-    for bits in range(1, last):
-        send, kept_second = merge(1, bits, kept_second, got_second)
-        got_second = swap(send, 1 << bits)
-        if bits == 1:
-            kept = later(kept, send)
-    guide = [(kept, got), (kept_second, got_second)]
     c_own = commands_init.reshape(-1, LANES)
     c_parts = [c_own] + [
         lax.ppermute(c_own, "rec", [(r, r ^ k) for r in range(rec_count)]) for k in range(1, rec_count)
     ]
-
-    gathered = lax.all_gather(later(screens, gathered_after), "tile", axis_index_groups=[ring])
+    wanted = offer(0, screens)
+    second = offer(1, later(screens, wanted))
+    kept, got = screens, swap(wanted, 1)
+    for bits in range(1, last):
+        send, kept, *flags = merge(0, bits, kept, got)
+        got = swap(send, 1 << bits)
+    guide = [(kept, got, *flags)]
+    kept, got = later(screens, send), swap(second, 1)
+    for bits in range(1, last):
+        send, kept, *flags = merge(1, bits, kept, got)
+        got = swap(send, 1 << bits)
+        if bits == 1:
+            guide[0] = (later(guide[0][0], send), *guide[0][1:])
+    guide.append((kept, got, *flags))
+
+    gathered = lax.all_gather(later(screens, wanted), "tile", axis_index_groups=[ring])
     gathered = gathered.reshape(n * layers * tiles_here, slab_rows, tile_px)
+
+    def own_items(x):
+        return lax.dynamic_slice_in_dim(x, my_tile * ITEMS + LG_DEV, SC_DEV, 2)
+
+    owner = own_items(owners)
+    at = jnp.where(owner % 2 == 0, owner // 2, n - 1 - owner // 2) * layers
+    places = (at + jnp.arange(layers, dtype=jnp.int32)[None, :, None]) * tiles_here + own_items(tile_slot)
+    places = places.reshape(-1)
 
     payload, slopes_first, c0 = pl.pallas_call(
         first_slopes,
         out_shape=payload_out + [jax.ShapeDtypeStruct((rec_count * block_rows, LANES), f32)],
-        in_specs=[smem()] + [vmem()] * (2 + rec_count + len(tables_in)),
+        in_specs=[vmem()] * (3 + rec_count + len(tables_in)),
         out_specs=[vmem()] * 3,
         scratch_shapes=[pltpu.VMEM((LG_DEV * SUB, LANES), f32)],
         compiler_params=limit,
         cost_estimate=microseconds(3),
-    )(owners, *guide[0], *tables_in, *c_parts)
+    )(*guide[0], *tables_in, *c_parts)
     slopes_first = own_lanes(slopes_first)
     updates = updates_of(later(exchange(payload), send), everyone)
     updates = lax.all_to_all(updates, ("tile", "rec"), split_axis=0, concat_axis=0, tiled=True)
     updates = updates.reshape(n, rec_count, block_rows, LANES)
 
-    payload, slopes_second, c1 = pl.pallas_call(
+    payload, slopes_second, c1, mine = pl.pallas_call(
         second_slopes,
-        out_shape=payload_out + [jax.ShapeDtypeStruct(c0.shape, f32)],
-        in_specs=[smem()] + [vmem()] * (4 + len(tables_in)),
-        out_specs=[vmem()] * 3,
+        out_shape=payload_out + [jax.ShapeDtypeStruct(r, f32) for r in (c0.shape, c_own.shape)],
+        in_specs=[vmem()] * (5 + len(tables_in)),
+        out_specs=[vmem()] * 4,
         scratch_shapes=[pltpu.VMEM((LG_DEV * SUB, LANES), f32)],
         compiler_params=limit,
         cost_estimate=microseconds(3),
-    )(owners, *guide[1], c0, updates, *tables_in)
+    )(*guide[1], c0, updates, *tables_in)
     updates = updates_of(exchange(payload), n)
     updates = lax.all_to_all(updates, "tile", split_axis=0, concat_axis=0, tiled=True)
     science = pl.pallas_call(
-        functools.partial(science_kernel, n, tiles_here),
+        science_kernel,
         out_shape=jax.ShapeDtypeStruct((frames, SC_DEV, slab_rows, tile_px), jnp.bfloat16),
-        in_specs=[smem()] * 2 + [vmem()] * 3 + [pl.BlockSpec(memory_space=pl.ANY)],
+        in_specs=[smem()] + [vmem()] * 3 + [pl.BlockSpec(memory_space=pl.ANY)],
         out_specs=vmem(),
         scratch_shapes=[
             pltpu.VMEM((n * layers * tiles_here, slab_rows, tile_px), screens.dtype),
             pltpu.VMEM((frames * PT * SUB, LANES), f32),
-            pltpu.SMEM((n,), jnp.int32),
-            pltpu.SemaphoreType.DMA,
+            pltpu.SemaphoreType.DMA((n,)),
         ],
         compiler_params=pltpu.CompilerParams(vmem_limit_bytes=60 << 20),
         cost_estimate=pl.CostEstimate(
@@ -561,9 +575,8 @@
             bytes_accessed=2 * (n * layers * tiles_here + frames * SC_DEV) * slab_rows * tile_px,
             transcendentals=0,
         ),
-    )(owners, tile_slot, c0, c1, table["mirror"], gathered)
+    )(places, c0, c1, table["mirror"], gathered)
     updates = later(updates, science)
-    mine = lax.dynamic_slice_in_dim(c1, my_rec * block_rows, block_rows, 0)
     c2 = mine + loop_gain * jnp.sum(updates, axis=0)
     return jnp.stack([slopes_first, own_lanes(slopes_second)], axis=0), science, c2.reshape(-1)
 

time: 112 us -> 109 us (0.973)
  Pallas kernels: 22.5 us -> 19.9 us
  local copies, waits for them, and re-layouts: 8.4 us -> 10.4 us
  waiting for transfers between devices: 35.4 us -> 34 us
    ppermute x6, waiting for transfers between devices: 20.1 us -> 18.7 us  [swap(): return lax.ppermute(x, 'tile', [(t, t ^ bit) for t in range(n)])]
    unnamed x33 -> x31, local copies, waits for them, and re-layouts: 8.25 us -> 8.83 us
  transfers between devices with their start and end apart: 14 -> 14, of which waited for: 5 -> 5; matrix products, arithmetic and copies ran while one was open for 1% -> 3% of each run, Pallas kernels for 20% -> 18%
where the time goes in v3:
time: 109 us; the launch traced here: 108 us
  waiting for transfers between devices  34 us (31%)
  starting transfers between devices  28.5 us (26%)
  Pallas kernels  19.9 us (18%)
  between operations  14.2 us (13%)
  local copies, waits for them, and re-layouts  10.4 us (10%)
  other arithmetic  1.29 us (1%)
    ppermute x6, waiting for transfers between devices, swap(): return lax.ppermute(x, 'tile', [(t, t ^ bit) for t in range(n)])  18.7 us
    all_to_all x2, waiting for transfers between devices, exchange(): lax.all_to_all(payload, ('tile', 'rec'), split_axis=0, concat_axis=0, til...  15.3 us
    ppermute x6, starting transfers between devices, swap(): return lax.ppermute(x, 'tile', [(t, t ^ bit) for t in range(n)])  11.7 us
    all_to_all x2, starting transfers between devices, exchange(): lax.all_to_all(payload, ('tile', 'rec'), split_axis=0, concat_axis=0, til...  8.93 us
    unnamed x31, local copies, waits for them, and re-layouts  8.83 us
    pallas_call x1, Pallas kernels, by_ring(): pl.pallas_call(science_kernel, out_shape=jax.ShapeDtypeStruct((frames, SC...  7.01 us
    pallas_call x4, Pallas kernels, merge(): pl.pallas_call(functools.partial(merge_kernel, frame, bits), in_specs=[sm...  4.65 us
    all_to_all x1, starting transfers between devices, by_ring(): lax.all_to_all(updates, 'tile', split_axis=0, concat_axis=0, tiled=True)  3.33 us
  transfers between devices with their start and end apart: 14, of which 5 were waited for; matrix products, arithmetic and copies ran while one was open for 3% of the time, Pallas kernels for 18%

profile of v3, /device:TPU:0, one launch (start us, length us, event | category | flops | bytes accessed | tf_op | source)
XLA Modules:
  0.0 108.3 jit_solution(16586630655583157636)
XLA Ops:
  7.2 0.0 all-gather.3.cloned.1.call-start
  7.2 0.0 copy-start
  7.2 1.1 %copy-done = bf16[2,48,32,128]{3,2,1,0:T(8,128)(2,1)S(1)} copy-done((bf16[2,48,32,128]{3,2,1,0:T(8,128)(2,1)S(1)}, bf16[2,48,32,128]{3,2,1,0:T(8,128)(2,1)}, u32[]{:S(2)}) %copy-start) | copy-done | bytes 786456
  8.3 0.7 copy-done.8
  9.1 0.0 copy-start.7
  9.1 0.9 shard_map.103
  10.0 0.0 all-gather.3.cloned.1.call-update
  10.0 3.0 %collective-permute-start = (bf16[4,2,4,32,128]{4,3,2,1,0:T(8,128)(2,1)S(1)}, bf16[4,2,4,32,128]{4,3,2,1,0:T(8,128)(2,1)S(1)}, u32[]{:S(2)}, u32[]{:S(2)}) collective-permute-start(bf16[4,2,4,32,128]{4,3,2,1,0:T(8,128)(2,1)S(1)} %shard_map.103), channel_id=1, source_target_pairs={{0,4},{4,0},{8,12},{12,8},{16,20},{20,16},{24,28},{28,24},{1,5},{5... | collective-permute-start | bytes 786440 | tf_op jit(solution)/shard_map/ppermute | solution.py:475
  13.0 1.1 %copy-done.1 = bf16[2,48,32,128]{3,2,1,0:T(8,128)(2,1)S(1)} copy-done((bf16[2,48,32,128]{3,2,1,0:T(8,128)(2,1)S(1)}, bf16[2,48,32,128]{3,2,1,0:T(8,128)(2,1)}, u32[]{:S(2)}) %copy-start.1) | copy-done | bytes 786456
  14.2 0.7 copy-done.9
  14.9 0.9 shard_map.106
  15.8 0.1 collective-permute-start.2
  15.8 0.7 copy.13
  16.6 4.1 %collective-permute-done.received = bf16[4,2,4,32,128]{4,3,2,1,0:T(8,128)(2,1)S(1)} collective-permute-done((bf16[4,2,4,32,128]{4,3,2,1,0:T(8,128)(2,1)S(1)}, bf16[4,2,4,32,128]{4,3,2,1,0:T(8,128)(2,1)S(1)}, u32[]{:S(2)}, u32[]{:S(2)}) %collective-permute-start) | collective-permute-done | bytes 262176 | tf_op jit(solution)/shard_map/ppermute | solution.py:475
  20.7 1.2 %shard_map.104 = (bf16[2,2,4,32,128]{4,3,2,1,0:T(8,128)(2,1)S(1)}, bf16[2,2,4,32,128]{4,3,2,1,0:T(8,128)(2,1)S(1)}) custom-call(s32[2,2,1024]{2,1,0:T(2,128)S(1)} %bitcast.17, s32[2,2,1024]{2,1,0:T(2,128)S(1)} %copy-done.9, bf16[2,48,32,128]{3,2,1,0:T(8,128)(2,1)S(1)} %copy-done.1, bf16[4,2,4,32,128]{4,3,2,1,0:T(8,128)(2,1)S(1)} %collective-permute-done.received), custom_call_target="tpu_custom_call" | custom-call | tf_op jit(solution)/shard_map/pallas_call | solution.py:492
  21.9 1.6 %collective-permute-start.1 = (bf16[2,2,4,32,128]{4,3,2,1,0:T(8,128)(2,1)S(1)}, bf16[2,2,4,32,128]{4,3,2,1,0:T(8,128)(2,1)S(1)}, u32[]{:S(2)}, u32[]{:S(2)}) collective-permute-start(bf16[2,2,4,32,128]{4,3,2,1,0:T(8,128)(2,1)S(1)} %get-tuple-element.26), channel_id=1, source_target_pairs={{0,8},{4,12},{8,0},{12,4},{16,24},{20,28},{24,16},{28,20},{1,9},{5... | collective-permute-start | bytes 393224 | tf_op jit(solution)/shard_map/ppermute | solution.py:475
  23.5 6.5 %collective-permute-done.1.received = bf16[2,2,4,32,128]{4,3,2,1,0:T(8,128)(2,1)S(1)} collective-permute-done((bf16[2,2,4,32,128]{4,3,2,1,0:T(8,128)(2,1)S(1)}, bf16[2,2,4,32,128]{4,3,2,1,0:T(8,128)(2,1)S(1)}, u32[]{:S(2)}, u32[]{:S(2)}) %collective-permute-start.1) | collective-permute-done | bytes 131104 | tf_op jit(solution)/shard_map/ppermute | solution.py:475
  30.0 1.1 %shard_map.105 = (bf16[1,2,4,32,128]{4,3,2,1,0:T(8,128)(2,1)S(1)}, bf16[1,2,4,32,128]{4,3,2,1,0:T(8,128)(2,1)S(1)}, f32[8,128]{1,0:T(8,128)S(1)}) custom-call(s32[2,2,1024]{2,1,0:T(2,128)S(1)} %bitcast.18, s32[2,2,1024]{2,1,0:T(2,128)S(1)} %copy-done.9, bf16[2,2,4,32,128]{4,3,2,1,0:T(8,128)(2,1)S(1)} %get-tuple-element.25.mine, ...), custom_call_target="tpu_custom_call" | custom-call | tf_op jit(solution)/shard_map/pallas_call | solution.py:492
  31.2 2.6 %collective-permute-start.3 = (bf16[1,2,4,32,128]{4,3,2,1,0:T(8,128)(2,1)S(1)}, bf16[1,2,4,32,128]{4,3,2,1,0:T(8,128)(2,1)S(1)}, u32[]{:S(2)}, u32[]{:S(2)}) collective-permute-start(bf16[1,2,4,32,128]{4,3,2,1,0:T(8,128)(2,1)S(1)} %get-tuple-element.28), channel_id=1, source_target_pairs={{0,16},{4,20},{8,24},{12,28},{16,0},{20,4},{24,8},{28,12},{1,17},{... | collective-permute-start | bytes 196616 | tf_op jit(solution)/shard_map/ppermute | solution.py:475
  33.8 0.0 collective-permute-start.4
  33.8 1.5 %collective-permute-start.5 = (f32[8,128]{1,0:T(8,128)}, f32[8,128]{1,0:T(8,128)S(1)}, u32[]{:S(2)}, u32[]{:S(2)}) collective-permute-start(f32[8,128]{1,0:T(8,128)} %bitcast.24), channel_id=1, source_target_pairs={{0,2},{1,3},{2,0},{3,1},{4,6},{5,7},{6,4},{7,5},{8,10},{9,11},{10,... | collective-permute-start | bytes 12296 | tf_op jit(solution)/shard_map/ppermute | solution.py:509
  35.3 0.4 collective-permute-start.6
  35.7 0.0 collective-permute-done.2.received
  35.7 1.1 %copy-done.2 = bf16[2,48,32,128]{3,2,1,0:T(8,128)(2,1)S(1)} copy-done((bf16[2,48,32,128]{3,2,1,0:T(8,128)(2,1)S(1)}, bf16[2,48,32,128]{3,2,1,0:T(8,128)(2,1)}, u32[]{:S(2)}) %copy-start.2) | copy-done | bytes 786456
  36.8 1.2 %shard_map.107 = (bf16[2,2,4,32,128]{4,3,2,1,0:T(8,128)(2,1)S(1)}, bf16[2,2,4,32,128]{4,3,2,1,0:T(8,128)(2,1)S(1)}) custom-call(s32[2,2,1024]{2,1,0:T(2,128)S(1)} %bitcast.19, s32[2,2,1024]{2,1,0:T(2,128)S(1)} %copy-done.9, bf16[2,48,32,128]{3,2,1,0:T(8,128)(2,1)S(1)} %copy-done.2, bf16[4,2,4,32,128]{4,3,2,1,0:T(8,128)(2,1)S(1)} %collective-permute-done.2.received), custom_call_target="tpu_custom_call" | custom-call | tf_op jit(solution)/shard_map/pallas_call | solution.py:492
  38.0 1.7 %collective-permute-start.7 = (bf16[2,2,4,32,128]{4,3,2,1,0:T(8,128)(2,1)S(1)}, bf16[2,2,4,32,128]{4,3,2,1,0:T(8,128)(2,1)S(1)}, u32[]{:S(2)}, u32[]{:S(2)}) collective-permute-start(bf16[2,2,4,32,128]{4,3,2,1,0:T(8,128)(2,1)S(1)} %get-tuple-element.31), channel_id=1, source_target_pairs={{0,8},{4,12},{8,0},{12,4},{16,24},{20,28},{24,16},{28,20},{1,9},{5... | collective-permute-start | bytes 393224 | tf_op jit(solution)/shard_map/ppermute | solution.py:475
  39.7 0.0 collective-permute-done.4.refs_1_
  39.7 0.0 collective-permute-done.5.refs_2_
  39.7 0.0 collective-permute-done.6.refs_3_
  39.7 0.0 collective-permute-done.3.received
  39.7 0.0 copy-start.3
  39.7 1.1 copy-done.3
  40.8 0.9 copy-done.6
  41.7 0.7 copy-done.13
  42.4 1.7 %shard_map.108 = (f32[32,4,128]{2,1,0:T(4,128)}, f32[4,128]{1,0:T(4,128)S(1)}, f32[32,128]{1,0:T(8,128)S(1)}) custom-call(bf16[1,2,4,32,128]{4,3,2,1,0:T(8,128)(2,1)S(1)} %get-tuple-element.32.kept, bf16[1,2,4,32,128]{4,3,2,1,0:T(8,128)(2,1)S(1)} %collective-permute-done.3.received, f32[8,128]{1,0:T(8,128)S(1)} %get-tuple-element.33.flags, ...), custom_call_target="tpu_custom_call" | custom-call | bytes 11070000 | tf_op jit(solution)/shard_map/pallas_call | solution.py:537
  44.1 5.2 %all-to-all-start = ((f32[32,4,128]{2,1,0:T(4,128)}), f32[32,4,128]{2,1,0:T(4,128)S(1)}, u32[]{:S(2)}, u32[]{:S(2)}) async-start(f32[32,4,128]{2,1,0:T(4,128)} %get-tuple-element.40), calls=%async_computation | async-start | bytes 131072 | tf_op jit(solution)/shard_map/all_to_all | solution.py:454
  49.3 0.0 collective-permute-done.7.received
  49.3 0.0 copy-done.10
  49.3 1.1 %shard_map.109 = (bf16[1,2,4,32,128]{4,3,2,1,0:T(8,128)(2,1)S(1)}, bf16[1,2,4,32,128]{4,3,2,1,0:T(8,128)(2,1)S(1)}, f32[8,128]{1,0:T(8,128)S(1)}) custom-call(s32[2,2,1024]{2,1,0:T(2,128)S(1)} %bitcast.20, s32[2,2,1024]{2,1,0:T(2,128)S(1)} %copy-done.10, bf16[2,2,4,32,128]{4,3,2,1,0:T(8,128)(2,1)S(1)} %get-tuple-element.35.mine, ...), custom_call_target="tpu_custom_call" | custom-call | tf_op jit(solution)/shard_map/pallas_call | solution.py:492
  50.4 7.1 %all-to-all-done = f32[32,4,128]{2,1,0:T(4,128)S(1)} async-done(((f32[32,4,128]{2,1,0:T(4,128)}), f32[32,4,128]{2,1,0:T(4,128)S(1)}, u32[]{:S(2)}, u32[]{:S(2)}) %all-to-all-start) | async-done | bytes 65568 | tf_op jit(solution)/shard_map/all_to_all | solution.py:454
  57.5 0.0 copy-done.5
  57.5 0.0 copy-done.14
  57.5 1.6 %shard_map.110 = f32[32,8,128]{2,1,0:T(8,128)} custom-call(s32[2,8]{1,0:T(2,128)S(1)} %bitcast.27, f32[8,4,4,128]{3,2,1,0:T(4,128)S(1)} %bitcast.22, bf16[8,2,128,128]{3,2,1,0:T(8,128)(2,1)S(1)} %copy-done.5), custom_call_target="tpu_custom_call" | custom-call | bytes 7380000 | tf_op jit(solution)/shard_map/pallas_call | solution.py:458
  59.1 2.6 %all-to-all-start.1 = ((f32[32,8,128]{2,1,0:T(8,128)}), f32[32,8,128]{2,1,0:T(8,128)S(1)}, u32[]{:S(2)}, u32[]{:S(2)}) async-start(f32[32,8,128]{2,1,0:T(8,128)} %shard_map.110), calls=%async_computation.1 | async-start | bytes 262144 | tf_op jit(solution)/shard_map/all_to_all | solution.py:548
  61.7 0.8 constant_dynamic-slice_fusion
  62.5 2.7 %collective-permute-start.8 = (bf16[1,2,4,32,128]{4,3,2,1,0:T(8,128)(2,1)S(1)}, bf16[1,2,4,32,128]{4,3,2,1,0:T(8,128)(2,1)S(1)}, u32[]{:S(2)}, u32[]{:S(2)}) collective-permute-start(bf16[1,2,4,32,128]{4,3,2,1,0:T(8,128)(2,1)S(1)} %get-tuple-element.37), channel_id=1, source_target_pairs={{0,16},{4,20},{8,24},{12,28},{16,0},{20,4},{24,8},{28,12},{1,17},{... | collective-permute-start | bytes 196616 | tf_op jit(solution)/shard_map/ppermute | solution.py:475
  65.1 0.1 dynamic-slice_add_fusion
  65.2 0.7 reshape.31.places
  65.9 8.1 %collective-permute-done.8.received = bf16[1,2,4,32,128]{4,3,2,1,0:T(8,128)(2,1)S(1)} collective-permute-done((bf16[1,2,4,32,128]{4,3,2,1,0:T(8,128)(2,1)S(1)}, bf16[1,2,4,32,128]{4,3,2,1,0:T(8,128)(2,1)S(1)}, u32[]{:S(2)}, u32[]{:S(2)}) %collective-permute-start.8) | collective-permute-done | bytes 65568 | tf_op jit(solution)/shard_map/ppermute | solution.py:475
  74.0 0.0 all-to-all-done.1
  74.0 0.0 copy-done.7
  74.0 1.7 %shard_map.111 = (f32[32,4,128]{2,1,0:T(4,128)}, f32[4,128]{1,0:T(4,128)S(1)}, f32[32,128]{1,0:T(8,128)S(1)}, f32[8,128]{1,0:T(8,128)S(1)}) custom-call(bf16[1,2,4,32,128]{4,3,2,1,0:T(8,128)(2,1)S(1)} %get-tuple-element.36.kept, bf16[1,2,4,32,128]{4,3,2,1,0:T(8,128)(2,1)S(1)} %collective-permute-done.8.received, f32[8,128]{1,0:T(8,128)S(1)} %get-tuple-element.38.flags, ...), custom_call_target="tpu_custom_call" | custom-call | bytes 11070000 | tf_op jit(solution)/shard_map/pallas_call | solution.py:551
  75.7 0.6 copy-done.12
  76.3 3.8 %all-to-all-start.2 = ((f32[32,4,128]{2,1,0:T(4,128)}), f32[32,4,128]{2,1,0:T(4,128)S(1)}, u32[]{:S(2)}, u32[]{:S(2)}) async-start(f32[32,4,128]{2,1,0:T(4,128)} %get-tuple-element.45), calls=%async_computation.2 | async-start | bytes 131072 | tf_op jit(solution)/shard_map/all_to_all | solution.py:454
  80.0 0.1 dynamic-slice_bitcast_fusion.1
  80.1 0.1 dynamic-slice_bitcast_fusion
  80.2 8.1 %all-to-all-done.2 = f32[32,4,128]{2,1,0:T(4,128)S(1)} async-done(((f32[32,4,128]{2,1,0:T(4,128)}), f32[32,4,128]{2,1,0:T(4,128)S(1)}, u32[]{:S(2)}, u32[]{:S(2)}) %all-to-all-start.2) | async-done | bytes 65568 | tf_op jit(solution)/shard_map/all_to_all | solution.py:454
  88.3 1.5 %shard_map.113 = f32[8,8,128]{2,1,0:T(8,128)} custom-call(s32[2,8]{1,0:T(2,128)S(1)} %bitcast.28, f32[8,4,4,128]{3,2,1,0:T(4,128)S(1)} %bitcast.21, bf16[8,2,128,128]{3,2,1,0:T(8,128)(2,1)S(1)} %copy-done.5), custom_call_target="tpu_custom_call" | custom-call | bytes 7380000 | tf_op jit(solution)/shard_map/pallas_call | solution.py:458
  89.9 3.3 %all-to-all-start.3 = ((f32[8,8,128]{2,1,0:T(8,128)}), f32[8,8,128]{2,1,0:T(8,128)S(1)}, u32[]{:S(2)}, u32[]{:S(2)}) async-start(f32[8,8,128]{2,1,0:T(8,128)} %shard_map.113), calls=%async_computation.3 | async-start | bytes 65536 | tf_op jit(solution)/shard_map/all_to_all | solution.py:561
  93.2 0.6 pad_maximum_fusion
  93.8 0.0 copy-done.11
  93.8 7.0 %shard_map.112 = bf16[2,124,32,128]{3,2,1,0:T(8,128)(2,1)} custom-call(s32[496]{0:T(512)} %reshape.31.places, f32[32,128]{1,0:T(8,128)} %copy-done.11, f32[32,128]{1,0:T(8,128)} %copy-done.12, f32[144,128]{1,0:T(8,128)} %constant.63.clone.mirror, bf16[768,32,128]{2,1,0:T(8,128)(2,1)} %bitcast.29), custom_call_target="tpu_custom_call" | custom-call | flops 8126464 | bytes 8323072 | tf_op jit(solution)/shard_map/pallas_call | solution.py:562
  100.8 0.0 all-to-all-done.3
  100.9 0.6 add_bitcast_fusion
  (15 shorter events, 0.0 us)
Async XLA Ops:
  7.2 86.6 %all-gather.3.cloned.1.call-start = ((), (), s32[]{:S(2)}) async-start(), calls=%async_computation.4 | async-start | bytes 7077888 | tf_op jit(solution)/shard_map/all_gather | solution.py:526
  7.2 1.1 %copy-start = (bf16[2,48,32,128]{3,2,1,0:T(8,128)(2,1)S(1)}, bf16[2,48,32,128]{3,2,1,0:T(8,128)(2,1)}, u32[]{:S(2)}) copy-start(bf16[2,48,32,128]{3,2,1,0:T(8,128)(2,1)} %mine.2) | copy-start | bytes 2359300
  8.3 0.7 copy-start.8
  9.1 40.2 %copy-start.10 = (s32[2,2,1024]{2,1,0:T(2,128)S(1)}, s32[2,2,1024]{2,1,0:T(2,128)}, u32[]{:S(2)}) copy-start(s32[2,2,1024]{2,1,0:T(2,128)} %slots.11) | copy-start | bytes 49156
  9.1 48.5 %copy-start.5 = (bf16[8,2,128,128]{3,2,1,0:T(8,128)(2,1)S(1)}, bf16[8,2,128,128]{3,2,1,0:T(8,128)(2,1)}, u32[]{:S(2)}) copy-start(bf16[8,2,128,128]{3,2,1,0:T(8,128)(2,1)} %blocks.3) | copy-start | bytes 1572868
  9.1 48.5 %copy-start.14 = (s32[8,2]{0,1:T(2,128)S(1)}, s32[8,2]{0,1:T(2,128)}, u32[]{:S(2)}) copy-start(s32[8,2]{0,1:T(2,128)} %param.13) | copy-start | bytes 196
  9.1 64.9 %copy-start.4 = (bf16[1296,256]{1,0:T(8,128)(2,1)S(1)}, bf16[1296,256]{1,0:T(8,128)(2,1)}, u32[]{:S(2)}) copy-start(bf16[1296,256]{1,0:T(8,128)(2,1)} %constant.62.clone.table) | copy-start | bytes 1990660
  9.1 64.9 %copy-start.7 = (f32[144,128]{1,0:T(8,128)S(1)}, f32[144,128]{1,0:T(8,128)}, u32[]{:S(2)}) copy-start(f32[144,128]{1,0:T(8,128)} %constant.63.clone.mirror) | copy-start | bytes 221188
  10.0 10.7 %collective-permute-start = (bf16[4,2,4,32,128]{4,3,2,1,0:T(8,128)(2,1)S(1)}, bf16[4,2,4,32,128]{4,3,2,1,0:T(8,128)(2,1)S(1)}, u32[]{:S(2)}, u32[]{:S(2)}) collective-permute-start(bf16[4,2,4,32,128]{4,3,2,1,0:T(8,128)(2,1)S(1)} %shard_map.103), channel_id=1, source_target_pairs={{0,4},{4,0},{8,12},{12,8},{16,20},{20,16},{24,28},{28,24},{1,5},{5... | collective-permute-start | bytes 786440 | tf_op jit(solution)/shard_map/ppermute | solution.py:475
  13.0 1.1 %copy-start.1 = (bf16[2,48,32,128]{3,2,1,0:T(8,128)(2,1)S(1)}, bf16[2,48,32,128]{3,2,1,0:T(8,128)(2,1)}, u32[]{:S(2)}) copy-start(bf16[2,48,32,128]{3,2,1,0:T(8,128)(2,1)} %mine.2) | copy-start | bytes 2359300
  14.2 0.7 copy-start.9
  15.8 19.9 %collective-permute-start.2 = (bf16[4,2,4,32,128]{4,3,2,1,0:T(8,128)(2,1)S(1)}, bf16[4,2,4,32,128]{4,3,2,1,0:T(8,128)(2,1)S(1)}, u32[]{:S(2)}, u32[]{:S(2)}) collective-permute-start(bf16[4,2,4,32,128]{4,3,2,1,0:T(8,128)(2,1)S(1)} %shard_map.106), channel_id=1, source_target_pairs={{0,4},{4,0},{8,12},{12,8},{16,20},{20,16},{24,28},{28,24},{1,5},{5... | collective-permute-start | bytes 786440 | tf_op jit(solution)/shard_map/ppermute | solution.py:475
  21.9 8.2 %collective-permute-start.1 = (bf16[2,2,4,32,128]{4,3,2,1,0:T(8,128)(2,1)S(1)}, bf16[2,2,4,32,128]{4,3,2,1,0:T(8,128)(2,1)S(1)}, u32[]{:S(2)}, u32[]{:S(2)}) collective-permute-start(bf16[2,2,4,32,128]{4,3,2,1,0:T(8,128)(2,1)S(1)} %get-tuple-element.26), channel_id=1, source_target_pairs={{0,8},{4,12},{8,0},{12,4},{16,24},{20,28},{24,16},{28,20},{1,9},{5... | collective-permute-start | bytes 393224 | tf_op jit(solution)/shard_map/ppermute | solution.py:475
  31.2 8.5 %collective-permute-start.3 = (bf16[1,2,4,32,128]{4,3,2,1,0:T(8,128)(2,1)S(1)}, bf16[1,2,4,32,128]{4,3,2,1,0:T(8,128)(2,1)S(1)}, u32[]{:S(2)}, u32[]{:S(2)}) collective-permute-start(bf16[1,2,4,32,128]{4,3,2,1,0:T(8,128)(2,1)S(1)} %get-tuple-element.28), channel_id=1, source_target_pairs={{0,16},{4,20},{8,24},{12,28},{16,0},{20,4},{24,8},{28,12},{1,17},{... | collective-permute-start | bytes 196616 | tf_op jit(solution)/shard_map/ppermute | solution.py:475
  33.8 5.9 %collective-permute-start.4 = (f32[8,128]{1,0:T(8,128)}, f32[8,128]{1,0:T(8,128)S(1)}, u32[]{:S(2)}, u32[]{:S(2)}) collective-permute-start(f32[8,128]{1,0:T(8,128)} %bitcast.23), channel_id=1, source_target_pairs={{0,1},{1,0},{2,3},{3,2},{4,5},{5,4},{6,7},{7,6},{8,9},{9,8},{10,11... | collective-permute-start | bytes 12296 | tf_op jit(solution)/shard_map/ppermute | solution.py:509
  33.8 5.9 %collective-permute-start.5 = (f32[8,128]{1,0:T(8,128)}, f32[8,128]{1,0:T(8,128)S(1)}, u32[]{:S(2)}, u32[]{:S(2)}) collective-permute-start(f32[8,128]{1,0:T(8,128)} %bitcast.24), channel_id=1, source_target_pairs={{0,2},{1,3},{2,0},{3,1},{4,6},{5,7},{6,4},{7,5},{8,10},{9,11},{10,... | collective-permute-start | bytes 12296 | tf_op jit(solution)/shard_map/ppermute | solution.py:509
  35.3 4.4 %collective-permute-start.6 = (f32[8,128]{1,0:T(8,128)}, f32[8,128]{1,0:T(8,128)S(1)}, u32[]{:S(2)}, u32[]{:S(2)}) collective-permute-start(f32[8,128]{1,0:T(8,128)} %bitcast.25), channel_id=1, source_target_pairs={{0,3},{1,2},{2,1},{3,0},{4,7},{5,6},{6,5},{7,4},{8,11},{9,10},{10,... | collective-permute-start | bytes 12296 | tf_op jit(solution)/shard_map/ppermute | solution.py:509
  35.7 1.1 %copy-start.2 = (bf16[2,48,32,128]{3,2,1,0:T(8,128)(2,1)S(1)}, bf16[2,48,32,128]{3,2,1,0:T(8,128)(2,1)}, u32[]{:S(2)}) copy-start(bf16[2,48,32,128]{3,2,1,0:T(8,128)(2,1)} %mine.2) | copy-start | bytes 2359300
  38.0 11.3 %collective-permute-start.7 = (bf16[2,2,4,32,128]{4,3,2,1,0:T(8,128)(2,1)S(1)}, bf16[2,2,4,32,128]{4,3,2,1,0:T(8,128)(2,1)S(1)}, u32[]{:S(2)}, u32[]{:S(2)}) collective-permute-start(bf16[2,2,4,32,128]{4,3,2,1,0:T(8,128)(2,1)S(1)} %get-tuple-element.31), channel_id=1, source_target_pairs={{0,8},{4,12},{8,0},{12,4},{16,24},{20,28},{24,16},{28,20},{1,9},{5... | collective-permute-start | bytes 393224 | tf_op jit(solution)/shard_map/ppermute | solution.py:475
  39.7 1.1 %copy-start.3 = (bf16[1296,256]{1,0:T(8,128)(2,1)S(1)}, bf16[1296,256]{1,0:T(8,128)(2,1)}, u32[]{:S(2)}) copy-start(bf16[1296,256]{1,0:T(8,128)(2,1)} %constant.62.clone.table) | copy-start | bytes 1990660
  40.8 0.9 copy-start.6
  41.7 0.7 copy-start.13
  44.1 49.7 %copy-start.11 = (f32[32,128]{1,0:T(8,128)}, f32[32,128]{1,0:T(8,128)S(1)}, u32[]{:S(2)}) copy-start(f32[32,128]{1,0:T(8,128)S(1)} %get-tuple-element.39.c_base.c_first) | copy-start | bytes 49156
  44.1 13.5 %all-to-all-start = ((f32[32,4,128]{2,1,0:T(4,128)}), f32[32,4,128]{2,1,0:T(4,128)S(1)}, u32[]{:S(2)}, u32[]{:S(2)}) async-start(f32[32,4,128]{2,1,0:T(4,128)} %get-tuple-element.40), calls=%async_computation | async-start | bytes 131072 | tf_op jit(solution)/shard_map/all_to_all | solution.py:454
  59.1 14.8 %all-to-all-start.1 = ((f32[32,8,128]{2,1,0:T(8,128)}), f32[32,8,128]{2,1,0:T(8,128)S(1)}, u32[]{:S(2)}, u32[]{:S(2)}) async-start(f32[32,8,128]{2,1,0:T(8,128)} %shard_map.110), calls=%async_computation.1 | async-start | bytes 262144 | tf_op jit(solution)/shard_map/all_to_all | solution.py:548
  62.5 11.5 %collective-permute-start.8 = (bf16[1,2,4,32,128]{4,3,2,1,0:T(8,128)(2,1)S(1)}, bf16[1,2,4,32,128]{4,3,2,1,0:T(8,128)(2,1)S(1)}, u32[]{:S(2)}, u32[]{:S(2)}) collective-permute-start(bf16[1,2,4,32,128]{4,3,2,1,0:T(8,128)(2,1)S(1)} %get-tuple-element.37), channel_id=1, source_target_pairs={{0,16},{4,20},{8,24},{12,28},{16,0},{20,4},{24,8},{28,12},{1,17},{... | collective-permute-start | bytes 196616 | tf_op jit(solution)/shard_map/ppermute | solution.py:475
  75.7 0.6 copy-start.12
  76.3 12.1 %all-to-all-start.2 = ((f32[32,4,128]{2,1,0:T(4,128)}), f32[32,4,128]{2,1,0:T(4,128)S(1)}, u32[]{:S(2)}, u32[]{:S(2)}) async-start(f32[32,4,128]{2,1,0:T(4,128)} %get-tuple-element.45), calls=%async_computation.2 | async-start | bytes 131072 | tf_op jit(solution)/shard_map/all_to_all | solution.py:454
  89.9 11.0 %all-to-all-start.3 = ((f32[8,8,128]{2,1,0:T(8,128)}), f32[8,8,128]{2,1,0:T(8,128)S(1)}, u32[]{:S(2)}, u32[]{:S(2)}) async-start(f32[8,8,128]{2,1,0:T(8,128)} %shard_map.113), calls=%async_computation.3 | async-start | bytes 65536 | tf_op jit(solution)/shard_map/all_to_all | solution.py:561
Sparse Core Ops, SparseCore 0:
  10.1 82.8 all-gather.2

commit v4 on v3

--- a/solution.py
+++ b/solution.py
@@ -274,6 +274,15 @@
                 out[k, l, i] = screens[l, slots[frame, l, d * ITEMS + i]]
 
 
+def stage_kernel(count, *refs):
+    inputs, outs, sem = refs[:count], refs[count + 1 : -1], refs[-1]
+    copies = [pltpu.make_async_copy(x, y, sem.at[i]) for i, (x, y) in enumerate(zip(inputs, outs))]
+    for copy in copies:
+        copy.start()
+    for copy in copies:
+        copy.wait()
+
+
 def merge_kernel(frame, bits, owners, slots, mine, received, send, keep, *flags):
     me = lax.axis_index("tile")
     count, layers = send.shape[0], send.shape[1]
@@ -382,10 +391,10 @@
     out[...] = jnp.broadcast_to(jnp.concatenate(rows, axis=0)[None], out.shape)
 
 
-def science_kernel(places, c_first, c_second, mirror, gathered, out, store, prof, sem):
+def science_kernel(places, c_first, c_second, mirror, gathered, out, store, ready, prof, sem):
     slab_rows = out.shape[2]
     my_tile, my_rec = lax.axis_index("tile"), lax.axis_index("rec")
-    parts = sem.shape[0]
+    parts = sem.shape[0] - out.shape[0]
     size = store.shape[0] // parts
     copies = [
         pltpu.make_async_copy(gathered.at[pl.ds(i * size, size)], store.at[pl.ds(i * size, size)], sem.at[i])
@@ -401,32 +410,40 @@
         copy.wait()
     layers = places.shape[0] // (out.shape[0] * SC_DEV)
     start = lax.rem(my_tile * SC_DEV, PT)
+    written = []
     for f in range(out.shape[0]):
 
-        def one(q, both):
-            row = f * profile_rows + lax.rem(start + q, PT) * SUB
-            shapes = [
-                w0 * prof[pl.ds(row + a0, 1), :] + w1 * prof[pl.ds(row + a1, 1), :]
-                for (a0, w0), (a1, w1) in weights
-            ]
-            shape = jnp.concatenate(shapes, axis=0)
-            for k in (q, q + PT)[: 1 + both]:
-                phase = None
-                for l in range(layers):
-                    tile = store[places[(f * layers + l) * SC_DEV + k]].astype(jnp.float32)
-                    phase = tile if phase is None else phase + tile
-                out[f, k] = (phase - shape).astype(jnp.bfloat16)
+        def some(qs):
+            results = []
+            for q in qs:
+                row = f * profile_rows + lax.rem(start + q, PT) * SUB
+                shapes = [
+                    w0 * prof[pl.ds(row + a0, 1), :] + w1 * prof[pl.ds(row + a1, 1), :]
+                    for (a0, w0), (a1, w1) in weights
+                ]
+                shape = jnp.concatenate(shapes, axis=0)
+                both = not isinstance(q, int) or q + PT < SC_DEV
+                for k in (q, q + PT)[: 1 + both]:
+                    phase = None
+                    for l in range(layers):
+                        tile = store[places[(f * layers + l) * SC_DEV + k]].astype(jnp.float32)
+                        phase = tile if phase is None else phase + tile
+                    results.append((k, (phase - shape).astype(jnp.bfloat16)))
+            for k, value in results:
+                ready[f, k] = value
 
         twice = SC_DEV - PT
-        together = 4
+        together = 6
 
         @pl.loop(0, twice // together)
         def _(q):
-            for j in range(together):
-                one(q * together + j, True)
-
-        for q in range(twice // together * together, PT):
-            one(q, q < twice)
+            some([q * together + j for j in range(together)])
+
+        some(range(twice // together * together, PT))
+        written.append(pltpu.make_async_copy(ready.at[f], out.at[f], sem.at[parts + f]))
+        written[-1].start()
+    for copy in written:
+        copy.wait()
 
 
 def by_ring(screens, tile_owner, tile_slot, commands_init, reconstructor, pattern):
@@ -510,12 +527,23 @@
     ]
     wanted = offer(0, screens)
     second = offer(1, later(screens, wanted))
-    kept, got = screens, swap(wanted, 1)
+    arrays = tables_in + [c_own, screens]
+    staged = pl.pallas_call(
+        functools.partial(stage_kernel, len(arrays)),
+        out_shape=[jax.ShapeDtypeStruct(x.shape, x.dtype) for x in arrays],
+        in_specs=[pl.BlockSpec(memory_space=pl.ANY)] * (len(arrays) + 1),
+        out_specs=[vmem()] * len(arrays),
+        scratch_shapes=[pltpu.SemaphoreType.DMA((len(arrays),))],
+        compiler_params=limit,
+    )(*arrays, second)
+    tables_in, c_parts[0] = staged[:2], staged[2]
+    near = staged[3]
+    kept, got = near, later(swap(wanted, 1), staged[0])
     for bits in range(1, last):
         send, kept, *flags = merge(0, bits, kept, got)
         got = swap(send, 1 << bits)
     guide = [(kept, got, *flags)]
-    kept, got = later(screens, send), swap(second, 1)
+    kept, got = near, later(swap(second, 1), send)
     for bits in range(1, last):
         send, kept, *flags = merge(1, bits, kept, got)
         got = swap(send, 1 << bits)
@@ -563,11 +591,12 @@
         science_kernel,
         out_shape=jax.ShapeDtypeStruct((frames, SC_DEV, slab_rows, tile_px), jnp.bfloat16),
         in_specs=[smem()] + [vmem()] * 3 + [pl.BlockSpec(memory_space=pl.ANY)],
-        out_specs=vmem(),
+        out_specs=pl.BlockSpec(memory_space=pl.ANY),
         scratch_shapes=[
             pltpu.VMEM((n * layers * tiles_here, slab_rows, tile_px), screens.dtype),
+            pltpu.VMEM((frames, SC_DEV, slab_rows, tile_px), jnp.bfloat16),
             pltpu.VMEM((frames * PT * SUB, LANES), f32),
-            pltpu.SemaphoreType.DMA((n,)),
+            pltpu.SemaphoreType.DMA((n + frames,)),
         ],
         compiler_params=pltpu.CompilerParams(vmem_limit_bytes=60 << 20),
         cost_estimate=pl.CostEstimate(

time: 109 us -> 108 us (level)
  waiting for transfers between devices: 34 us -> 30.4 us
  starting transfers between devices: 28.5 us -> 30.1 us
    ppermute x6, waiting for transfers between devices: 18.7 us -> 14.7 us  [swap(): return lax.ppermute(x, 'tile', [(t, t ^ bit) for t in range(n)])]
    unnamed x31 -> x29, local copies, waits for them, and re-layouts: 8.83 us -> 9.54 us
where the time goes in v4:
time: 108 us; the launch traced here: 107 us
  waiting for transfers between devices  30.4 us (28%)
  starting transfers between devices  30.1 us (28%)
  Pallas kernels  19.9 us (18%)
  between operations  14.2 us (13%)
  local copies, waits for them, and re-layouts  11.1 us (10%)
  other arithmetic  1.29 us (1%)
    all_to_all x2, waiting for transfers between devices, exchange(): lax.all_to_all(payload, ('tile', 'rec'), split_axis=0, concat_axis=0, til...  15.3 us
    ppermute x6, waiting for transfers between devices, swap(): return lax.ppermute(x, 'tile', [(t, t ^ bit) for t in range(n)])  14.7 us
    ppermute x6, starting transfers between devices, swap(): return lax.ppermute(x, 'tile', [(t, t ^ bit) for t in range(n)])  12.6 us
    all_to_all x2, starting transfers between devices, exchange(): lax.all_to_all(payload, ('tile', 'rec'), split_axis=0, concat_axis=0, til...  9.75 us
    unnamed x29, local copies, waits for them, and re-layouts  9.54 us
    pallas_call x1, Pallas kernels, by_ring(): pl.pallas_call(science_kernel, out_shape=jax.ShapeDtypeStruct((frames, SC...  6.59 us
    pallas_call x4, Pallas kernels, merge(): pl.pallas_call(functools.partial(merge_kernel, frame, bits), in_specs=[sm...  4.65 us
    all_to_all x1, starting transfers between devices, by_ring(): lax.all_to_all(updates, 'tile', split_axis=0, concat_axis=0, tiled=True)  3.33 us
  transfers between devices with their start and end apart: 14, of which 5 were waited for; matrix products, arithmetic and copies ran while one was open for 3% of the time, Pallas kernels for 18%

profile of v4, /device:TPU:0, one launch (start us, length us, event | category | flops | bytes accessed | tf_op | source)
XLA Modules:
  0.0 107.1 jit_solution(1238525999102786966)
XLA Ops:
  7.2 0.0 all-gather.3.cloned.1.call-start
  7.2 0.0 copy-start
  7.2 1.1 %copy-done = bf16[2,48,32,128]{3,2,1,0:T(8,128)(2,1)S(1)} copy-done((bf16[2,48,32,128]{3,2,1,0:T(8,128)(2,1)S(1)}, bf16[2,48,32,128]{3,2,1,0:T(8,128)(2,1)}, u32[]{:S(2)}) %copy-start) | copy-done | bytes 786456
  8.3 0.7 copy-done.5
  9.1 0.9 shard_map.103
  9.9 0.0 all-gather.3.cloned.1.call-update
  10.0 3.0 %collective-permute-start = (bf16[4,2,4,32,128]{4,3,2,1,0:T(8,128)(2,1)S(1)}, bf16[4,2,4,32,128]{4,3,2,1,0:T(8,128)(2,1)S(1)}, u32[]{:S(2)}, u32[]{:S(2)}) collective-permute-start(bf16[4,2,4,32,128]{4,3,2,1,0:T(8,128)(2,1)S(1)} %shard_map.103), channel_id=1, source_target_pairs={{0,4},{4,0},{8,12},{12,8},{16,20},{20,16},{24,28},{28,24},{1,5},{5... | collective-permute-start | bytes 786440 | tf_op jit(solution)/shard_map/ppermute | solution.py:492
  13.0 1.1 %copy-done.1 = bf16[2,48,32,128]{3,2,1,0:T(8,128)(2,1)S(1)} copy-done((bf16[2,48,32,128]{3,2,1,0:T(8,128)(2,1)S(1)}, bf16[2,48,32,128]{3,2,1,0:T(8,128)(2,1)}, u32[]{:S(2)}) %copy-start.1) | copy-done | bytes 786456
  14.1 0.7 copy-done.6
  14.9 0.9 shard_map.104.refs_4_
  15.7 0.1 collective-permute-start.2
  15.8 0.7 copy.13
  16.5 0.0 copy-start.2
  16.6 1.1 %copy-done.2 = bf16[2,48,32,128]{3,2,1,0:T(8,128)(2,1)S(1)} copy-done((bf16[2,48,32,128]{3,2,1,0:T(8,128)(2,1)S(1)}, bf16[2,48,32,128]{3,2,1,0:T(8,128)(2,1)}, u32[]{:S(2)}) %copy-start.2) | copy-done | bytes 786456
  17.7 1.1 %copy-done.4 = bf16[1296,256]{1,0:T(8,128)(2,1)S(1)} copy-done((bf16[1296,256]{1,0:T(8,128)(2,1)S(1)}, bf16[1296,256]{1,0:T(8,128)(2,1)}, u32[]{:S(2)}) %copy-start.4) | copy-done | bytes 663576
  18.8 0.9 copy-done.9
  19.7 0.7 copy-done.12
  20.4 0.4 shard_map.105
  20.7 0.0 collective-permute-done.received
  20.8 0.0 copy-start.7
  20.8 0.7 copy-done.7
  21.5 1.2 %shard_map.106 = (bf16[2,2,4,32,128]{4,3,2,1,0:T(8,128)(2,1)S(1)}, bf16[2,2,4,32,128]{4,3,2,1,0:T(8,128)(2,1)S(1)}) custom-call(s32[2,2,1024]{2,1,0:T(2,128)S(1)} %bitcast.17, s32[2,2,1024]{2,1,0:T(2,128)S(1)} %copy-done.7, bf16[2,48,32,128]{3,2,1,0:T(8,128)(2,1)S(1)} %get-tuple-element.31.mine, bf16[4,2,4,32,128]{4,3,2,1,0:T(8,128)(2,1)S(1)} %collective-permute-done.received), custom_call_target="tpu_custom_call" | custom-call | tf_op jit(solution)/shard_map/pallas_call | solution.py:509
  22.7 2.2 %collective-permute-start.1 = (bf16[2,2,4,32,128]{4,3,2,1,0:T(8,128)(2,1)S(1)}, bf16[2,2,4,32,128]{4,3,2,1,0:T(8,128)(2,1)S(1)}, u32[]{:S(2)}, u32[]{:S(2)}) collective-permute-start(bf16[2,2,4,32,128]{4,3,2,1,0:T(8,128)(2,1)S(1)} %get-tuple-element.35), channel_id=1, source_target_pairs={{0,8},{4,12},{8,0},{12,4},{16,24},{20,28},{24,16},{28,20},{1,9},{5... | collective-permute-start | bytes 393224 | tf_op jit(solution)/shard_map/ppermute | solution.py:492
  24.8 6.6 %collective-permute-done.1.received = bf16[2,2,4,32,128]{4,3,2,1,0:T(8,128)(2,1)S(1)} collective-permute-done((bf16[2,2,4,32,128]{4,3,2,1,0:T(8,128)(2,1)S(1)}, bf16[2,2,4,32,128]{4,3,2,1,0:T(8,128)(2,1)S(1)}, u32[]{:S(2)}, u32[]{:S(2)}) %collective-permute-start.1) | collective-permute-done | bytes 131104 | tf_op jit(solution)/shard_map/ppermute | solution.py:492
  31.5 1.1 %shard_map.107 = (bf16[1,2,4,32,128]{4,3,2,1,0:T(8,128)(2,1)S(1)}, bf16[1,2,4,32,128]{4,3,2,1,0:T(8,128)(2,1)S(1)}, f32[8,128]{1,0:T(8,128)S(1)}) custom-call(s32[2,2,1024]{2,1,0:T(2,128)S(1)} %bitcast.18, s32[2,2,1024]{2,1,0:T(2,128)S(1)} %copy-done.7, bf16[2,2,4,32,128]{4,3,2,1,0:T(8,128)(2,1)S(1)} %get-tuple-element.34.mine, ...), custom_call_target="tpu_custom_call" | custom-call | tf_op jit(solution)/shard_map/pallas_call | solution.py:509
  32.6 3.0 %collective-permute-start.3 = (bf16[1,2,4,32,128]{4,3,2,1,0:T(8,128)(2,1)S(1)}, bf16[1,2,4,32,128]{4,3,2,1,0:T(8,128)(2,1)S(1)}, u32[]{:S(2)}, u32[]{:S(2)}) collective-permute-start(bf16[1,2,4,32,128]{4,3,2,1,0:T(8,128)(2,1)S(1)} %get-tuple-element.37), channel_id=1, source_target_pairs={{0,16},{4,20},{8,24},{12,28},{16,0},{20,4},{24,8},{28,12},{1,17},{... | collective-permute-start | bytes 196616 | tf_op jit(solution)/shard_map/ppermute | solution.py:492
  35.6 0.0 collective-permute-start.4
  35.6 1.5 %collective-permute-start.5 = (f32[8,128]{1,0:T(8,128)S(1)}, f32[8,128]{1,0:T(8,128)S(1)}, u32[]{:S(2)}, u32[]{:S(2)}) collective-permute-start(f32[8,128]{1,0:T(8,128)S(1)} %bitcast.25), channel_id=1, source_target_pairs={{0,2},{1,3},{2,0},{3,1},{4,6},{5,7},{6,4},{7,5},{8,10},{9,11},{10,... | collective-permute-start | bytes 12296 | tf_op jit(solution)/shard_map/ppermute | solution.py:526
  37.1 0.4 collective-permute-start.6
  37.5 0.0 collective-permute-done.2.received
  37.5 1.2 %shard_map.108 = (bf16[2,2,4,32,128]{4,3,2,1,0:T(8,128)(2,1)S(1)}, bf16[2,2,4,32,128]{4,3,2,1,0:T(8,128)(2,1)S(1)}) custom-call(s32[2,2,1024]{2,1,0:T(2,128)S(1)} %bitcast.19, s32[2,2,1024]{2,1,0:T(2,128)S(1)} %copy-done.7, bf16[2,48,32,128]{3,2,1,0:T(8,128)(2,1)S(1)} %get-tuple-element.31.mine, bf16[4,2,4,32,128]{4,3,2,1,0:T(8,128)(2,1)S(1)} %collective-permute-done.2.received), custom_call_target="tpu_custom_call" | custom-call | tf_op jit(solution)/shard_map/pallas_call | solution.py:509
  38.7 1.6 %collective-permute-start.7 = (bf16[2,2,4,32,128]{4,3,2,1,0:T(8,128)(2,1)S(1)}, bf16[2,2,4,32,128]{4,3,2,1,0:T(8,128)(2,1)S(1)}, u32[]{:S(2)}, u32[]{:S(2)}) collective-permute-start(bf16[2,2,4,32,128]{4,3,2,1,0:T(8,128)(2,1)S(1)} %get-tuple-element.39), channel_id=1, source_target_pairs={{0,8},{4,12},{8,0},{12,4},{16,24},{20,28},{24,16},{28,20},{1,9},{5... | collective-permute-start | bytes 393224 | tf_op jit(solution)/shard_map/ppermute | solution.py:492
  40.3 0.0 collective-permute-done.4.refs_1_
  40.3 0.0 collective-permute-done.5.refs_2_
  40.3 0.0 collective-permute-done.6.refs_3_
  40.3 0.0 collective-permute-done.3.received
  40.4 1.7 %shard_map.109 = (f32[32,4,128]{2,1,0:T(4,128)}, f32[4,128]{1,0:T(4,128)S(1)}, f32[32,128]{1,0:T(8,128)S(1)}) custom-call(bf16[1,2,4,32,128]{4,3,2,1,0:T(8,128)(2,1)S(1)} %get-tuple-element.40.kept, bf16[1,2,4,32,128]{4,3,2,1,0:T(8,128)(2,1)S(1)} %collective-permute-done.3.received, f32[8,128]{1,0:T(8,128)S(1)} %get-tuple-element.41.flags, ...), custom_call_target="tpu_custom_call" | custom-call | bytes 11070000 | tf_op jit(solution)/shard_map/pallas_call | solution.py:565
  42.0 5.9 %all-to-all-start = ((f32[32,4,128]{2,1,0:T(4,128)}), f32[32,4,128]{2,1,0:T(4,128)S(1)}, u32[]{:S(2)}, u32[]{:S(2)}) async-start(f32[32,4,128]{2,1,0:T(4,128)} %get-tuple-element.50), calls=%async_computation | async-start | bytes 131072 | tf_op jit(solution)/shard_map/all_to_all | solution.py:471
  48.0 0.0 collective-permute-done.7.received
  48.0 0.0 copy-done.8
  48.0 1.1 %shard_map.110 = (bf16[1,2,4,32,128]{4,3,2,1,0:T(8,128)(2,1)S(1)}, bf16[1,2,4,32,128]{4,3,2,1,0:T(8,128)(2,1)S(1)}, f32[8,128]{1,0:T(8,128)S(1)}) custom-call(s32[2,2,1024]{2,1,0:T(2,128)S(1)} %bitcast.20, s32[2,2,1024]{2,1,0:T(2,128)S(1)} %copy-done.8, bf16[2,2,4,32,128]{4,3,2,1,0:T(8,128)(2,1)S(1)} %get-tuple-element.45.mine, ...), custom_call_target="tpu_custom_call" | custom-call | tf_op jit(solution)/shard_map/pallas_call | solution.py:509
  49.1 7.1 %all-to-all-done = f32[32,4,128]{2,1,0:T(4,128)S(1)} async-done(((f32[32,4,128]{2,1,0:T(4,128)}), f32[32,4,128]{2,1,0:T(4,128)S(1)}, u32[]{:S(2)}, u32[]{:S(2)}) %all-to-all-start) | async-done | bytes 65568 | tf_op jit(solution)/shard_map/all_to_all | solution.py:471
  56.3 0.0 copy-done.3
  56.3 1.6 %shard_map.111 = f32[32,8,128]{2,1,0:T(8,128)} custom-call(s32[2,8]{1,0:T(2,128)S(1)} %bitcast.27, f32[8,4,4,128]{3,2,1,0:T(4,128)S(1)} %bitcast.22, bf16[8,2,128,128]{3,2,1,0:T(8,128)(2,1)S(1)} %copy-done.3), custom_call_target="tpu_custom_call" | custom-call | bytes 7380000 | tf_op jit(solution)/shard_map/pallas_call | solution.py:475
  57.9 2.6 %all-to-all-start.1 = ((f32[32,8,128]{2,1,0:T(8,128)}), f32[32,8,128]{2,1,0:T(8,128)S(1)}, u32[]{:S(2)}, u32[]{:S(2)}) async-start(f32[32,8,128]{2,1,0:T(8,128)} %shard_map.111), calls=%async_computation.1 | async-start | bytes 262144 | tf_op jit(solution)/shard_map/all_to_all | solution.py:576
  60.5 0.8 constant_dynamic-slice_fusion
  61.2 2.7 %collective-permute-start.8 = (bf16[1,2,4,32,128]{4,3,2,1,0:T(8,128)(2,1)S(1)}, bf16[1,2,4,32,128]{4,3,2,1,0:T(8,128)(2,1)S(1)}, u32[]{:S(2)}, u32[]{:S(2)}) collective-permute-start(bf16[1,2,4,32,128]{4,3,2,1,0:T(8,128)(2,1)S(1)} %get-tuple-element.47), channel_id=1, source_target_pairs={{0,16},{4,20},{8,24},{12,28},{16,0},{20,4},{24,8},{28,12},{1,17},{... | collective-permute-start | bytes 196616 | tf_op jit(solution)/shard_map/ppermute | solution.py:492
  63.9 0.1 dynamic-slice_add_fusion
  63.9 0.7 reshape.31.places
  64.6 8.0 %collective-permute-done.8.received = bf16[1,2,4,32,128]{4,3,2,1,0:T(8,128)(2,1)S(1)} collective-permute-done((bf16[1,2,4,32,128]{4,3,2,1,0:T(8,128)(2,1)S(1)}, bf16[1,2,4,32,128]{4,3,2,1,0:T(8,128)(2,1)S(1)}, u32[]{:S(2)}, u32[]{:S(2)}) %collective-permute-start.8) | collective-permute-done | bytes 65568 | tf_op jit(solution)/shard_map/ppermute | solution.py:492
  72.6 0.0 all-to-all-done.1
  72.6 1.7 %shard_map.112 = (f32[32,4,128]{2,1,0:T(4,128)}, f32[4,128]{1,0:T(4,128)S(1)}, f32[32,128]{1,0:T(8,128)S(1)}, f32[8,128]{1,0:T(8,128)S(1)}) custom-call(bf16[1,2,4,32,128]{4,3,2,1,0:T(8,128)(2,1)S(1)} %get-tuple-element.46.kept, bf16[1,2,4,32,128]{4,3,2,1,0:T(8,128)(2,1)S(1)} %collective-permute-done.8.received, f32[8,128]{1,0:T(8,128)S(1)} %get-tuple-element.48.flags, ...), custom_call_target="tpu_custom_call" | custom-call | bytes 11070000 | tf_op jit(solution)/shard_map/pallas_call | solution.py:579
  74.3 0.6 copy-done.11
  74.9 3.8 %all-to-all-start.2 = ((f32[32,4,128]{2,1,0:T(4,128)}), f32[32,4,128]{2,1,0:T(4,128)S(1)}, u32[]{:S(2)}, u32[]{:S(2)}) async-start(f32[32,4,128]{2,1,0:T(4,128)} %get-tuple-element.55), calls=%async_computation.2 | async-start | bytes 131072 | tf_op jit(solution)/shard_map/all_to_all | solution.py:471
  78.7 0.1 dynamic-slice_bitcast_fusion.1
  78.8 0.1 dynamic-slice_bitcast_fusion
  78.9 8.1 %all-to-all-done.2 = f32[32,4,128]{2,1,0:T(4,128)S(1)} async-done(((f32[32,4,128]{2,1,0:T(4,128)}), f32[32,4,128]{2,1,0:T(4,128)S(1)}, u32[]{:S(2)}, u32[]{:S(2)}) %all-to-all-start.2) | async-done | bytes 65568 | tf_op jit(solution)/shard_map/all_to_all | solution.py:471
  87.0 1.5 %shard_map.114 = f32[8,8,128]{2,1,0:T(8,128)} custom-call(s32[2,8]{1,0:T(2,128)S(1)} %bitcast.28, f32[8,4,4,128]{3,2,1,0:T(4,128)S(1)} %bitcast.21, bf16[8,2,128,128]{3,2,1,0:T(8,128)(2,1)S(1)} %copy-done.3), custom_call_target="tpu_custom_call" | custom-call | bytes 7380000 | tf_op jit(solution)/shard_map/pallas_call | solution.py:475
  88.6 3.3 %all-to-all-start.3 = ((f32[8,8,128]{2,1,0:T(8,128)}), f32[8,8,128]{2,1,0:T(8,128)S(1)}, u32[]{:S(2)}, u32[]{:S(2)}) async-start(f32[8,8,128]{2,1,0:T(8,128)} %shard_map.114), calls=%async_computation.3 | async-start | bytes 65536 | tf_op jit(solution)/shard_map/all_to_all | solution.py:589
  91.9 0.6 pad_maximum_fusion
  92.5 0.5 all-gather.3.cloned.1.call-done
  93.0 6.6 %shard_map.113 = bf16[2,124,32,128]{3,2,1,0:T(8,128)(2,1)} custom-call(s32[496]{0:T(512)} %reshape.31.places, f32[32,128]{1,0:T(8,128)} %copy-done.10, f32[32,128]{1,0:T(8,128)} %copy-done.11, f32[144,128]{1,0:T(8,128)} %constant.63.clone.refs_0_.mirror, bf16[768,32,128]{2,1,0:T(8,128)(2,1)} %bitcast.29), custom_call_target="tpu_custom_call" | custom-call | flops 8126464 | bytes 8323072 | tf_op jit(solution)/shard_map/pallas_call | solution.py:590
  99.6 0.0 all-to-all-done.3
  99.6 0.6 add_bitcast_fusion
  (14 shorter events, 0.0 us)
Async XLA Ops:
  7.2 85.8 %all-gather.3.cloned.1.call-start = ((), (), s32[]{:S(2)}) async-start(), calls=%async_computation.4 | async-start | bytes 7077888 | tf_op jit(solution)/shard_map/all_gather | solution.py:554
  7.2 1.1 %copy-start = (bf16[2,48,32,128]{3,2,1,0:T(8,128)(2,1)S(1)}, bf16[2,48,32,128]{3,2,1,0:T(8,128)(2,1)}, u32[]{:S(2)}) copy-start(bf16[2,48,32,128]{3,2,1,0:T(8,128)(2,1)} %refs_3_.1) | copy-start | bytes 2359300
  8.3 0.7 copy-start.5
  9.1 38.9 %copy-start.8 = (s32[2,2,1024]{2,1,0:T(2,128)S(1)}, s32[2,2,1024]{2,1,0:T(2,128)}, u32[]{:S(2)}) copy-start(s32[2,2,1024]{2,1,0:T(2,128)} %slots.11) | copy-start | bytes 49156
  9.1 47.2 %copy-start.3 = (bf16[8,2,128,128]{3,2,1,0:T(8,128)(2,1)S(1)}, bf16[8,2,128,128]{3,2,1,0:T(8,128)(2,1)}, u32[]{:S(2)}) copy-start(bf16[8,2,128,128]{3,2,1,0:T(8,128)(2,1)} %blocks.3) | copy-start | bytes 1572868
  9.1 47.2 %copy-start.13 = (s32[8,2]{0,1:T(2,128)S(1)}, s32[8,2]{0,1:T(2,128)}, u32[]{:S(2)}) copy-start(s32[8,2]{0,1:T(2,128)} %param.13) | copy-start | bytes 196
  10.0 10.8 %collective-permute-start = (bf16[4,2,4,32,128]{4,3,2,1,0:T(8,128)(2,1)S(1)}, bf16[4,2,4,32,128]{4,3,2,1,0:T(8,128)(2,1)S(1)}, u32[]{:S(2)}, u32[]{:S(2)}) collective-permute-start(bf16[4,2,4,32,128]{4,3,2,1,0:T(8,128)(2,1)S(1)} %shard_map.103), channel_id=1, source_target_pairs={{0,4},{4,0},{8,12},{12,8},{16,20},{20,16},{24,28},{28,24},{1,5},{5... | collective-permute-start | bytes 786440 | tf_op jit(solution)/shard_map/ppermute | solution.py:492
  13.0 1.1 %copy-start.1 = (bf16[2,48,32,128]{3,2,1,0:T(8,128)(2,1)S(1)}, bf16[2,48,32,128]{3,2,1,0:T(8,128)(2,1)}, u32[]{:S(2)}) copy-start(bf16[2,48,32,128]{3,2,1,0:T(8,128)(2,1)} %refs_3_.1) | copy-start | bytes 2359300
  14.1 0.7 copy-start.6
  15.7 21.8 %collective-permute-start.2 = (bf16[4,2,4,32,128]{4,3,2,1,0:T(8,128)(2,1)S(1)}, bf16[4,2,4,32,128]{4,3,2,1,0:T(8,128)(2,1)S(1)}, u32[]{:S(2)}, u32[]{:S(2)}) collective-permute-start(bf16[4,2,4,32,128]{4,3,2,1,0:T(8,128)(2,1)S(1)} %shard_map.104.refs_4_), channel_id=1, source_target_pairs={{0,4},{4,0},{8,12},{12,8},{16,20},{20,16},{24,28},{28,24},{1,5},{5... | collective-permute-start | bytes 786440 | tf_op jit(solution)/shard_map/ppermute | solution.py:492
  16.5 1.1 %copy-start.2 = (bf16[2,48,32,128]{3,2,1,0:T(8,128)(2,1)S(1)}, bf16[2,48,32,128]{3,2,1,0:T(8,128)(2,1)}, u32[]{:S(2)}) copy-start(bf16[2,48,32,128]{3,2,1,0:T(8,128)(2,1)} %refs_3_.1) | copy-start | bytes 2359300
  17.7 1.1 %copy-start.4 = (bf16[1296,256]{1,0:T(8,128)(2,1)S(1)}, bf16[1296,256]{1,0:T(8,128)(2,1)}, u32[]{:S(2)}) copy-start(bf16[1296,256]{1,0:T(8,128)(2,1)} %constant.62.clone.refs_1_) | copy-start | bytes 1990660
  18.8 0.9 copy-start.9
  19.7 0.7 copy-start.12
  20.8 0.7 copy-start.7
  22.7 8.8 %collective-permute-start.1 = (bf16[2,2,4,32,128]{4,3,2,1,0:T(8,128)(2,1)S(1)}, bf16[2,2,4,32,128]{4,3,2,1,0:T(8,128)(2,1)S(1)}, u32[]{:S(2)}, u32[]{:S(2)}) collective-permute-start(bf16[2,2,4,32,128]{4,3,2,1,0:T(8,128)(2,1)S(1)} %get-tuple-element.35), channel_id=1, source_target_pairs={{0,8},{4,12},{8,0},{12,4},{16,24},{20,28},{24,16},{28,20},{1,9},{5... | collective-permute-start | bytes 393224 | tf_op jit(solution)/shard_map/ppermute | solution.py:492
  32.6 7.7 %collective-permute-start.3 = (bf16[1,2,4,32,128]{4,3,2,1,0:T(8,128)(2,1)S(1)}, bf16[1,2,4,32,128]{4,3,2,1,0:T(8,128)(2,1)S(1)}, u32[]{:S(2)}, u32[]{:S(2)}) collective-permute-start(bf16[1,2,4,32,128]{4,3,2,1,0:T(8,128)(2,1)S(1)} %get-tuple-element.37), channel_id=1, source_target_pairs={{0,16},{4,20},{8,24},{12,28},{16,0},{20,4},{24,8},{28,12},{1,17},{... | collective-permute-start | bytes 196616 | tf_op jit(solution)/shard_map/ppermute | solution.py:492
  35.6 4.7 %collective-permute-start.4 = (f32[8,128]{1,0:T(8,128)S(1)}, f32[8,128]{1,0:T(8,128)S(1)}, u32[]{:S(2)}, u32[]{:S(2)}) collective-permute-start(f32[8,128]{1,0:T(8,128)S(1)} %bitcast.24), channel_id=1, source_target_pairs={{0,1},{1,0},{2,3},{3,2},{4,5},{5,4},{6,7},{7,6},{8,9},{9,8},{10,11... | collective-permute-start | bytes 12296 | tf_op jit(solution)/shard_map/ppermute | solution.py:526
  35.6 4.7 %collective-permute-start.5 = (f32[8,128]{1,0:T(8,128)S(1)}, f32[8,128]{1,0:T(8,128)S(1)}, u32[]{:S(2)}, u32[]{:S(2)}) collective-permute-start(f32[8,128]{1,0:T(8,128)S(1)} %bitcast.25), channel_id=1, source_target_pairs={{0,2},{1,3},{2,0},{3,1},{4,6},{5,7},{6,4},{7,5},{8,10},{9,11},{10,... | collective-permute-start | bytes 12296 | tf_op jit(solution)/shard_map/ppermute | solution.py:526
  37.1 3.2 %collective-permute-start.6 = (f32[8,128]{1,0:T(8,128)S(1)}, f32[8,128]{1,0:T(8,128)S(1)}, u32[]{:S(2)}, u32[]{:S(2)}) collective-permute-start(f32[8,128]{1,0:T(8,128)S(1)} %bitcast.26), channel_id=1, source_target_pairs={{0,3},{1,2},{2,1},{3,0},{4,7},{5,6},{6,5},{7,4},{8,11},{9,10},{10,... | collective-permute-start | bytes 12296 | tf_op jit(solution)/shard_map/ppermute | solution.py:526
  38.7 9.3 %collective-permute-start.7 = (bf16[2,2,4,32,128]{4,3,2,1,0:T(8,128)(2,1)S(1)}, bf16[2,2,4,32,128]{4,3,2,1,0:T(8,128)(2,1)S(1)}, u32[]{:S(2)}, u32[]{:S(2)}) collective-permute-start(bf16[2,2,4,32,128]{4,3,2,1,0:T(8,128)(2,1)S(1)} %get-tuple-element.39), channel_id=1, source_target_pairs={{0,8},{4,12},{8,0},{12,4},{16,24},{20,28},{24,16},{28,20},{1,9},{5... | collective-permute-start | bytes 393224 | tf_op jit(solution)/shard_map/ppermute | solution.py:492
  42.0 51.0 %copy-start.10 = (f32[32,128]{1,0:T(8,128)}, f32[32,128]{1,0:T(8,128)S(1)}, u32[]{:S(2)}) copy-start(f32[32,128]{1,0:T(8,128)S(1)} %get-tuple-element.49.c_base.c_first) | copy-start | bytes 49156
  42.0 14.2 %all-to-all-start = ((f32[32,4,128]{2,1,0:T(4,128)}), f32[32,4,128]{2,1,0:T(4,128)S(1)}, u32[]{:S(2)}, u32[]{:S(2)}) async-start(f32[32,4,128]{2,1,0:T(4,128)} %get-tuple-element.50), calls=%async_computation | async-start | bytes 131072 | tf_op jit(solution)/shard_map/all_to_all | solution.py:471
  57.9 14.8 %all-to-all-start.1 = ((f32[32,8,128]{2,1,0:T(8,128)}), f32[32,8,128]{2,1,0:T(8,128)S(1)}, u32[]{:S(2)}, u32[]{:S(2)}) async-start(f32[32,8,128]{2,1,0:T(8,128)} %shard_map.111), calls=%async_computation.1 | async-start | bytes 262144 | tf_op jit(solution)/shard_map/all_to_all | solution.py:576
  61.2 11.4 %collective-permute-start.8 = (bf16[1,2,4,32,128]{4,3,2,1,0:T(8,128)(2,1)S(1)}, bf16[1,2,4,32,128]{4,3,2,1,0:T(8,128)(2,1)S(1)}, u32[]{:S(2)}, u32[]{:S(2)}) collective-permute-start(bf16[1,2,4,32,128]{4,3,2,1,0:T(8,128)(2,1)S(1)} %get-tuple-element.47), channel_id=1, source_target_pairs={{0,16},{4,20},{8,24},{12,28},{16,0},{20,4},{24,8},{28,12},{1,17},{... | collective-permute-start | bytes 196616 | tf_op jit(solution)/shard_map/ppermute | solution.py:492
  74.3 0.6 copy-start.11
  74.9 12.1 %all-to-all-start.2 = ((f32[32,4,128]{2,1,0:T(4,128)}), f32[32,4,128]{2,1,0:T(4,128)S(1)}, u32[]{:S(2)}, u32[]{:S(2)}) async-start(f32[32,4,128]{2,1,0:T(4,128)} %get-tuple-element.55), calls=%async_computation.2 | async-start | bytes 131072 | tf_op jit(solution)/shard_map/all_to_all | solution.py:471
  88.6 11.0 %all-to-all-start.3 = ((f32[8,8,128]{2,1,0:T(8,128)}), f32[8,8,128]{2,1,0:T(8,128)S(1)}, u32[]{:S(2)}, u32[]{:S(2)}) async-start(f32[8,8,128]{2,1,0:T(8,128)} %shard_map.114), calls=%async_computation.3 | async-start | bytes 65536 | tf_op jit(solution)/shard_map/all_to_all | solution.py:589
Sparse Core Ops, SparseCore 0:
  10.1 82.8 all-gather.2

commit v5 on v4

--- a/solution.py
+++ b/solution.py
@@ -345,7 +345,8 @@
     own = ratio[:LG_DEV]
     for a in range(1, sub_rows):
         own = own + ratio[a * LG_DEV : (a + 1) * LG_DEV]
-    slopes[...] = own
+    width = slopes.shape[-1]
+    slopes[...] = functools.reduce(jnp.add, [own[:, at : at + width] for at in range(0, LANES, width)])
     payload[...] = jnp.broadcast_to(own.astype(jnp.bfloat16).astype(jnp.float32)[None], payload.shape)
 
 
@@ -366,14 +367,15 @@
     slopes_from(tiles, prof, table, payload, slopes)
 
 
-def second_slopes(kept, received, flags, c_base, updates, mirror, table, payload, slopes, c_out, c_own, prof):
+def second_slopes(kept, received, flags, c_base, updates, earlier, mirror, table, payload, slopes, c_out, c_own, prof):
     my_tile = lax.axis_index("tile")
     c_out[...] = c_base[...] + loop_gain * jnp.sum(updates[...], axis=0).reshape(c_base.shape)
     c_own[...] = c_out[pl.ds(lax.axis_index("rec") * c_own.shape[0], c_own.shape[0]), :]
     base, need = own_rows(my_tile)
     prof[...] = column_profiles(c_out[pl.ds(base, need), :], mirror)
     tiles = last_merge(kept, received, flags)
-    slopes_from(tiles, prof, table, payload, slopes)
+    slopes[0] = earlier[...]
+    slopes_from(tiles, prof, table, payload, slopes.at[1])
 
 
 def update_kernel(pattern, received, blocks, out, slopes):
@@ -462,9 +464,10 @@
 
     owners = tile_owner[..., 0]
     tables_in = [table["mirror"], table["exact"]]
+    width = slab_rows // SUBPX * SUB * 2
     payload_out = [
         jax.ShapeDtypeStruct((everyone, LG_DEV, LANES), f32),
-        jax.ShapeDtypeStruct((LG_DEV, LANES), f32),
+        jax.ShapeDtypeStruct((LG_DEV, width), f32),
     ]
 
     def exchange(payload):
@@ -515,10 +518,6 @@
 
     def later(value, after):
         return lax.optimization_barrier((value, after))[0]
-
-    def own_lanes(slopes):
-        width = slab_rows // SUBPX * SUB * 2
-        return lax.dynamic_slice_in_dim(slopes, my_rec * width, width, 1)
 
     last = n.bit_length() - 1
     c_own = commands_init.reshape(-1, LANES)
@@ -571,20 +570,19 @@
         compiler_params=limit,
         cost_estimate=microseconds(3),
     )(*guide[0], *tables_in, *c_parts)
-    slopes_first = own_lanes(slopes_first)
     updates = updates_of(later(exchange(payload), send), everyone)
     updates = lax.all_to_all(updates, ("tile", "rec"), split_axis=0, concat_axis=0, tiled=True)
     updates = updates.reshape(n, rec_count, block_rows, LANES)
 
-    payload, slopes_second, c1, mine = pl.pallas_call(
+    payload, slopes, c1, mine = pl.pallas_call(
         second_slopes,
-        out_shape=payload_out + [jax.ShapeDtypeStruct(r, f32) for r in (c0.shape, c_own.shape)],
-        in_specs=[vmem()] * (5 + len(tables_in)),
+        out_shape=payload_out[:1] + [jax.ShapeDtypeStruct(r, f32) for r in ((frames, LG_DEV, width), c0.shape, c_own.shape)],
+        in_specs=[vmem()] * (6 + len(tables_in)),
         out_specs=[vmem()] * 4,
         scratch_shapes=[pltpu.VMEM((LG_DEV * SUB, LANES), f32)],
         compiler_params=limit,
         cost_estimate=microseconds(3),
-    )(*guide[1], c0, updates, *tables_in)
+    )(*guide[1], c0, updates, slopes_first, *tables_in)
     updates = updates_of(exchange(payload), n)
     updates = lax.all_to_all(updates, "tile", split_axis=0, concat_axis=0, tiled=True)
     science = pl.pallas_call(
@@ -607,7 +605,7 @@
     )(places, c0, c1, table["mirror"], gathered)
     updates = later(updates, science)
     c2 = mine + loop_gain * jnp.sum(updates, axis=0)
-    return jnp.stack([slopes_first, own_lanes(slopes_second)], axis=0), science, c2.reshape(-1)
+    return slopes, science, c2.reshape(-1)
 
 
 def per_device(screens, tile_owner, *rest):

time: 108 us -> 108 us (level)
    ppermute x6, waiting for transfers between devices: 14.7 us -> 16.1 us  [swap(): return lax.ppermute(x, 'tile', [(t, t ^ bit) for t in range(n)])]
  transfers between devices with their start and end apart: 14 -> 14, of which waited for: 5 -> 5; matrix products, arithmetic and copies ran while one was open for 3% -> 2% of each run, Pallas kernels for 18% -> 18%
where the time goes in v5:
time: 108 us; the launch traced here: 107 us
  waiting for transfers between devices  31.1 us (29%)
  starting transfers between devices  30.2 us (28%)
  Pallas kernels  19.9 us (18%)
  between operations  14.2 us (13%)
  local copies, waits for them, and re-layouts  11 us (10%)
    ppermute x6, waiting for transfers between devices, swap(): return lax.ppermute(x, 'tile', [(t, t ^ bit) for t in range(n)])  16.1 us
    all_to_all x2, waiting for transfers between devices, exchange(): lax.all_to_all(payload, ('tile', 'rec'), split_axis=0, concat_axis=0, til...  14.6 us
    ppermute x6, starting transfers between devices, swap(): return lax.ppermute(x, 'tile', [(t, t ^ bit) for t in range(n)])  12.7 us
    all_to_all x2, starting transfers between devices, exchange(): lax.all_to_all(payload, ('tile', 'rec'), split_axis=0, concat_axis=0, til...  9.75 us
    unnamed x29, local copies, waits for them, and re-layouts  9.54 us
    pallas_call x1, Pallas kernels, by_ring(): pl.pallas_call(science_kernel, out_shape=jax.ShapeDtypeStruct((frames, SC...  6.59 us
    pallas_call x4, Pallas kernels, merge(): pl.pallas_call(functools.partial(merge_kernel, frame, bits), in_specs=[sm...  4.65 us
    all_to_all x1, starting transfers between devices, by_ring(): lax.all_to_all(updates, 'tile', split_axis=0, concat_axis=0, tiled=True)  3.33 us
  transfers between devices with their start and end apart: 14, of which 5 were waited for; matrix products, arithmetic and copies ran while one was open for 2% of the time, Pallas kernels for 18%

profile of v5, /device:TPU:0, one launch (start us, length us, event | category | flops | bytes accessed | tf_op | source)
XLA Modules:
  0.0 107.1 jit_solution(4404806702900302791)
XLA Ops:
  7.2 0.0 all-gather.3.cloned.1.call-start
  7.2 0.0 copy-start
  7.2 1.1 %copy-done = bf16[2,48,32,128]{3,2,1,0:T(8,128)(2,1)S(1)} copy-done((bf16[2,48,32,128]{3,2,1,0:T(8,128)(2,1)S(1)}, bf16[2,48,32,128]{3,2,1,0:T(8,128)(2,1)}, u32[]{:S(2)}) %copy-start) | copy-done | bytes 786456
  8.3 0.0 copy-start.5
  8.3 0.7 copy-done.5
  9.1 0.9 shard_map.103
  9.9 0.0 all-gather.3.cloned.1.call-update
  10.0 3.0 %collective-permute-start.1 = (bf16[4,2,4,32,128]{4,3,2,1,0:T(8,128)(2,1)S(1)}, bf16[4,2,4,32,128]{4,3,2,1,0:T(8,128)(2,1)S(1)}, u32[]{:S(2)}, u32[]{:S(2)}) collective-permute-start(bf16[4,2,4,32,128]{4,3,2,1,0:T(8,128)(2,1)S(1)} %shard_map.103), channel_id=1, source_target_pairs={{0,4},{4,0},{8,12},{12,8},{16,20},{20,16},{24,28},{28,24},{1,5},{5... | collective-permute-start | bytes 786440 | tf_op jit(solution)/shard_map/ppermute | solution.py:495
  13.0 1.1 %copy-done.1 = bf16[2,48,32,128]{3,2,1,0:T(8,128)(2,1)S(1)} copy-done((bf16[2,48,32,128]{3,2,1,0:T(8,128)(2,1)S(1)}, bf16[2,48,32,128]{3,2,1,0:T(8,128)(2,1)}, u32[]{:S(2)}) %copy-start.1) | copy-done | bytes 786456
  14.1 0.7 copy-done.6
  14.9 0.9 shard_map.104.refs_4_
  15.7 0.1 collective-permute-start
  15.8 0.7 copy.13
  16.5 0.0 copy-start.2
  16.6 1.1 %copy-done.2 = bf16[2,48,32,128]{3,2,1,0:T(8,128)(2,1)S(1)} copy-done((bf16[2,48,32,128]{3,2,1,0:T(8,128)(2,1)S(1)}, bf16[2,48,32,128]{3,2,1,0:T(8,128)(2,1)}, u32[]{:S(2)}) %copy-start.2) | copy-done | bytes 786456
  17.7 1.1 %copy-done.4 = bf16[1296,256]{1,0:T(8,128)(2,1)S(1)} copy-done((bf16[1296,256]{1,0:T(8,128)(2,1)S(1)}, bf16[1296,256]{1,0:T(8,128)(2,1)}, u32[]{:S(2)}) %copy-start.4) | copy-done | bytes 663576
  18.8 0.9 copy-done.9
  19.7 0.7 copy-done.12
  20.4 0.4 shard_map.105
  20.7 0.0 collective-permute-done.1.received
  20.8 0.0 copy-start.7
  20.8 0.7 copy-done.7
  21.5 1.2 %shard_map.106 = (bf16[2,2,4,32,128]{4,3,2,1,0:T(8,128)(2,1)S(1)}, bf16[2,2,4,32,128]{4,3,2,1,0:T(8,128)(2,1)S(1)}) custom-call(s32[2,2,1024]{2,1,0:T(2,128)S(1)} %bitcast.13, s32[2,2,1024]{2,1,0:T(2,128)S(1)} %copy-done.7, bf16[2,48,32,128]{3,2,1,0:T(8,128)(2,1)S(1)} %get-tuple-element.31.mine, bf16[4,2,4,32,128]{4,3,2,1,0:T(8,128)(2,1)S(1)} %collective-permute-done.1.received), custom_call_target="tpu_custom_call" | custom-call | tf_op jit(solution)/shard_map/pallas_call | solution.py:512
  22.7 2.2 %collective-permute-start.2 = (bf16[2,2,4,32,128]{4,3,2,1,0:T(8,128)(2,1)S(1)}, bf16[2,2,4,32,128]{4,3,2,1,0:T(8,128)(2,1)S(1)}, u32[]{:S(2)}, u32[]{:S(2)}) collective-permute-start(bf16[2,2,4,32,128]{4,3,2,1,0:T(8,128)(2,1)S(1)} %get-tuple-element.35), channel_id=1, source_target_pairs={{0,8},{4,12},{8,0},{12,4},{16,24},{20,28},{24,16},{28,20},{1,9},{5... | collective-permute-start | bytes 393224 | tf_op jit(solution)/shard_map/ppermute | solution.py:495
  24.8 6.6 %collective-permute-done.2.received = bf16[2,2,4,32,128]{4,3,2,1,0:T(8,128)(2,1)S(1)} collective-permute-done((bf16[2,2,4,32,128]{4,3,2,1,0:T(8,128)(2,1)S(1)}, bf16[2,2,4,32,128]{4,3,2,1,0:T(8,128)(2,1)S(1)}, u32[]{:S(2)}, u32[]{:S(2)}) %collective-permute-start.2) | collective-permute-done | bytes 131104 | tf_op jit(solution)/shard_map/ppermute | solution.py:495
  31.5 1.1 %shard_map.107 = (bf16[1,2,4,32,128]{4,3,2,1,0:T(8,128)(2,1)S(1)}, bf16[1,2,4,32,128]{4,3,2,1,0:T(8,128)(2,1)S(1)}, f32[8,128]{1,0:T(8,128)S(1)}) custom-call(s32[2,2,1024]{2,1,0:T(2,128)S(1)} %bitcast.14, s32[2,2,1024]{2,1,0:T(2,128)S(1)} %copy-done.7, bf16[2,2,4,32,128]{4,3,2,1,0:T(8,128)(2,1)S(1)} %get-tuple-element.34.mine, ...), custom_call_target="tpu_custom_call" | custom-call | tf_op jit(solution)/shard_map/pallas_call | solution.py:512
  32.6 3.0 %collective-permute-start.5 = (bf16[1,2,4,32,128]{4,3,2,1,0:T(8,128)(2,1)S(1)}, bf16[1,2,4,32,128]{4,3,2,1,0:T(8,128)(2,1)S(1)}, u32[]{:S(2)}, u32[]{:S(2)}) collective-permute-start(bf16[1,2,4,32,128]{4,3,2,1,0:T(8,128)(2,1)S(1)} %get-tuple-element.36), channel_id=1, source_target_pairs={{0,16},{4,20},{8,24},{12,28},{16,0},{20,4},{24,8},{28,12},{1,17},{... | collective-permute-start | bytes 196616 | tf_op jit(solution)/shard_map/ppermute | solution.py:495
  35.6 0.0 collective-permute-start.6
  35.6 1.5 %collective-permute-start.7 = (f32[8,128]{1,0:T(8,128)S(1)}, f32[8,128]{1,0:T(8,128)S(1)}, u32[]{:S(2)}, u32[]{:S(2)}) collective-permute-start(f32[8,128]{1,0:T(8,128)S(1)} %bitcast.21), channel_id=1, source_target_pairs={{0,2},{1,3},{2,0},{3,1},{4,6},{5,7},{6,4},{7,5},{8,10},{9,11},{10,... | collective-permute-start | bytes 12296 | tf_op jit(solution)/shard_map/ppermute | solution.py:525
  37.1 0.4 collective-permute-start.8
  37.5 0.0 collective-permute-done.received
  37.5 1.2 %shard_map.108 = (bf16[2,2,4,32,128]{4,3,2,1,0:T(8,128)(2,1)S(1)}, bf16[2,2,4,32,128]{4,3,2,1,0:T(8,128)(2,1)S(1)}) custom-call(s32[2,2,1024]{2,1,0:T(2,128)S(1)} %bitcast.15, s32[2,2,1024]{2,1,0:T(2,128)S(1)} %copy-done.7, bf16[2,48,32,128]{3,2,1,0:T(8,128)(2,1)S(1)} %get-tuple-element.31.mine, bf16[4,2,4,32,128]{4,3,2,1,0:T(8,128)(2,1)S(1)} %collective-permute-done.received), custom_call_target="tpu_custom_call" | custom-call | tf_op jit(solution)/shard_map/pallas_call | solution.py:512
  38.7 1.6 %collective-permute-start.3 = (bf16[2,2,4,32,128]{4,3,2,1,0:T(8,128)(2,1)S(1)}, bf16[2,2,4,32,128]{4,3,2,1,0:T(8,128)(2,1)S(1)}, u32[]{:S(2)}, u32[]{:S(2)}) collective-permute-start(bf16[2,2,4,32,128]{4,3,2,1,0:T(8,128)(2,1)S(1)} %get-tuple-element.39), channel_id=1, source_target_pairs={{0,8},{4,12},{8,0},{12,4},{16,24},{20,28},{24,16},{28,20},{1,9},{5... | collective-permute-start | bytes 393224 | tf_op jit(solution)/shard_map/ppermute | solution.py:495
  40.3 0.0 collective-permute-done.6.refs_1_
  40.3 0.0 collective-permute-done.7.refs_2_
  40.3 0.0 collective-permute-done.8.refs_3_
  40.3 0.0 collective-permute-done.5.received
  40.4 1.7 %shard_map.110 = (f32[32,4,128]{2,1,0:T(4,128)}, f32[4,32]{1,0:T(4,128)S(1)}, f32[32,128]{1,0:T(8,128)S(1)}) custom-call(bf16[1,2,4,32,128]{4,3,2,1,0:T(8,128)(2,1)S(1)} %get-tuple-element.44.kept, bf16[1,2,4,32,128]{4,3,2,1,0:T(8,128)(2,1)S(1)} %collective-permute-done.5.received, f32[8,128]{1,0:T(8,128)S(1)} %get-tuple-element.45.flags, ...), custom_call_target="tpu_custom_call" | custom-call | bytes 11070000 | tf_op jit(solution)/shard_map/pallas_call | solution.py:564
  42.0 5.9 %all-to-all-start = ((f32[32,4,128]{2,1,0:T(4,128)}), f32[32,4,128]{2,1,0:T(4,128)S(1)}, u32[]{:S(2)}, u32[]{:S(2)}) async-start(f32[32,4,128]{2,1,0:T(4,128)} %get-tuple-element.49), calls=%async_computation | async-start | bytes 131072 | tf_op jit(solution)/shard_map/all_to_all | solution.py:474
  48.0 0.0 collective-permute-done.3.received
  48.0 0.0 copy-done.8
  48.0 1.1 %shard_map.109 = (bf16[1,2,4,32,128]{4,3,2,1,0:T(8,128)(2,1)S(1)}, bf16[1,2,4,32,128]{4,3,2,1,0:T(8,128)(2,1)S(1)}, f32[8,128]{1,0:T(8,128)S(1)}) custom-call(s32[2,2,1024]{2,1,0:T(2,128)S(1)} %bitcast.16, s32[2,2,1024]{2,1,0:T(2,128)S(1)} %copy-done.8, bf16[2,2,4,32,128]{4,3,2,1,0:T(8,128)(2,1)S(1)} %get-tuple-element.38.mine, ...), custom_call_target="tpu_custom_call" | custom-call | tf_op jit(solution)/shard_map/pallas_call | solution.py:512
  49.1 7.1 %all-to-all-done = f32[32,4,128]{2,1,0:T(4,128)S(1)} async-done(((f32[32,4,128]{2,1,0:T(4,128)}), f32[32,4,128]{2,1,0:T(4,128)S(1)}, u32[]{:S(2)}, u32[]{:S(2)}) %all-to-all-start) | async-done | bytes 65568 | tf_op jit(solution)/shard_map/all_to_all | solution.py:474
  56.3 0.0 copy-done.3
  56.3 0.0 copy-done.13
  56.3 1.6 %shard_map.111 = f32[32,8,128]{2,1,0:T(8,128)} custom-call(s32[2,8]{1,0:T(2,128)S(1)} %bitcast.23, f32[8,4,4,128]{3,2,1,0:T(4,128)S(1)} %bitcast.18, bf16[8,2,128,128]{3,2,1,0:T(8,128)(2,1)S(1)} %copy-done.3), custom_call_target="tpu_custom_call" | custom-call | bytes 7380000 | tf_op jit(solution)/shard_map/pallas_call | solution.py:478
  57.9 2.6 %all-to-all-start.1 = ((f32[32,8,128]{2,1,0:T(8,128)}), f32[32,8,128]{2,1,0:T(8,128)S(1)}, u32[]{:S(2)}, u32[]{:S(2)}) async-start(f32[32,8,128]{2,1,0:T(8,128)} %shard_map.111), calls=%async_computation.1 | async-start | bytes 262144 | tf_op jit(solution)/shard_map/all_to_all | solution.py:574
  60.4 2.7 %collective-permute-start.4 = (bf16[1,2,4,32,128]{4,3,2,1,0:T(8,128)(2,1)S(1)}, bf16[1,2,4,32,128]{4,3,2,1,0:T(8,128)(2,1)S(1)}, u32[]{:S(2)}, u32[]{:S(2)}) collective-permute-start(bf16[1,2,4,32,128]{4,3,2,1,0:T(8,128)(2,1)S(1)} %get-tuple-element.41), channel_id=1, source_target_pairs={{0,16},{4,20},{8,24},{12,28},{16,0},{20,4},{24,8},{28,12},{1,17},{... | collective-permute-start | bytes 196616 | tf_op jit(solution)/shard_map/ppermute | solution.py:495
  63.2 9.4 %collective-permute-done.4.received = bf16[1,2,4,32,128]{4,3,2,1,0:T(8,128)(2,1)S(1)} collective-permute-done((bf16[1,2,4,32,128]{4,3,2,1,0:T(8,128)(2,1)S(1)}, bf16[1,2,4,32,128]{4,3,2,1,0:T(8,128)(2,1)S(1)}, u32[]{:S(2)}, u32[]{:S(2)}) %collective-permute-start.4) | collective-permute-done | bytes 65568 | tf_op jit(solution)/shard_map/ppermute | solution.py:495
  72.6 0.0 all-to-all-done.1
  72.6 1.7 %shard_map.112 = (f32[32,4,128]{2,1,0:T(4,128)}, f32[2,4,32]{2,1,0:T(4,128)}, f32[32,128]{1,0:T(8,128)S(1)}, f32[8,128]{1,0:T(8,128)S(1)}) custom-call(bf16[1,2,4,32,128]{4,3,2,1,0:T(8,128)(2,1)S(1)} %get-tuple-element.40.kept, bf16[1,2,4,32,128]{4,3,2,1,0:T(8,128)(2,1)S(1)} %collective-permute-done.4.received, f32[8,128]{1,0:T(8,128)S(1)} %get-tuple-element.42.flags, ...), custom_call_target="tpu_custom_call" | custom-call | bytes 11070000 | tf_op jit(solution)/shard_map/pallas_call | solution.py:577
  74.3 0.6 copy-done.11
  74.9 3.8 %all-to-all-start.2 = ((f32[32,4,128]{2,1,0:T(4,128)}), f32[32,4,128]{2,1,0:T(4,128)S(1)}, u32[]{:S(2)}, u32[]{:S(2)}) async-start(f32[32,4,128]{2,1,0:T(4,128)} %get-tuple-element.55), calls=%async_computation.2 | async-start | bytes 131072 | tf_op jit(solution)/shard_map/all_to_all | solution.py:474
  78.8 0.8 constant_dynamic-slice_fusion
  79.5 7.5 %all-to-all-done.2 = f32[32,4,128]{2,1,0:T(4,128)S(1)} async-done(((f32[32,4,128]{2,1,0:T(4,128)}), f32[32,4,128]{2,1,0:T(4,128)S(1)}, u32[]{:S(2)}, u32[]{:S(2)}) %all-to-all-start.2) | async-done | bytes 65568 | tf_op jit(solution)/shard_map/all_to_all | solution.py:474
  87.1 1.5 %shard_map.114 = f32[8,8,128]{2,1,0:T(8,128)} custom-call(s32[2,8]{1,0:T(2,128)S(1)} %bitcast.24, f32[8,4,4,128]{3,2,1,0:T(4,128)S(1)} %bitcast.17, bf16[8,2,128,128]{3,2,1,0:T(8,128)(2,1)S(1)} %copy-done.3), custom_call_target="tpu_custom_call" | custom-call | bytes 7380000 | tf_op jit(solution)/shard_map/pallas_call | solution.py:478
  88.6 3.3 %all-to-all-start.3 = ((f32[8,8,128]{2,1,0:T(8,128)}), f32[8,8,128]{2,1,0:T(8,128)S(1)}, u32[]{:S(2)}, u32[]{:S(2)}) async-start(f32[8,8,128]{2,1,0:T(8,128)} %shard_map.114), calls=%async_computation.3 | async-start | bytes 65536 | tf_op jit(solution)/shard_map/all_to_all | solution.py:587
  91.9 0.1 dynamic-slice_add_fusion
  92.0 0.7 reshape.31.places
  92.7 0.3 all-gather.3.cloned.1.call-done
  93.0 0.0 copy-done.10
  93.0 6.6 %shard_map.113 = bf16[2,124,32,128]{3,2,1,0:T(8,128)(2,1)} custom-call(s32[496]{0:T(512)} %reshape.31.places, f32[32,128]{1,0:T(8,128)} %copy-done.10, f32[32,128]{1,0:T(8,128)} %copy-done.11, f32[144,128]{1,0:T(8,128)} %constant.58.clone.refs_0_.mirror, bf16[768,32,128]{2,1,0:T(8,128)(2,1)} %bitcast.25), custom_call_target="tpu_custom_call" | custom-call | flops 8126464 | bytes 8323072 | tf_op jit(solution)/shard_map/pallas_call | solution.py:588
  99.6 0.0 all-to-all-done.3
  99.6 0.6 add_bitcast_fusion
  (11 shorter events, 0.0 us)
Async XLA Ops:
  7.2 85.8 %all-gather.3.cloned.1.call-start = ((), (), s32[]{:S(2)}) async-start(), calls=%async_computation.4 | async-start | bytes 7077888 | tf_op jit(solution)/shard_map/all_gather | solution.py:553
  7.2 1.1 %copy-start = (bf16[2,48,32,128]{3,2,1,0:T(8,128)(2,1)S(1)}, bf16[2,48,32,128]{3,2,1,0:T(8,128)(2,1)}, u32[]{:S(2)}) copy-start(bf16[2,48,32,128]{3,2,1,0:T(8,128)(2,1)} %refs_3_.1) | copy-start | bytes 2359300
  8.3 0.7 copy-start.5
  9.1 38.9 %copy-start.8 = (s32[2,2,1024]{2,1,0:T(2,128)S(1)}, s32[2,2,1024]{2,1,0:T(2,128)}, u32[]{:S(2)}) copy-start(s32[2,2,1024]{2,1,0:T(2,128)} %slots.11) | copy-start | bytes 49156
  9.1 47.2 %copy-start.3 = (bf16[8,2,128,128]{3,2,1,0:T(8,128)(2,1)S(1)}, bf16[8,2,128,128]{3,2,1,0:T(8,128)(2,1)}, u32[]{:S(2)}) copy-start(bf16[8,2,128,128]{3,2,1,0:T(8,128)(2,1)} %blocks.3) | copy-start | bytes 1572868
  9.1 47.2 %copy-start.13 = (s32[8,2]{0,1:T(2,128)S(1)}, s32[8,2]{0,1:T(2,128)}, u32[]{:S(2)}) copy-start(s32[8,2]{0,1:T(2,128)} %param.13) | copy-start | bytes 196
  10.0 10.8 %collective-permute-start.1 = (bf16[4,2,4,32,128]{4,3,2,1,0:T(8,128)(2,1)S(1)}, bf16[4,2,4,32,128]{4,3,2,1,0:T(8,128)(2,1)S(1)}, u32[]{:S(2)}, u32[]{:S(2)}) collective-permute-start(bf16[4,2,4,32,128]{4,3,2,1,0:T(8,128)(2,1)S(1)} %shard_map.103), channel_id=1, source_target_pairs={{0,4},{4,0},{8,12},{12,8},{16,20},{20,16},{24,28},{28,24},{1,5},{5... | collective-permute-start | bytes 786440 | tf_op jit(solution)/shard_map/ppermute | solution.py:495
  13.0 1.1 %copy-start.1 = (bf16[2,48,32,128]{3,2,1,0:T(8,128)(2,1)S(1)}, bf16[2,48,32,128]{3,2,1,0:T(8,128)(2,1)}, u32[]{:S(2)}) copy-start(bf16[2,48,32,128]{3,2,1,0:T(8,128)(2,1)} %refs_3_.1) | copy-start | bytes 2359300
  14.1 0.7 copy-start.6
  15.7 21.8 %collective-permute-start = (bf16[4,2,4,32,128]{4,3,2,1,0:T(8,128)(2,1)S(1)}, bf16[4,2,4,32,128]{4,3,2,1,0:T(8,128)(2,1)S(1)}, u32[]{:S(2)}, u32[]{:S(2)}) collective-permute-start(bf16[4,2,4,32,128]{4,3,2,1,0:T(8,128)(2,1)S(1)} %shard_map.104.refs_4_), channel_id=1, source_target_pairs={{0,4},{4,0},{8,12},{12,8},{16,20},{20,16},{24,28},{28,24},{1,5},{5... | collective-permute-start | bytes 786440 | tf_op jit(solution)/shard_map/ppermute | solution.py:495
  16.5 1.1 %copy-start.2 = (bf16[2,48,32,128]{3,2,1,0:T(8,128)(2,1)S(1)}, bf16[2,48,32,128]{3,2,1,0:T(8,128)(2,1)}, u32[]{:S(2)}) copy-start(bf16[2,48,32,128]{3,2,1,0:T(8,128)(2,1)} %refs_3_.1) | copy-start | bytes 2359300
  17.7 1.1 %copy-start.4 = (bf16[1296,256]{1,0:T(8,128)(2,1)S(1)}, bf16[1296,256]{1,0:T(8,128)(2,1)}, u32[]{:S(2)}) copy-start(bf16[1296,256]{1,0:T(8,128)(2,1)} %constant.57.clone.refs_1_) | copy-start | bytes 1990660
  18.8 0.9 copy-start.9
  19.7 0.7 copy-start.12
  20.8 0.7 copy-start.7
  22.7 8.8 %collective-permute-start.2 = (bf16[2,2,4,32,128]{4,3,2,1,0:T(8,128)(2,1)S(1)}, bf16[2,2,4,32,128]{4,3,2,1,0:T(8,128)(2,1)S(1)}, u32[]{:S(2)}, u32[]{:S(2)}) collective-permute-start(bf16[2,2,4,32,128]{4,3,2,1,0:T(8,128)(2,1)S(1)} %get-tuple-element.35), channel_id=1, source_target_pairs={{0,8},{4,12},{8,0},{12,4},{16,24},{20,28},{24,16},{28,20},{1,9},{5... | collective-permute-start | bytes 393224 | tf_op jit(solution)/shard_map/ppermute | solution.py:495
  32.6 7.7 %collective-permute-start.5 = (bf16[1,2,4,32,128]{4,3,2,1,0:T(8,128)(2,1)S(1)}, bf16[1,2,4,32,128]{4,3,2,1,0:T(8,128)(2,1)S(1)}, u32[]{:S(2)}, u32[]{:S(2)}) collective-permute-start(bf16[1,2,4,32,128]{4,3,2,1,0:T(8,128)(2,1)S(1)} %get-tuple-element.36), channel_id=1, source_target_pairs={{0,16},{4,20},{8,24},{12,28},{16,0},{20,4},{24,8},{28,12},{1,17},{... | collective-permute-start | bytes 196616 | tf_op jit(solution)/shard_map/ppermute | solution.py:495
  35.6 4.7 %collective-permute-start.6 = (f32[8,128]{1,0:T(8,128)S(1)}, f32[8,128]{1,0:T(8,128)S(1)}, u32[]{:S(2)}, u32[]{:S(2)}) collective-permute-start(f32[8,128]{1,0:T(8,128)S(1)} %bitcast.20), channel_id=1, source_target_pairs={{0,1},{1,0},{2,3},{3,2},{4,5},{5,4},{6,7},{7,6},{8,9},{9,8},{10,11... | collective-permute-start | bytes 12296 | tf_op jit(solution)/shard_map/ppermute | solution.py:525
  35.6 4.7 %collective-permute-start.7 = (f32[8,128]{1,0:T(8,128)S(1)}, f32[8,128]{1,0:T(8,128)S(1)}, u32[]{:S(2)}, u32[]{:S(2)}) collective-permute-start(f32[8,128]{1,0:T(8,128)S(1)} %bitcast.21), channel_id=1, source_target_pairs={{0,2},{1,3},{2,0},{3,1},{4,6},{5,7},{6,4},{7,5},{8,10},{9,11},{10,... | collective-permute-start | bytes 12296 | tf_op jit(solution)/shard_map/ppermute | solution.py:525
  37.1 3.2 %collective-permute-start.8 = (f32[8,128]{1,0:T(8,128)S(1)}, f32[8,128]{1,0:T(8,128)S(1)}, u32[]{:S(2)}, u32[]{:S(2)}) collective-permute-start(f32[8,128]{1,0:T(8,128)S(1)} %bitcast.22), channel_id=1, source_target_pairs={{0,3},{1,2},{2,1},{3,0},{4,7},{5,6},{6,5},{7,4},{8,11},{9,10},{10,... | collective-permute-start | bytes 12296 | tf_op jit(solution)/shard_map/ppermute | solution.py:525
  38.7 9.3 %collective-permute-start.3 = (bf16[2,2,4,32,128]{4,3,2,1,0:T(8,128)(2,1)S(1)}, bf16[2,2,4,32,128]{4,3,2,1,0:T(8,128)(2,1)S(1)}, u32[]{:S(2)}, u32[]{:S(2)}) collective-permute-start(bf16[2,2,4,32,128]{4,3,2,1,0:T(8,128)(2,1)S(1)} %get-tuple-element.39), channel_id=1, source_target_pairs={{0,8},{4,12},{8,0},{12,4},{16,24},{20,28},{24,16},{28,20},{1,9},{5... | collective-permute-start | bytes 393224 | tf_op jit(solution)/shard_map/ppermute | solution.py:495
  42.0 51.0 %copy-start.10 = (f32[32,128]{1,0:T(8,128)}, f32[32,128]{1,0:T(8,128)S(1)}, u32[]{:S(2)}) copy-start(f32[32,128]{1,0:T(8,128)S(1)} %get-tuple-element.48.c_base.c_first) | copy-start | bytes 49156
  42.0 14.2 %all-to-all-start = ((f32[32,4,128]{2,1,0:T(4,128)}), f32[32,4,128]{2,1,0:T(4,128)S(1)}, u32[]{:S(2)}, u32[]{:S(2)}) async-start(f32[32,4,128]{2,1,0:T(4,128)} %get-tuple-element.49), calls=%async_computation | async-start | bytes 131072 | tf_op jit(solution)/shard_map/all_to_all | solution.py:474
  57.9 14.8 %all-to-all-start.1 = ((f32[32,8,128]{2,1,0:T(8,128)}), f32[32,8,128]{2,1,0:T(8,128)S(1)}, u32[]{:S(2)}, u32[]{:S(2)}) async-start(f32[32,8,128]{2,1,0:T(8,128)} %shard_map.111), calls=%async_computation.1 | async-start | bytes 262144 | tf_op jit(solution)/shard_map/all_to_all | solution.py:574
  60.4 12.2 %collective-permute-start.4 = (bf16[1,2,4,32,128]{4,3,2,1,0:T(8,128)(2,1)S(1)}, bf16[1,2,4,32,128]{4,3,2,1,0:T(8,128)(2,1)S(1)}, u32[]{:S(2)}, u32[]{:S(2)}) collective-permute-start(bf16[1,2,4,32,128]{4,3,2,1,0:T(8,128)(2,1)S(1)} %get-tuple-element.41), channel_id=1, source_target_pairs={{0,16},{4,20},{8,24},{12,28},{16,0},{20,4},{24,8},{28,12},{1,17},{... | collective-permute-start | bytes 196616 | tf_op jit(solution)/shard_map/ppermute | solution.py:495
  74.3 0.6 copy-start.11
  74.9 12.1 %all-to-all-start.2 = ((f32[32,4,128]{2,1,0:T(4,128)}), f32[32,4,128]{2,1,0:T(4,128)S(1)}, u32[]{:S(2)}, u32[]{:S(2)}) async-start(f32[32,4,128]{2,1,0:T(4,128)} %get-tuple-element.55), calls=%async_computation.2 | async-start | bytes 131072 | tf_op jit(solution)/shard_map/all_to_all | solution.py:474
  88.6 11.0 %all-to-all-start.3 = ((f32[8,8,128]{2,1,0:T(8,128)}), f32[8,8,128]{2,1,0:T(8,128)S(1)}, u32[]{:S(2)}, u32[]{:S(2)}) async-start(f32[8,8,128]{2,1,0:T(8,128)} %shard_map.114), calls=%async_computation.3 | async-start | bytes 65536 | tf_op jit(solution)/shard_map/all_to_all | solution.py:587
Sparse Core Ops, SparseCore 0:
  10.1 82.8 all-gather.2

commit v6 on v5

--- a/solution.py
+++ b/solution.py
@@ -393,26 +393,31 @@
     out[...] = jnp.broadcast_to(jnp.concatenate(rows, axis=0)[None], out.shape)
 
 
-def science_kernel(places, c_first, c_second, mirror, gathered, out, store, ready, prof, sem):
+def science_kernel(places, c_first, c_second, mirror, gathered, out, store, part, ready, prof, sem):
     slab_rows = out.shape[2]
     my_tile, my_rec = lax.axis_index("tile"), lax.axis_index("rec")
+    layers = places.shape[0] // (out.shape[0] * SC_DEV)
     parts = sem.shape[0] - out.shape[0]
     size = store.shape[0] // parts
-    copies = [
-        pltpu.make_async_copy(gathered.at[pl.ds(i * size, size)], store.at[pl.ds(i * size, size)], sem.at[i])
-        for i in range(parts)
-    ]
+    copies = []
+    for i in range(parts):
+        at = (i % (parts // layers) * layers + i // (parts // layers)) * size
+        copies.append(pltpu.make_async_copy(gathered.at[pl.ds(at, size)], store.at[pl.ds(at, size)], sem.at[i]))
     for copy in copies:
         copy.start()
     weights = row_weights(my_rec, slab_rows)
     profile_rows = PT * SUB
     for f, c in enumerate((c_first, c_second)):
         prof[pl.ds(f * profile_rows, profile_rows)] = column_profiles(c[...], mirror)
-    for copy in copies:
+    start = lax.rem(my_tile * SC_DEV, PT)
+    twice = SC_DEV - PT
+    together = 6
+
+    def tile(f, l, k):
+        return store[places[(f * layers + l) * SC_DEV + k]].astype(jnp.float32)
+
+    for copy in copies[: parts // layers]:
         copy.wait()
-    layers = places.shape[0] // (out.shape[0] * SC_DEV)
-    start = lax.rem(my_tile * SC_DEV, PT)
-    written = []
     for f in range(out.shape[0]):
 
         def some(qs):
@@ -425,23 +430,30 @@
                 ]
                 shape = jnp.concatenate(shapes, axis=0)
                 both = not isinstance(q, int) or q + PT < SC_DEV
-                for k in (q, q + PT)[: 1 + both]:
-                    phase = None
-                    for l in range(layers):
-                        tile = store[places[(f * layers + l) * SC_DEV + k]].astype(jnp.float32)
-                        phase = tile if phase is None else phase + tile
-                    results.append((k, (phase - shape).astype(jnp.bfloat16)))
+                results += [(k, tile(f, 0, k) - shape) for k in (q, q + PT)[: 1 + both]]
             for k, value in results:
-                ready[f, k] = value
-
-        twice = SC_DEV - PT
-        together = 6
+                part[f, k] = value
 
         @pl.loop(0, twice // together)
         def _(q):
             some([q * together + j for j in range(together)])
 
         some(range(twice // together * together, PT))
+    for copy in copies[parts // layers :]:
+        copy.wait()
+    written = []
+    for f in range(out.shape[0]):
+
+        def rest(ks):
+            results = [(k, part[f, k] + functools.reduce(jnp.add, [tile(f, l, k) for l in range(1, layers)])) for k in ks]
+            for k, value in results:
+                ready[f, k] = value.astype(jnp.bfloat16)
+
+        @pl.loop(0, SC_DEV // 10)
+        def _(q):
+            rest([q * 10 + j for j in range(10)])
+
+        rest(range(SC_DEV // 10 * 10, SC_DEV))
         written.append(pltpu.make_async_copy(ready.at[f], out.at[f], sem.at[parts + f]))
         written[-1].start()
     for copy in written:
@@ -592,9 +604,10 @@
         out_specs=pl.BlockSpec(memory_space=pl.ANY),
         scratch_shapes=[
             pltpu.VMEM((n * layers * tiles_here, slab_rows, tile_px), screens.dtype),
+            pltpu.VMEM((frames, SC_DEV, slab_rows, tile_px), f32),
             pltpu.VMEM((frames, SC_DEV, slab_rows, tile_px), jnp.bfloat16),
             pltpu.VMEM((frames * PT * SUB, LANES), f32),
-            pltpu.SemaphoreType.DMA((n + frames,)),
+            pltpu.SemaphoreType.DMA((n * layers + frames,)),
         ],
         compiler_params=pltpu.CompilerParams(vmem_limit_bytes=60 << 20),
         cost_estimate=pl.CostEstimate(

time: 108 us -> 107 us (level)
  transfers between devices with their start and end apart: 14 -> 14, of which waited for: 5 -> 5; matrix products, arithmetic and copies ran while one was open for 2% -> 2% of each run, Pallas kernels for 18% -> 17%
where the time goes in v6:
time: 107 us
  waiting for transfers between devices  31.1 us (29%)
  starting transfers between devices  30.2 us (28%)
  Pallas kernels  19.4 us (18%)
  between operations  14.2 us (13%)
  local copies, waits for them, and re-layouts  11 us (10%)
    ppermute x6, waiting for transfers between devices, swap(): return lax.ppermute(x, 'tile', [(t, t ^ bit) for t in range(n)])  16.1 us
    all_to_all x2, waiting for transfers between devices, exchange(): lax.all_to_all(payload, ('tile', 'rec'), split_axis=0, concat_axis=0, til...  14.6 us
    ppermute x6, starting transfers between devices, swap(): return lax.ppermute(x, 'tile', [(t, t ^ bit) for t in range(n)])  12.7 us
    all_to_all x2, starting transfers between devices, exchange(): lax.all_to_all(payload, ('tile', 'rec'), split_axis=0, concat_axis=0, til...  9.75 us
    unnamed x29, local copies, waits for them, and re-layouts  9.54 us
    pallas_call x1, Pallas kernels, by_ring(): pl.pallas_call(science_kernel, out_shape=jax.ShapeDtypeStruct((frames, SC...  6.08 us
    pallas_call x4, Pallas kernels, merge(): pl.pallas_call(functools.partial(merge_kernel, frame, bits), in_specs=[sm...  4.65 us
    all_to_all x1, starting transfers between devices, by_ring(): lax.all_to_all(updates, 'tile', split_axis=0, concat_axis=0, tiled=True)  3.33 us
  transfers between devices with their start and end apart: 14, of which 5 were waited for; matrix products, arithmetic and copies ran while one was open for 2% of the time, Pallas kernels for 17%

profile of v6, /device:TPU:0, one launch (start us, length us, event | category | flops | bytes accessed | tf_op | source)
XLA Modules:
  0.0 106.6 jit_solution(5030008429604770093)
XLA Ops:
  7.2 0.0 all-gather.3.cloned.1.call-start
  7.2 0.0 copy-start
  7.2 1.1 %copy-done = bf16[2,48,32,128]{3,2,1,0:T(8,128)(2,1)S(1)} copy-done((bf16[2,48,32,128]{3,2,1,0:T(8,128)(2,1)S(1)}, bf16[2,48,32,128]{3,2,1,0:T(8,128)(2,1)}, u32[]{:S(2)}) %copy-start) | copy-done | bytes 786456
  8.3 0.0 copy-start.5
  8.3 0.7 copy-done.5
  9.1 0.9 shard_map.103
  9.9 0.0 all-gather.3.cloned.1.call-update
  10.0 3.0 %collective-permute-start.1 = (bf16[4,2,4,32,128]{4,3,2,1,0:T(8,128)(2,1)S(1)}, bf16[4,2,4,32,128]{4,3,2,1,0:T(8,128)(2,1)S(1)}, u32[]{:S(2)}, u32[]{:S(2)}) collective-permute-start(bf16[4,2,4,32,128]{4,3,2,1,0:T(8,128)(2,1)S(1)} %shard_map.103), channel_id=1, source_target_pairs={{0,4},{4,0},{8,12},{12,8},{16,20},{20,16},{24,28},{28,24},{1,5},{5... | collective-permute-start | bytes 786440 | tf_op jit(solution)/shard_map/ppermute | solution.py:507
  13.0 1.1 %copy-done.1 = bf16[2,48,32,128]{3,2,1,0:T(8,128)(2,1)S(1)} copy-done((bf16[2,48,32,128]{3,2,1,0:T(8,128)(2,1)S(1)}, bf16[2,48,32,128]{3,2,1,0:T(8,128)(2,1)}, u32[]{:S(2)}) %copy-start.1) | copy-done | bytes 786456
  14.1 0.7 copy-done.6
  14.9 0.9 shard_map.104.refs_4_
  15.7 0.1 collective-permute-start
  15.8 0.7 copy.13
  16.5 0.0 copy-start.2
  16.6 1.1 %copy-done.2 = bf16[2,48,32,128]{3,2,1,0:T(8,128)(2,1)S(1)} copy-done((bf16[2,48,32,128]{3,2,1,0:T(8,128)(2,1)S(1)}, bf16[2,48,32,128]{3,2,1,0:T(8,128)(2,1)}, u32[]{:S(2)}) %copy-start.2) | copy-done | bytes 786456
  17.7 1.1 %copy-done.4 = bf16[1296,256]{1,0:T(8,128)(2,1)S(1)} copy-done((bf16[1296,256]{1,0:T(8,128)(2,1)S(1)}, bf16[1296,256]{1,0:T(8,128)(2,1)}, u32[]{:S(2)}) %copy-start.4) | copy-done | bytes 663576
  18.8 0.9 copy-done.9
  19.7 0.7 copy-done.12
  20.4 0.4 shard_map.105
  20.7 0.0 collective-permute-done.1.received
  20.8 0.0 copy-start.7
  20.8 0.7 copy-done.7
  21.5 1.2 %shard_map.106 = (bf16[2,2,4,32,128]{4,3,2,1,0:T(8,128)(2,1)S(1)}, bf16[2,2,4,32,128]{4,3,2,1,0:T(8,128)(2,1)S(1)}) custom-call(s32[2,2,1024]{2,1,0:T(2,128)S(1)} %bitcast.13, s32[2,2,1024]{2,1,0:T(2,128)S(1)} %copy-done.7, bf16[2,48,32,128]{3,2,1,0:T(8,128)(2,1)S(1)} %get-tuple-element.31.mine, bf16[4,2,4,32,128]{4,3,2,1,0:T(8,128)(2,1)S(1)} %collective-permute-done.1.received), custom_call_target="tpu_custom_call" | custom-call | tf_op jit(solution)/shard_map/pallas_call | solution.py:524
  22.7 2.2 %collective-permute-start.2 = (bf16[2,2,4,32,128]{4,3,2,1,0:T(8,128)(2,1)S(1)}, bf16[2,2,4,32,128]{4,3,2,1,0:T(8,128)(2,1)S(1)}, u32[]{:S(2)}, u32[]{:S(2)}) collective-permute-start(bf16[2,2,4,32,128]{4,3,2,1,0:T(8,128)(2,1)S(1)} %get-tuple-element.35), channel_id=1, source_target_pairs={{0,8},{4,12},{8,0},{12,4},{16,24},{20,28},{24,16},{28,20},{1,9},{5... | collective-permute-start | bytes 393224 | tf_op jit(solution)/shard_map/ppermute | solution.py:507
  24.8 6.6 %collective-permute-done.2.received = bf16[2,2,4,32,128]{4,3,2,1,0:T(8,128)(2,1)S(1)} collective-permute-done((bf16[2,2,4,32,128]{4,3,2,1,0:T(8,128)(2,1)S(1)}, bf16[2,2,4,32,128]{4,3,2,1,0:T(8,128)(2,1)S(1)}, u32[]{:S(2)}, u32[]{:S(2)}) %collective-permute-start.2) | collective-permute-done | bytes 131104 | tf_op jit(solution)/shard_map/ppermute | solution.py:507
  31.5 1.1 %shard_map.107 = (bf16[1,2,4,32,128]{4,3,2,1,0:T(8,128)(2,1)S(1)}, bf16[1,2,4,32,128]{4,3,2,1,0:T(8,128)(2,1)S(1)}, f32[8,128]{1,0:T(8,128)S(1)}) custom-call(s32[2,2,1024]{2,1,0:T(2,128)S(1)} %bitcast.14, s32[2,2,1024]{2,1,0:T(2,128)S(1)} %copy-done.7, bf16[2,2,4,32,128]{4,3,2,1,0:T(8,128)(2,1)S(1)} %get-tuple-element.34.mine, ...), custom_call_target="tpu_custom_call" | custom-call | tf_op jit(solution)/shard_map/pallas_call | solution.py:524
  32.6 3.0 %collective-permute-start.5 = (bf16[1,2,4,32,128]{4,3,2,1,0:T(8,128)(2,1)S(1)}, bf16[1,2,4,32,128]{4,3,2,1,0:T(8,128)(2,1)S(1)}, u32[]{:S(2)}, u32[]{:S(2)}) collective-permute-start(bf16[1,2,4,32,128]{4,3,2,1,0:T(8,128)(2,1)S(1)} %get-tuple-element.36), channel_id=1, source_target_pairs={{0,16},{4,20},{8,24},{12,28},{16,0},{20,4},{24,8},{28,12},{1,17},{... | collective-permute-start | bytes 196616 | tf_op jit(solution)/shard_map/ppermute | solution.py:507
  35.6 0.0 collective-permute-start.6
  35.6 1.5 %collective-permute-start.7 = (f32[8,128]{1,0:T(8,128)S(1)}, f32[8,128]{1,0:T(8,128)S(1)}, u32[]{:S(2)}, u32[]{:S(2)}) collective-permute-start(f32[8,128]{1,0:T(8,128)S(1)} %bitcast.21), channel_id=1, source_target_pairs={{0,2},{1,3},{2,0},{3,1},{4,6},{5,7},{6,4},{7,5},{8,10},{9,11},{10,... | collective-permute-start | bytes 12296 | tf_op jit(solution)/shard_map/ppermute | solution.py:537
  37.1 0.4 collective-permute-start.8
  37.5 0.0 collective-permute-done.received
  37.5 1.2 %shard_map.108 = (bf16[2,2,4,32,128]{4,3,2,1,0:T(8,128)(2,1)S(1)}, bf16[2,2,4,32,128]{4,3,2,1,0:T(8,128)(2,1)S(1)}) custom-call(s32[2,2,1024]{2,1,0:T(2,128)S(1)} %bitcast.15, s32[2,2,1024]{2,1,0:T(2,128)S(1)} %copy-done.7, bf16[2,48,32,128]{3,2,1,0:T(8,128)(2,1)S(1)} %get-tuple-element.31.mine, bf16[4,2,4,32,128]{4,3,2,1,0:T(8,128)(2,1)S(1)} %collective-permute-done.received), custom_call_target="tpu_custom_call" | custom-call | tf_op jit(solution)/shard_map/pallas_call | solution.py:524
  38.7 1.6 %collective-permute-start.3 = (bf16[2,2,4,32,128]{4,3,2,1,0:T(8,128)(2,1)S(1)}, bf16[2,2,4,32,128]{4,3,2,1,0:T(8,128)(2,1)S(1)}, u32[]{:S(2)}, u32[]{:S(2)}) collective-permute-start(bf16[2,2,4,32,128]{4,3,2,1,0:T(8,128)(2,1)S(1)} %get-tuple-element.39), channel_id=1, source_target_pairs={{0,8},{4,12},{8,0},{12,4},{16,24},{20,28},{24,16},{28,20},{1,9},{5... | collective-permute-start | bytes 393224 | tf_op jit(solution)/shard_map/ppermute | solution.py:507
  40.3 0.0 collective-permute-done.6.refs_1_
  40.3 0.0 collective-permute-done.7.refs_2_
  40.3 0.0 collective-permute-done.8.refs_3_
  40.3 0.0 collective-permute-done.5.received
  40.4 1.7 %shard_map.110 = (f32[32,4,128]{2,1,0:T(4,128)}, f32[4,32]{1,0:T(4,128)S(1)}, f32[32,128]{1,0:T(8,128)S(1)}) custom-call(bf16[1,2,4,32,128]{4,3,2,1,0:T(8,128)(2,1)S(1)} %get-tuple-element.44.kept, bf16[1,2,4,32,128]{4,3,2,1,0:T(8,128)(2,1)S(1)} %collective-permute-done.5.received, f32[8,128]{1,0:T(8,128)S(1)} %get-tuple-element.45.flags, ...), custom_call_target="tpu_custom_call" | custom-call | bytes 11070000 | tf_op jit(solution)/shard_map/pallas_call | solution.py:576
  42.0 5.9 %all-to-all-start = ((f32[32,4,128]{2,1,0:T(4,128)}), f32[32,4,128]{2,1,0:T(4,128)S(1)}, u32[]{:S(2)}, u32[]{:S(2)}) async-start(f32[32,4,128]{2,1,0:T(4,128)} %get-tuple-element.49), calls=%async_computation | async-start | bytes 131072 | tf_op jit(solution)/shard_map/all_to_all | solution.py:486
  48.0 0.0 collective-permute-done.3.received
  48.0 0.0 copy-done.8
  48.0 1.1 %shard_map.109 = (bf16[1,2,4,32,128]{4,3,2,1,0:T(8,128)(2,1)S(1)}, bf16[1,2,4,32,128]{4,3,2,1,0:T(8,128)(2,1)S(1)}, f32[8,128]{1,0:T(8,128)S(1)}) custom-call(s32[2,2,1024]{2,1,0:T(2,128)S(1)} %bitcast.16, s32[2,2,1024]{2,1,0:T(2,128)S(1)} %copy-done.8, bf16[2,2,4,32,128]{4,3,2,1,0:T(8,128)(2,1)S(1)} %get-tuple-element.38.mine, ...), custom_call_target="tpu_custom_call" | custom-call | tf_op jit(solution)/shard_map/pallas_call | solution.py:524
  49.1 7.1 %all-to-all-done = f32[32,4,128]{2,1,0:T(4,128)S(1)} async-done(((f32[32,4,128]{2,1,0:T(4,128)}), f32[32,4,128]{2,1,0:T(4,128)S(1)}, u32[]{:S(2)}, u32[]{:S(2)}) %all-to-all-start) | async-done | bytes 65568 | tf_op jit(solution)/shard_map/all_to_all | solution.py:486
  56.3 0.0 copy-done.3
  56.3 0.0 copy-done.13
  56.3 1.6 %shard_map.111 = f32[32,8,128]{2,1,0:T(8,128)} custom-call(s32[2,8]{1,0:T(2,128)S(1)} %bitcast.23, f32[8,4,4,128]{3,2,1,0:T(4,128)S(1)} %bitcast.18, bf16[8,2,128,128]{3,2,1,0:T(8,128)(2,1)S(1)} %copy-done.3), custom_call_target="tpu_custom_call" | custom-call | bytes 7380000 | tf_op jit(solution)/shard_map/pallas_call | solution.py:490
  57.9 2.6 %all-to-all-start.1 = ((f32[32,8,128]{2,1,0:T(8,128)}), f32[32,8,128]{2,1,0:T(8,128)S(1)}, u32[]{:S(2)}, u32[]{:S(2)}) async-start(f32[32,8,128]{2,1,0:T(8,128)} %shard_map.111), calls=%async_computation.1 | async-start | bytes 262144 | tf_op jit(solution)/shard_map/all_to_all | solution.py:586
  60.5 2.7 %collective-permute-start.4 = (bf16[1,2,4,32,128]{4,3,2,1,0:T(8,128)(2,1)S(1)}, bf16[1,2,4,32,128]{4,3,2,1,0:T(8,128)(2,1)S(1)}, u32[]{:S(2)}, u32[]{:S(2)}) collective-permute-start(bf16[1,2,4,32,128]{4,3,2,1,0:T(8,128)(2,1)S(1)} %get-tuple-element.41), channel_id=1, source_target_pairs={{0,16},{4,20},{8,24},{12,28},{16,0},{20,4},{24,8},{28,12},{1,17},{... | collective-permute-start | bytes 196616 | tf_op jit(solution)/shard_map/ppermute | solution.py:507
  63.2 9.4 %collective-permute-done.4.received = bf16[1,2,4,32,128]{4,3,2,1,0:T(8,128)(2,1)S(1)} collective-permute-done((bf16[1,2,4,32,128]{4,3,2,1,0:T(8,128)(2,1)S(1)}, bf16[1,2,4,32,128]{4,3,2,1,0:T(8,128)(2,1)S(1)}, u32[]{:S(2)}, u32[]{:S(2)}) %collective-permute-start.4) | collective-permute-done | bytes 65568 | tf_op jit(solution)/shard_map/ppermute | solution.py:507
  72.6 0.0 all-to-all-done.1
  72.6 1.7 %shard_map.112 = (f32[32,4,128]{2,1,0:T(4,128)}, f32[2,4,32]{2,1,0:T(4,128)}, f32[32,128]{1,0:T(8,128)S(1)}, f32[8,128]{1,0:T(8,128)S(1)}) custom-call(bf16[1,2,4,32,128]{4,3,2,1,0:T(8,128)(2,1)S(1)} %get-tuple-element.40.kept, bf16[1,2,4,32,128]{4,3,2,1,0:T(8,128)(2,1)S(1)} %collective-permute-done.4.received, f32[8,128]{1,0:T(8,128)S(1)} %get-tuple-element.42.flags, ...), custom_call_target="tpu_custom_call" | custom-call | bytes 11070000 | tf_op jit(solution)/shard_map/pallas_call | solution.py:589
  74.3 0.6 copy-done.11
  74.9 3.8 %all-to-all-start.2 = ((f32[32,4,128]{2,1,0:T(4,128)}), f32[32,4,128]{2,1,0:T(4,128)S(1)}, u32[]{:S(2)}, u32[]{:S(2)}) async-start(f32[32,4,128]{2,1,0:T(4,128)} %get-tuple-element.55), calls=%async_computation.2 | async-start | bytes 131072 | tf_op jit(solution)/shard_map/all_to_all | solution.py:486
  78.8 0.8 constant_dynamic-slice_fusion
  79.5 7.5 %all-to-all-done.2 = f32[32,4,128]{2,1,0:T(4,128)S(1)} async-done(((f32[32,4,128]{2,1,0:T(4,128)}), f32[32,4,128]{2,1,0:T(4,128)S(1)}, u32[]{:S(2)}, u32[]{:S(2)}) %all-to-all-start.2) | async-done | bytes 65568 | tf_op jit(solution)/shard_map/all_to_all | solution.py:486
  87.1 1.5 %shard_map.114 = f32[8,8,128]{2,1,0:T(8,128)} custom-call(s32[2,8]{1,0:T(2,128)S(1)} %bitcast.24, f32[8,4,4,128]{3,2,1,0:T(4,128)S(1)} %bitcast.17, bf16[8,2,128,128]{3,2,1,0:T(8,128)(2,1)S(1)} %copy-done.3), custom_call_target="tpu_custom_call" | custom-call | bytes 7380000 | tf_op jit(solution)/shard_map/pallas_call | solution.py:490
  88.6 3.3 %all-to-all-start.3 = ((f32[8,8,128]{2,1,0:T(8,128)}), f32[8,8,128]{2,1,0:T(8,128)S(1)}, u32[]{:S(2)}, u32[]{:S(2)}) async-start(f32[8,8,128]{2,1,0:T(8,128)} %shard_map.114), calls=%async_computation.3 | async-start | bytes 65536 | tf_op jit(solution)/shard_map/all_to_all | solution.py:599
  91.9 0.1 dynamic-slice_add_fusion
  92.0 0.7 reshape.31.places
  92.7 0.3 all-gather.3.cloned.1.call-done
  93.0 0.0 copy-done.10
  93.0 6.1 %shard_map.113 = bf16[2,124,32,128]{3,2,1,0:T(8,128)(2,1)} custom-call(s32[496]{0:T(512)} %reshape.31.places, f32[32,128]{1,0:T(8,128)} %copy-done.10, f32[32,128]{1,0:T(8,128)} %copy-done.11, f32[144,128]{1,0:T(8,128)} %constant.58.clone.refs_0_.mirror, bf16[768,32,128]{2,1,0:T(8,128)(2,1)} %bitcast.25), custom_call_target="tpu_custom_call" | custom-call | flops 8126464 | bytes 8323072 | tf_op jit(solution)/shard_map/pallas_call | solution.py:600
  99.1 0.0 all-to-all-done.3
  99.1 0.6 add_bitcast_fusion
  (11 shorter events, 0.0 us)
Async XLA Ops:
  7.2 85.8 %all-gather.3.cloned.1.call-start = ((), (), s32[]{:S(2)}) async-start(), calls=%async_computation.4 | async-start | bytes 7077888 | tf_op jit(solution)/shard_map/all_gather | solution.py:565
  7.2 1.1 %copy-start = (bf16[2,48,32,128]{3,2,1,0:T(8,128)(2,1)S(1)}, bf16[2,48,32,128]{3,2,1,0:T(8,128)(2,1)}, u32[]{:S(2)}) copy-start(bf16[2,48,32,128]{3,2,1,0:T(8,128)(2,1)} %refs_3_.1) | copy-start | bytes 2359300
  8.3 0.7 copy-start.5
  9.1 38.9 %copy-start.8 = (s32[2,2,1024]{2,1,0:T(2,128)S(1)}, s32[2,2,1024]{2,1,0:T(2,128)}, u32[]{:S(2)}) copy-start(s32[2,2,1024]{2,1,0:T(2,128)} %slots.11) | copy-start | bytes 49156
  9.1 47.2 %copy-start.3 = (bf16[8,2,128,128]{3,2,1,0:T(8,128)(2,1)S(1)}, bf16[8,2,128,128]{3,2,1,0:T(8,128)(2,1)}, u32[]{:S(2)}) copy-start(bf16[8,2,128,128]{3,2,1,0:T(8,128)(2,1)} %blocks.3) | copy-start | bytes 1572868
  9.1 47.2 %copy-start.13 = (s32[8,2]{0,1:T(2,128)S(1)}, s32[8,2]{0,1:T(2,128)}, u32[]{:S(2)}) copy-start(s32[8,2]{0,1:T(2,128)} %param.13) | copy-start | bytes 196
  10.0 10.8 %collective-permute-start.1 = (bf16[4,2,4,32,128]{4,3,2,1,0:T(8,128)(2,1)S(1)}, bf16[4,2,4,32,128]{4,3,2,1,0:T(8,128)(2,1)S(1)}, u32[]{:S(2)}, u32[]{:S(2)}) collective-permute-start(bf16[4,2,4,32,128]{4,3,2,1,0:T(8,128)(2,1)S(1)} %shard_map.103), channel_id=1, source_target_pairs={{0,4},{4,0},{8,12},{12,8},{16,20},{20,16},{24,28},{28,24},{1,5},{5... | collective-permute-start | bytes 786440 | tf_op jit(solution)/shard_map/ppermute | solution.py:507
  13.0 1.1 %copy-start.1 = (bf16[2,48,32,128]{3,2,1,0:T(8,128)(2,1)S(1)}, bf16[2,48,32,128]{3,2,1,0:T(8,128)(2,1)}, u32[]{:S(2)}) copy-start(bf16[2,48,32,128]{3,2,1,0:T(8,128)(2,1)} %refs_3_.1) | copy-start | bytes 2359300
  14.1 0.7 copy-start.6
  15.7 21.8 %collective-permute-start = (bf16[4,2,4,32,128]{4,3,2,1,0:T(8,128)(2,1)S(1)}, bf16[4,2,4,32,128]{4,3,2,1,0:T(8,128)(2,1)S(1)}, u32[]{:S(2)}, u32[]{:S(2)}) collective-permute-start(bf16[4,2,4,32,128]{4,3,2,1,0:T(8,128)(2,1)S(1)} %shard_map.104.refs_4_), channel_id=1, source_target_pairs={{0,4},{4,0},{8,12},{12,8},{16,20},{20,16},{24,28},{28,24},{1,5},{5... | collective-permute-start | bytes 786440 | tf_op jit(solution)/shard_map/ppermute | solution.py:507
  16.5 1.1 %copy-start.2 = (bf16[2,48,32,128]{3,2,1,0:T(8,128)(2,1)S(1)}, bf16[2,48,32,128]{3,2,1,0:T(8,128)(2,1)}, u32[]{:S(2)}) copy-start(bf16[2,48,32,128]{3,2,1,0:T(8,128)(2,1)} %refs_3_.1) | copy-start | bytes 2359300
  17.7 1.1 %copy-start.4 = (bf16[1296,256]{1,0:T(8,128)(2,1)S(1)}, bf16[1296,256]{1,0:T(8,128)(2,1)}, u32[]{:S(2)}) copy-start(bf16[1296,256]{1,0:T(8,128)(2,1)} %constant.57.clone.refs_1_) | copy-start | bytes 1990660
  18.8 0.9 copy-start.9
  19.7 0.7 copy-start.12
  20.8 0.7 copy-start.7
  22.7 8.8 %collective-permute-start.2 = (bf16[2,2,4,32,128]{4,3,2,1,0:T(8,128)(2,1)S(1)}, bf16[2,2,4,32,128]{4,3,2,1,0:T(8,128)(2,1)S(1)}, u32[]{:S(2)}, u32[]{:S(2)}) collective-permute-start(bf16[2,2,4,32,128]{4,3,2,1,0:T(8,128)(2,1)S(1)} %get-tuple-element.35), channel_id=1, source_target_pairs={{0,8},{4,12},{8,0},{12,4},{16,24},{20,28},{24,16},{28,20},{1,9},{5... | collective-permute-start | bytes 393224 | tf_op jit(solution)/shard_map/ppermute | solution.py:507
  32.6 7.7 %collective-permute-start.5 = (bf16[1,2,4,32,128]{4,3,2,1,0:T(8,128)(2,1)S(1)}, bf16[1,2,4,32,128]{4,3,2,1,0:T(8,128)(2,1)S(1)}, u32[]{:S(2)}, u32[]{:S(2)}) collective-permute-start(bf16[1,2,4,32,128]{4,3,2,1,0:T(8,128)(2,1)S(1)} %get-tuple-element.36), channel_id=1, source_target_pairs={{0,16},{4,20},{8,24},{12,28},{16,0},{20,4},{24,8},{28,12},{1,17},{... | collective-permute-start | bytes 196616 | tf_op jit(solution)/shard_map/ppermute | solution.py:507
  35.6 4.7 %collective-permute-start.6 = (f32[8,128]{1,0:T(8,128)S(1)}, f32[8,128]{1,0:T(8,128)S(1)}, u32[]{:S(2)}, u32[]{:S(2)}) collective-permute-start(f32[8,128]{1,0:T(8,128)S(1)} %bitcast.20), channel_id=1, source_target_pairs={{0,1},{1,0},{2,3},{3,2},{4,5},{5,4},{6,7},{7,6},{8,9},{9,8},{10,11... | collective-permute-start | bytes 12296 | tf_op jit(solution)/shard_map/ppermute | solution.py:537
  35.6 4.7 %collective-permute-start.7 = (f32[8,128]{1,0:T(8,128)S(1)}, f32[8,128]{1,0:T(8,128)S(1)}, u32[]{:S(2)}, u32[]{:S(2)}) collective-permute-start(f32[8,128]{1,0:T(8,128)S(1)} %bitcast.21), channel_id=1, source_target_pairs={{0,2},{1,3},{2,0},{3,1},{4,6},{5,7},{6,4},{7,5},{8,10},{9,11},{10,... | collective-permute-start | bytes 12296 | tf_op jit(solution)/shard_map/ppermute | solution.py:537
  37.1 3.2 %collective-permute-start.8 = (f32[8,128]{1,0:T(8,128)S(1)}, f32[8,128]{1,0:T(8,128)S(1)}, u32[]{:S(2)}, u32[]{:S(2)}) collective-permute-start(f32[8,128]{1,0:T(8,128)S(1)} %bitcast.22), channel_id=1, source_target_pairs={{0,3},{1,2},{2,1},{3,0},{4,7},{5,6},{6,5},{7,4},{8,11},{9,10},{10,... | collective-permute-start | bytes 12296 | tf_op jit(solution)/shard_map/ppermute | solution.py:537
  38.7 9.3 %collective-permute-start.3 = (bf16[2,2,4,32,128]{4,3,2,1,0:T(8,128)(2,1)S(1)}, bf16[2,2,4,32,128]{4,3,2,1,0:T(8,128)(2,1)S(1)}, u32[]{:S(2)}, u32[]{:S(2)}) collective-permute-start(bf16[2,2,4,32,128]{4,3,2,1,0:T(8,128)(2,1)S(1)} %get-tuple-element.39), channel_id=1, source_target_pairs={{0,8},{4,12},{8,0},{12,4},{16,24},{20,28},{24,16},{28,20},{1,9},{5... | collective-permute-start | bytes 393224 | tf_op jit(solution)/shard_map/ppermute | solution.py:507
  42.0 51.0 %copy-start.10 = (f32[32,128]{1,0:T(8,128)}, f32[32,128]{1,0:T(8,128)S(1)}, u32[]{:S(2)}) copy-start(f32[32,128]{1,0:T(8,128)S(1)} %get-tuple-element.48.c_base.c_first) | copy-start | bytes 49156
  42.0 14.2 %all-to-all-start = ((f32[32,4,128]{2,1,0:T(4,128)}), f32[32,4,128]{2,1,0:T(4,128)S(1)}, u32[]{:S(2)}, u32[]{:S(2)}) async-start(f32[32,4,128]{2,1,0:T(4,128)} %get-tuple-element.49), calls=%async_computation | async-start | bytes 131072 | tf_op jit(solution)/shard_map/all_to_all | solution.py:486
  57.9 14.8 %all-to-all-start.1 = ((f32[32,8,128]{2,1,0:T(8,128)}), f32[32,8,128]{2,1,0:T(8,128)S(1)}, u32[]{:S(2)}, u32[]{:S(2)}) async-start(f32[32,8,128]{2,1,0:T(8,128)} %shard_map.111), calls=%async_computation.1 | async-start | bytes 262144 | tf_op jit(solution)/shard_map/all_to_all | solution.py:586
  60.5 12.2 %collective-permute-start.4 = (bf16[1,2,4,32,128]{4,3,2,1,0:T(8,128)(2,1)S(1)}, bf16[1,2,4,32,128]{4,3,2,1,0:T(8,128)(2,1)S(1)}, u32[]{:S(2)}, u32[]{:S(2)}) collective-permute-start(bf16[1,2,4,32,128]{4,3,2,1,0:T(8,128)(2,1)S(1)} %get-tuple-element.41), channel_id=1, source_target_pairs={{0,16},{4,20},{8,24},{12,28},{16,0},{20,4},{24,8},{28,12},{1,17},{... | collective-permute-start | bytes 196616 | tf_op jit(solution)/shard_map/ppermute | solution.py:507
  74.3 0.6 copy-start.11
  74.9 12.1 %all-to-all-start.2 = ((f32[32,4,128]{2,1,0:T(4,128)}), f32[32,4,128]{2,1,0:T(4,128)S(1)}, u32[]{:S(2)}, u32[]{:S(2)}) async-start(f32[32,4,128]{2,1,0:T(4,128)} %get-tuple-element.55), calls=%async_computation.2 | async-start | bytes 131072 | tf_op jit(solution)/shard_map/all_to_all | solution.py:486
  88.6 10.5 %all-to-all-start.3 = ((f32[8,8,128]{2,1,0:T(8,128)}), f32[8,8,128]{2,1,0:T(8,128)S(1)}, u32[]{:S(2)}, u32[]{:S(2)}) async-start(f32[8,8,128]{2,1,0:T(8,128)} %shard_map.114), calls=%async_computation.3 | async-start | bytes 65536 | tf_op jit(solution)/shard_map/all_to_all | solution.py:599
Sparse Core Ops, SparseCore 0:
  10.1 82.8 all-gather.2

commit v7 on v6

--- a/solution.py
+++ b/solution.py
@@ -609,7 +609,7 @@
             pltpu.VMEM((frames * PT * SUB, LANES), f32),
             pltpu.SemaphoreType.DMA((n * layers + frames,)),
         ],
-        compiler_params=pltpu.CompilerParams(vmem_limit_bytes=60 << 20),
+        compiler_params=pltpu.CompilerParams(vmem_limit_bytes=50 << 20),
         cost_estimate=pl.CostEstimate(
             flops=8 * frames * SC_DEV * slab_rows * tile_px,
             bytes_accessed=2 * (n * layers * tiles_here + frames * SC_DEV) * slab_rows * tile_px,

time: 107 us -> 107 us (level)
  local copies, waits for them, and re-layouts: 11 us -> 9.79 us
  waiting for transfers between devices: 31.1 us -> 32.3 us
    all_gather x1, waiting for transfers between devices: 0.32 us -> 1.5 us  [by_ring(): lax.all_gather(later(screens, wanted), 'tile', axis_index_groups=[ring])]
    unnamed x29 -> x27, local copies, waits for them, and re-layouts: 9.54 us -> 8.95 us
where the time goes in v7:
time: 107 us; the launch traced here: 106 us
  waiting for transfers between devices  32.3 us (30%)
  starting transfers between devices  30.2 us (28%)
  Pallas kernels  19 us (18%)
  between operations  14.2 us (13%)
  local copies, waits for them, and re-layouts  9.79 us (9%)
    ppermute x6, waiting for transfers between devices, swap(): return lax.ppermute(x, 'tile', [(t, t ^ bit) for t in range(n)])  16.1 us
    all_to_all x2, waiting for transfers between devices, exchange(): lax.all_to_all(payload, ('tile', 'rec'), split_axis=0, concat_axis=0, til...  14.6 us
    ppermute x6, starting transfers between devices, swap(): return lax.ppermute(x, 'tile', [(t, t ^ bit) for t in range(n)])  12.7 us
    all_to_all x2, starting transfers between devices, exchange(): lax.all_to_all(payload, ('tile', 'rec'), split_axis=0, concat_axis=0, til...  9.74 us
    unnamed x27, local copies, waits for them, and re-layouts  8.95 us
    pallas_call x1, Pallas kernels, by_ring(): pl.pallas_call(science_kernel, out_shape=jax.ShapeDtypeStruct((frames, SC...  5.72 us
    pallas_call x4, Pallas kernels, merge(): pl.pallas_call(functools.partial(merge_kernel, frame, bits), in_specs=[sm...  4.65 us
    all_to_all x1, starting transfers between devices, by_ring(): lax.all_to_all(updates, 'tile', split_axis=0, concat_axis=0, tiled=True)  3.33 us
  transfers between devices with their start and end apart: 14, of which 5 were waited for; matrix products, arithmetic and copies ran while one was open for 2% of the time, Pallas kernels for 17%

profile of v7, /device:TPU:0, one launch (start us, length us, event | category | flops | bytes accessed | tf_op | source)
XLA Modules:
  0.0 106.2 jit_solution(12516349278200751456)
XLA Ops:
  7.2 0.0 all-gather.3.cloned.1.call-start
  7.2 0.0 copy-start
  7.2 1.1 %copy-done = bf16[2,48,32,128]{3,2,1,0:T(8,128)(2,1)S(1)} copy-done((bf16[2,48,32,128]{3,2,1,0:T(8,128)(2,1)S(1)}, bf16[2,48,32,128]{3,2,1,0:T(8,128)(2,1)}, u32[]{:S(2)}) %copy-start) | copy-done | bytes 786456
  8.3 0.0 copy-start.5
  8.3 0.7 copy-done.5
  9.1 0.0 copy-start.8
  9.1 0.9 shard_map.103
  10.0 0.0 all-gather.3.cloned.1.call-update
  10.0 3.0 %collective-permute-start.1 = (bf16[4,2,4,32,128]{4,3,2,1,0:T(8,128)(2,1)S(1)}, bf16[4,2,4,32,128]{4,3,2,1,0:T(8,128)(2,1)S(1)}, u32[]{:S(2)}, u32[]{:S(2)}) collective-permute-start(bf16[4,2,4,32,128]{4,3,2,1,0:T(8,128)(2,1)S(1)} %shard_map.103), channel_id=1, source_target_pairs={{0,4},{4,0},{8,12},{12,8},{16,20},{20,16},{24,28},{28,24},{1,5},{5... | collective-permute-start | bytes 786440 | tf_op jit(solution)/shard_map/ppermute | solution.py:507
  13.0 1.1 %copy-done.1 = bf16[2,48,32,128]{3,2,1,0:T(8,128)(2,1)S(1)} copy-done((bf16[2,48,32,128]{3,2,1,0:T(8,128)(2,1)S(1)}, bf16[2,48,32,128]{3,2,1,0:T(8,128)(2,1)}, u32[]{:S(2)}) %copy-start.1) | copy-done | bytes 786456
  14.1 0.7 copy-done.6
  14.9 0.9 shard_map.104.refs_4_
  15.7 0.1 collective-permute-start
  15.8 0.7 copy.13
  16.6 0.0 copy-start.2
  16.6 1.1 %copy-done.2 = bf16[2,48,32,128]{3,2,1,0:T(8,128)(2,1)S(1)} copy-done((bf16[2,48,32,128]{3,2,1,0:T(8,128)(2,1)S(1)}, bf16[2,48,32,128]{3,2,1,0:T(8,128)(2,1)}, u32[]{:S(2)}) %copy-start.2) | copy-done | bytes 786456
  17.7 1.1 %copy-done.4 = bf16[1296,256]{1,0:T(8,128)(2,1)S(1)} copy-done((bf16[1296,256]{1,0:T(8,128)(2,1)S(1)}, bf16[1296,256]{1,0:T(8,128)(2,1)}, u32[]{:S(2)}) %copy-start.4) | copy-done | bytes 663576
  18.8 0.9 copy-done.9
  19.7 0.7 copy-done.11
  20.4 0.4 shard_map.105
  20.8 0.0 collective-permute-done.1.received
  20.8 0.0 copy-start.7
  20.8 0.7 copy-done.7
  21.5 1.2 %shard_map.106 = (bf16[2,2,4,32,128]{4,3,2,1,0:T(8,128)(2,1)S(1)}, bf16[2,2,4,32,128]{4,3,2,1,0:T(8,128)(2,1)S(1)}) custom-call(s32[2,2,1024]{2,1,0:T(2,128)S(1)} %bitcast.13, s32[2,2,1024]{2,1,0:T(2,128)S(1)} %copy-done.7, bf16[2,48,32,128]{3,2,1,0:T(8,128)(2,1)S(1)} %get-tuple-element.31.mine, bf16[4,2,4,32,128]{4,3,2,1,0:T(8,128)(2,1)S(1)} %collective-permute-done.1.received), custom_call_target="tpu_custom_call" | custom-call | tf_op jit(solution)/shard_map/pallas_call | solution.py:524
  22.7 2.2 %collective-permute-start.2 = (bf16[2,2,4,32,128]{4,3,2,1,0:T(8,128)(2,1)S(1)}, bf16[2,2,4,32,128]{4,3,2,1,0:T(8,128)(2,1)S(1)}, u32[]{:S(2)}, u32[]{:S(2)}) collective-permute-start(bf16[2,2,4,32,128]{4,3,2,1,0:T(8,128)(2,1)S(1)} %get-tuple-element.35), channel_id=1, source_target_pairs={{0,8},{4,12},{8,0},{12,4},{16,24},{20,28},{24,16},{28,20},{1,9},{5... | collective-permute-start | bytes 393224 | tf_op jit(solution)/shard_map/ppermute | solution.py:507
  24.8 6.6 %collective-permute-done.2.received = bf16[2,2,4,32,128]{4,3,2,1,0:T(8,128)(2,1)S(1)} collective-permute-done((bf16[2,2,4,32,128]{4,3,2,1,0:T(8,128)(2,1)S(1)}, bf16[2,2,4,32,128]{4,3,2,1,0:T(8,128)(2,1)S(1)}, u32[]{:S(2)}, u32[]{:S(2)}) %collective-permute-start.2) | collective-permute-done | bytes 131104 | tf_op jit(solution)/shard_map/ppermute | solution.py:507
  31.5 1.1 %shard_map.107 = (bf16[1,2,4,32,128]{4,3,2,1,0:T(8,128)(2,1)S(1)}, bf16[1,2,4,32,128]{4,3,2,1,0:T(8,128)(2,1)S(1)}, f32[8,128]{1,0:T(8,128)S(1)}) custom-call(s32[2,2,1024]{2,1,0:T(2,128)S(1)} %bitcast.14, s32[2,2,1024]{2,1,0:T(2,128)S(1)} %copy-done.7, bf16[2,2,4,32,128]{4,3,2,1,0:T(8,128)(2,1)S(1)} %get-tuple-element.34.mine, ...), custom_call_target="tpu_custom_call" | custom-call | tf_op jit(solution)/shard_map/pallas_call | solution.py:524
  32.6 3.0 %collective-permute-start.5 = (bf16[1,2,4,32,128]{4,3,2,1,0:T(8,128)(2,1)S(1)}, bf16[1,2,4,32,128]{4,3,2,1,0:T(8,128)(2,1)S(1)}, u32[]{:S(2)}, u32[]{:S(2)}) collective-permute-start(bf16[1,2,4,32,128]{4,3,2,1,0:T(8,128)(2,1)S(1)} %get-tuple-element.36), channel_id=1, source_target_pairs={{0,16},{4,20},{8,24},{12,28},{16,0},{20,4},{24,8},{28,12},{1,17},{... | collective-permute-start | bytes 196616 | tf_op jit(solution)/shard_map/ppermute | solution.py:507
  35.6 0.0 collective-permute-start.6
  35.6 1.5 %collective-permute-start.7 = (f32[8,128]{1,0:T(8,128)S(1)}, f32[8,128]{1,0:T(8,128)S(1)}, u32[]{:S(2)}, u32[]{:S(2)}) collective-permute-start(f32[8,128]{1,0:T(8,128)S(1)} %bitcast.21), channel_id=1, source_target_pairs={{0,2},{1,3},{2,0},{3,1},{4,6},{5,7},{6,4},{7,5},{8,10},{9,11},{10,... | collective-permute-start | bytes 12296 | tf_op jit(solution)/shard_map/ppermute | solution.py:537
  37.1 0.4 collective-permute-start.8
  37.5 0.0 collective-permute-done.received
  37.5 1.2 %shard_map.108 = (bf16[2,2,4,32,128]{4,3,2,1,0:T(8,128)(2,1)S(1)}, bf16[2,2,4,32,128]{4,3,2,1,0:T(8,128)(2,1)S(1)}) custom-call(s32[2,2,1024]{2,1,0:T(2,128)S(1)} %bitcast.15, s32[2,2,1024]{2,1,0:T(2,128)S(1)} %copy-done.7, bf16[2,48,32,128]{3,2,1,0:T(8,128)(2,1)S(1)} %get-tuple-element.31.mine, bf16[4,2,4,32,128]{4,3,2,1,0:T(8,128)(2,1)S(1)} %collective-permute-done.received), custom_call_target="tpu_custom_call" | custom-call | tf_op jit(solution)/shard_map/pallas_call | solution.py:524
  38.7 1.6 %collective-permute-start.3 = (bf16[2,2,4,32,128]{4,3,2,1,0:T(8,128)(2,1)S(1)}, bf16[2,2,4,32,128]{4,3,2,1,0:T(8,128)(2,1)S(1)}, u32[]{:S(2)}, u32[]{:S(2)}) collective-permute-start(bf16[2,2,4,32,128]{4,3,2,1,0:T(8,128)(2,1)S(1)} %get-tuple-element.39), channel_id=1, source_target_pairs={{0,8},{4,12},{8,0},{12,4},{16,24},{20,28},{24,16},{28,20},{1,9},{5... | collective-permute-start | bytes 393224 | tf_op jit(solution)/shard_map/ppermute | solution.py:507
  40.3 0.0 collective-permute-done.6.refs_1_
  40.3 0.0 collective-permute-done.7.refs_2_
  40.3 0.0 collective-permute-done.8.refs_3_
  40.4 0.0 collective-permute-done.5.received
  40.4 1.7 %shard_map.110 = (f32[32,4,128]{2,1,0:T(4,128)}, f32[4,32]{1,0:T(4,128)S(1)}, f32[32,128]{1,0:T(8,128)S(1)}) custom-call(bf16[1,2,4,32,128]{4,3,2,1,0:T(8,128)(2,1)S(1)} %get-tuple-element.44.kept, bf16[1,2,4,32,128]{4,3,2,1,0:T(8,128)(2,1)S(1)} %collective-permute-done.5.received, f32[8,128]{1,0:T(8,128)S(1)} %get-tuple-element.45.flags, ...), custom_call_target="tpu_custom_call" | custom-call | bytes 11070000 | tf_op jit(solution)/shard_map/pallas_call | solution.py:576
  42.0 5.9 %all-to-all-start = ((f32[32,4,128]{2,1,0:T(4,128)}), f32[32,4,128]{2,1,0:T(4,128)S(1)}, u32[]{:S(2)}, u32[]{:S(2)}) async-start(f32[32,4,128]{2,1,0:T(4,128)} %get-tuple-element.49), calls=%async_computation | async-start | bytes 131072 | tf_op jit(solution)/shard_map/all_to_all | solution.py:486
  48.0 0.0 collective-permute-done.3.received
  48.0 0.0 copy-done.8
  48.0 1.1 %shard_map.109 = (bf16[1,2,4,32,128]{4,3,2,1,0:T(8,128)(2,1)S(1)}, bf16[1,2,4,32,128]{4,3,2,1,0:T(8,128)(2,1)S(1)}, f32[8,128]{1,0:T(8,128)S(1)}) custom-call(s32[2,2,1024]{2,1,0:T(2,128)S(1)} %bitcast.16, s32[2,2,1024]{2,1,0:T(2,128)S(1)} %copy-done.8, bf16[2,2,4,32,128]{4,3,2,1,0:T(8,128)(2,1)S(1)} %get-tuple-element.38.mine, ...), custom_call_target="tpu_custom_call" | custom-call | tf_op jit(solution)/shard_map/pallas_call | solution.py:524
  49.1 7.1 %all-to-all-done = f32[32,4,128]{2,1,0:T(4,128)S(1)} async-done(((f32[32,4,128]{2,1,0:T(4,128)}), f32[32,4,128]{2,1,0:T(4,128)S(1)}, u32[]{:S(2)}, u32[]{:S(2)}) %all-to-all-start) | async-done | bytes 65568 | tf_op jit(solution)/shard_map/all_to_all | solution.py:486
  56.3 0.0 copy-done.3
  56.3 0.0 copy-done.12
  56.3 1.6 %shard_map.111 = f32[32,8,128]{2,1,0:T(8,128)} custom-call(s32[2,8]{1,0:T(2,128)S(1)} %bitcast.23, f32[8,4,4,128]{3,2,1,0:T(4,128)S(1)} %bitcast.18, bf16[8,2,128,128]{3,2,1,0:T(8,128)(2,1)S(1)} %copy-done.3), custom_call_target="tpu_custom_call" | custom-call | bytes 7380000 | tf_op jit(solution)/shard_map/pallas_call | solution.py:490
  57.9 2.6 %all-to-all-start.1 = ((f32[32,8,128]{2,1,0:T(8,128)}), f32[32,8,128]{2,1,0:T(8,128)S(1)}, u32[]{:S(2)}, u32[]{:S(2)}) async-start(f32[32,8,128]{2,1,0:T(8,128)} %shard_map.111), calls=%async_computation.1 | async-start | bytes 262144 | tf_op jit(solution)/shard_map/all_to_all | solution.py:586
  60.5 2.7 %collective-permute-start.4 = (bf16[1,2,4,32,128]{4,3,2,1,0:T(8,128)(2,1)S(1)}, bf16[1,2,4,32,128]{4,3,2,1,0:T(8,128)(2,1)S(1)}, u32[]{:S(2)}, u32[]{:S(2)}) collective-permute-start(bf16[1,2,4,32,128]{4,3,2,1,0:T(8,128)(2,1)S(1)} %get-tuple-element.41), channel_id=1, source_target_pairs={{0,16},{4,20},{8,24},{12,28},{16,0},{20,4},{24,8},{28,12},{1,17},{... | collective-permute-start | bytes 196616 | tf_op jit(solution)/shard_map/ppermute | solution.py:507
  63.2 9.5 %collective-permute-done.4.received = bf16[1,2,4,32,128]{4,3,2,1,0:T(8,128)(2,1)S(1)} collective-permute-done((bf16[1,2,4,32,128]{4,3,2,1,0:T(8,128)(2,1)S(1)}, bf16[1,2,4,32,128]{4,3,2,1,0:T(8,128)(2,1)S(1)}, u32[]{:S(2)}, u32[]{:S(2)}) %collective-permute-start.4) | collective-permute-done | bytes 65568 | tf_op jit(solution)/shard_map/ppermute | solution.py:507
  72.6 0.0 all-to-all-done.1
  72.6 1.7 %shard_map.112 = (f32[32,4,128]{2,1,0:T(4,128)}, f32[2,4,32]{2,1,0:T(4,128)}, f32[32,128]{1,0:T(8,128)S(1)}, f32[8,128]{1,0:T(8,128)S(1)}) custom-call(bf16[1,2,4,32,128]{4,3,2,1,0:T(8,128)(2,1)S(1)} %get-tuple-element.40.kept, bf16[1,2,4,32,128]{4,3,2,1,0:T(8,128)(2,1)S(1)} %collective-permute-done.4.received, f32[8,128]{1,0:T(8,128)S(1)} %get-tuple-element.42.flags, ...), custom_call_target="tpu_custom_call" | custom-call | bytes 11070000 | tf_op jit(solution)/shard_map/pallas_call | solution.py:589
  74.3 3.8 %all-to-all-start.2 = ((f32[32,4,128]{2,1,0:T(4,128)}), f32[32,4,128]{2,1,0:T(4,128)S(1)}, u32[]{:S(2)}, u32[]{:S(2)}) async-start(f32[32,4,128]{2,1,0:T(4,128)} %get-tuple-element.55), calls=%async_computation.2 | async-start | bytes 131072 | tf_op jit(solution)/shard_map/all_to_all | solution.py:486
  78.2 0.8 constant_dynamic-slice_fusion
  78.9 7.5 %all-to-all-done.2 = f32[32,4,128]{2,1,0:T(4,128)S(1)} async-done(((f32[32,4,128]{2,1,0:T(4,128)}), f32[32,4,128]{2,1,0:T(4,128)S(1)}, u32[]{:S(2)}, u32[]{:S(2)}) %all-to-all-start.2) | async-done | bytes 65568 | tf_op jit(solution)/shard_map/all_to_all | solution.py:486
  86.5 1.6 %shard_map.114 = f32[8,8,128]{2,1,0:T(8,128)} custom-call(s32[2,8]{1,0:T(2,128)S(1)} %bitcast.24, f32[8,4,4,128]{3,2,1,0:T(4,128)S(1)} %bitcast.17, bf16[8,2,128,128]{3,2,1,0:T(8,128)(2,1)S(1)} %copy-done.3), custom_call_target="tpu_custom_call" | custom-call | bytes 7380000 | tf_op jit(solution)/shard_map/pallas_call | solution.py:490
  88.0 3.3 %all-to-all-start.3 = ((f32[8,8,128]{2,1,0:T(8,128)}), f32[8,8,128]{2,1,0:T(8,128)S(1)}, u32[]{:S(2)}, u32[]{:S(2)}) async-start(f32[8,8,128]{2,1,0:T(8,128)} %shard_map.114), calls=%async_computation.3 | async-start | bytes 65536 | tf_op jit(solution)/shard_map/all_to_all | solution.py:599
  91.3 0.1 dynamic-slice_add_fusion
  91.4 0.1 reshape.31.places
  91.5 1.5 %all-gather.3.cloned.1.call-done = bf16[16,48,32,128]{3,2,1,0:T(8,128)(2,1)} async-done(((bf16[2,48,32,128]{3,2,1,0:T(8,128)(2,1)}), bf16[16,48,32,128]{3,2,1,0:T(8,128)(2,1)}) %all-gather.3.cloned.1.call-update) | async-done | bytes 6291472 | tf_op jit(solution)/shard_map/all_gather | solution.py:565
  93.0 0.0 copy-done.10
  93.0 5.7 %shard_map.113 = bf16[2,124,32,128]{3,2,1,0:T(8,128)(2,1)} custom-call(s32[496]{0:T(512)S(1)} %reshape.31.places, f32[32,128]{1,0:T(8,128)S(1)} %get-tuple-element.48.c_base.c_first, f32[32,128]{1,0:T(8,128)S(1)} %get-tuple-element.53.c_second, f32[144,128]{1,0:T(8,128)S(1)} %copy-done.10, bf16[768,32,128]{2,1,0:T(8,128)(2,1)} %bitcast.25), custom_call_target="tpu_custom_call" | custom-call | flops 8126464 | bytes 8323072 | tf_op jit(solution)/shard_map/pallas_call | solution.py:600
  98.7 0.0 all-to-all-done.3
  98.8 0.6 add_bitcast_fusion
  (9 shorter events, 0.0 us)
Async XLA Ops:
  7.2 85.9 %all-gather.3.cloned.1.call-start = ((), (), s32[]{:S(2)}) async-start(), calls=%async_computation.4 | async-start | bytes 7077888 | tf_op jit(solution)/shard_map/all_gather | solution.py:565
  7.2 1.1 %copy-start = (bf16[2,48,32,128]{3,2,1,0:T(8,128)(2,1)S(1)}, bf16[2,48,32,128]{3,2,1,0:T(8,128)(2,1)}, u32[]{:S(2)}) copy-start(bf16[2,48,32,128]{3,2,1,0:T(8,128)(2,1)} %refs_3_.1) | copy-start | bytes 2359300
  8.3 0.7 copy-start.5
  9.1 38.9 %copy-start.8 = (s32[2,2,1024]{2,1,0:T(2,128)S(1)}, s32[2,2,1024]{2,1,0:T(2,128)}, u32[]{:S(2)}) copy-start(s32[2,2,1024]{2,1,0:T(2,128)} %slots.11) | copy-start | bytes 49156
  9.1 47.2 %copy-start.3 = (bf16[8,2,128,128]{3,2,1,0:T(8,128)(2,1)S(1)}, bf16[8,2,128,128]{3,2,1,0:T(8,128)(2,1)}, u32[]{:S(2)}) copy-start(bf16[8,2,128,128]{3,2,1,0:T(8,128)(2,1)} %blocks.3) | copy-start | bytes 1572868
  9.1 47.2 %copy-start.12 = (s32[8,2]{0,1:T(2,128)S(1)}, s32[8,2]{0,1:T(2,128)}, u32[]{:S(2)}) copy-start(s32[8,2]{0,1:T(2,128)} %param.13) | copy-start | bytes 196
  9.1 84.0 %copy-start.10 = (f32[144,128]{1,0:T(8,128)S(1)}, f32[144,128]{1,0:T(8,128)}, u32[]{:S(2)}) copy-start(f32[144,128]{1,0:T(8,128)} %constant.58.clone.refs_0_.mirror) | copy-start | bytes 221188
  10.0 10.8 %collective-permute-start.1 = (bf16[4,2,4,32,128]{4,3,2,1,0:T(8,128)(2,1)S(1)}, bf16[4,2,4,32,128]{4,3,2,1,0:T(8,128)(2,1)S(1)}, u32[]{:S(2)}, u32[]{:S(2)}) collective-permute-start(bf16[4,2,4,32,128]{4,3,2,1,0:T(8,128)(2,1)S(1)} %shard_map.103), channel_id=1, source_target_pairs={{0,4},{4,0},{8,12},{12,8},{16,20},{20,16},{24,28},{28,24},{1,5},{5... | collective-permute-start | bytes 786440 | tf_op jit(solution)/shard_map/ppermute | solution.py:507
  13.0 1.1 %copy-start.1 = (bf16[2,48,32,128]{3,2,1,0:T(8,128)(2,1)S(1)}, bf16[2,48,32,128]{3,2,1,0:T(8,128)(2,1)}, u32[]{:S(2)}) copy-start(bf16[2,48,32,128]{3,2,1,0:T(8,128)(2,1)} %refs_3_.1) | copy-start | bytes 2359300
  14.1 0.7 copy-start.6
  15.7 21.8 %collective-permute-start = (bf16[4,2,4,32,128]{4,3,2,1,0:T(8,128)(2,1)S(1)}, bf16[4,2,4,32,128]{4,3,2,1,0:T(8,128)(2,1)S(1)}, u32[]{:S(2)}, u32[]{:S(2)}) collective-permute-start(bf16[4,2,4,32,128]{4,3,2,1,0:T(8,128)(2,1)S(1)} %shard_map.104.refs_4_), channel_id=1, source_target_pairs={{0,4},{4,0},{8,12},{12,8},{16,20},{20,16},{24,28},{28,24},{1,5},{5... | collective-permute-start | bytes 786440 | tf_op jit(solution)/shard_map/ppermute | solution.py:507
  16.6 1.1 %copy-start.2 = (bf16[2,48,32,128]{3,2,1,0:T(8,128)(2,1)S(1)}, bf16[2,48,32,128]{3,2,1,0:T(8,128)(2,1)}, u32[]{:S(2)}) copy-start(bf16[2,48,32,128]{3,2,1,0:T(8,128)(2,1)} %refs_3_.1) | copy-start | bytes 2359300
  17.7 1.1 %copy-start.4 = (bf16[1296,256]{1,0:T(8,128)(2,1)S(1)}, bf16[1296,256]{1,0:T(8,128)(2,1)}, u32[]{:S(2)}) copy-start(bf16[1296,256]{1,0:T(8,128)(2,1)} %constant.57.clone.refs_1_) | copy-start | bytes 1990660
  18.8 0.9 copy-start.9
  19.7 0.7 copy-start.11
  20.8 0.7 copy-start.7
  22.7 8.8 %collective-permute-start.2 = (bf16[2,2,4,32,128]{4,3,2,1,0:T(8,128)(2,1)S(1)}, bf16[2,2,4,32,128]{4,3,2,1,0:T(8,128)(2,1)S(1)}, u32[]{:S(2)}, u32[]{:S(2)}) collective-permute-start(bf16[2,2,4,32,128]{4,3,2,1,0:T(8,128)(2,1)S(1)} %get-tuple-element.35), channel_id=1, source_target_pairs={{0,8},{4,12},{8,0},{12,4},{16,24},{20,28},{24,16},{28,20},{1,9},{5... | collective-permute-start | bytes 393224 | tf_op jit(solution)/shard_map/ppermute | solution.py:507
  32.6 7.7 %collective-permute-start.5 = (bf16[1,2,4,32,128]{4,3,2,1,0:T(8,128)(2,1)S(1)}, bf16[1,2,4,32,128]{4,3,2,1,0:T(8,128)(2,1)S(1)}, u32[]{:S(2)}, u32[]{:S(2)}) collective-permute-start(bf16[1,2,4,32,128]{4,3,2,1,0:T(8,128)(2,1)S(1)} %get-tuple-element.36), channel_id=1, source_target_pairs={{0,16},{4,20},{8,24},{12,28},{16,0},{20,4},{24,8},{28,12},{1,17},{... | collective-permute-start | bytes 196616 | tf_op jit(solution)/shard_map/ppermute | solution.py:507
  35.6 4.7 %collective-permute-start.6 = (f32[8,128]{1,0:T(8,128)S(1)}, f32[8,128]{1,0:T(8,128)S(1)}, u32[]{:S(2)}, u32[]{:S(2)}) collective-permute-start(f32[8,128]{1,0:T(8,128)S(1)} %bitcast.20), channel_id=1, source_target_pairs={{0,1},{1,0},{2,3},{3,2},{4,5},{5,4},{6,7},{7,6},{8,9},{9,8},{10,11... | collective-permute-start | bytes 12296 | tf_op jit(solution)/shard_map/ppermute | solution.py:537
  35.6 4.7 %collective-permute-start.7 = (f32[8,128]{1,0:T(8,128)S(1)}, f32[8,128]{1,0:T(8,128)S(1)}, u32[]{:S(2)}, u32[]{:S(2)}) collective-permute-start(f32[8,128]{1,0:T(8,128)S(1)} %bitcast.21), channel_id=1, source_target_pairs={{0,2},{1,3},{2,0},{3,1},{4,6},{5,7},{6,4},{7,5},{8,10},{9,11},{10,... | collective-permute-start | bytes 12296 | tf_op jit(solution)/shard_map/ppermute | solution.py:537
  37.1 3.2 %collective-permute-start.8 = (f32[8,128]{1,0:T(8,128)S(1)}, f32[8,128]{1,0:T(8,128)S(1)}, u32[]{:S(2)}, u32[]{:S(2)}) collective-permute-start(f32[8,128]{1,0:T(8,128)S(1)} %bitcast.22), channel_id=1, source_target_pairs={{0,3},{1,2},{2,1},{3,0},{4,7},{5,6},{6,5},{7,4},{8,11},{9,10},{10,... | collective-permute-start | bytes 12296 | tf_op jit(solution)/shard_map/ppermute | solution.py:537
  38.7 9.3 %collective-permute-start.3 = (bf16[2,2,4,32,128]{4,3,2,1,0:T(8,128)(2,1)S(1)}, bf16[2,2,4,32,128]{4,3,2,1,0:T(8,128)(2,1)S(1)}, u32[]{:S(2)}, u32[]{:S(2)}) collective-permute-start(bf16[2,2,4,32,128]{4,3,2,1,0:T(8,128)(2,1)S(1)} %get-tuple-element.39), channel_id=1, source_target_pairs={{0,8},{4,12},{8,0},{12,4},{16,24},{20,28},{24,16},{28,20},{1,9},{5... | collective-permute-start | bytes 393224 | tf_op jit(solution)/shard_map/ppermute | solution.py:507
  42.0 14.2 %all-to-all-start = ((f32[32,4,128]{2,1,0:T(4,128)}), f32[32,4,128]{2,1,0:T(4,128)S(1)}, u32[]{:S(2)}, u32[]{:S(2)}) async-start(f32[32,4,128]{2,1,0:T(4,128)} %get-tuple-element.49), calls=%async_computation | async-start | bytes 131072 | tf_op jit(solution)/shard_map/all_to_all | solution.py:486
  57.9 14.8 %all-to-all-start.1 = ((f32[32,8,128]{2,1,0:T(8,128)}), f32[32,8,128]{2,1,0:T(8,128)S(1)}, u32[]{:S(2)}, u32[]{:S(2)}) async-start(f32[32,8,128]{2,1,0:T(8,128)} %shard_map.111), calls=%async_computation.1 | async-start | bytes 262144 | tf_op jit(solution)/shard_map/all_to_all | solution.py:586
  60.5 12.2 %collective-permute-start.4 = (bf16[1,2,4,32,128]{4,3,2,1,0:T(8,128)(2,1)S(1)}, bf16[1,2,4,32,128]{4,3,2,1,0:T(8,128)(2,1)S(1)}, u32[]{:S(2)}, u32[]{:S(2)}) collective-permute-start(bf16[1,2,4,32,128]{4,3,2,1,0:T(8,128)(2,1)S(1)} %get-tuple-element.41), channel_id=1, source_target_pairs={{0,16},{4,20},{8,24},{12,28},{16,0},{20,4},{24,8},{28,12},{1,17},{... | collective-permute-start | bytes 196616 | tf_op jit(solution)/shard_map/ppermute | solution.py:507
  74.3 12.1 %all-to-all-start.2 = ((f32[32,4,128]{2,1,0:T(4,128)}), f32[32,4,128]{2,1,0:T(4,128)S(1)}, u32[]{:S(2)}, u32[]{:S(2)}) async-start(f32[32,4,128]{2,1,0:T(4,128)} %get-tuple-element.55), calls=%async_computation.2 | async-start | bytes 131072 | tf_op jit(solution)/shard_map/all_to_all | solution.py:486
  88.0 10.7 %all-to-all-start.3 = ((f32[8,8,128]{2,1,0:T(8,128)}), f32[8,8,128]{2,1,0:T(8,128)S(1)}, u32[]{:S(2)}, u32[]{:S(2)}) async-start(f32[8,8,128]{2,1,0:T(8,128)} %shard_map.114), calls=%async_computation.3 | async-start | bytes 65536 | tf_op jit(solution)/shard_map/all_to_all | solution.py:599
Sparse Core Ops, SparseCore 0:
  10.1 82.8 all-gather.2

commit v8 on v7

--- a/solution.py
+++ b/solution.py
@@ -411,7 +411,7 @@
         prof[pl.ds(f * profile_rows, profile_rows)] = column_profiles(c[...], mirror)
     start = lax.rem(my_tile * SC_DEV, PT)
     twice = SC_DEV - PT
-    together = 6
+    together = 10
 
     def tile(f, l, k):
         return store[places[(f * layers + l) * SC_DEV + k]].astype(jnp.float32)

time: 107 us -> 107 us (level)
  no operation moved by 1% of the time
where the time goes in v8:
time: 107 us; the launch traced here: 106 us
  waiting for transfers between devices  32.3 us (30%)
  starting transfers between devices  30.2 us (28%)
  Pallas kernels  19 us (18%)
  between operations  14.2 us (13%)
  local copies, waits for them, and re-layouts  9.79 us (9%)
    ppermute x6, waiting for transfers between devices, swap(): return lax.ppermute(x, 'tile', [(t, t ^ bit) for t in range(n)])  16.1 us
    all_to_all x2, waiting for transfers between devices, exchange(): lax.all_to_all(payload, ('tile', 'rec'), split_axis=0, concat_axis=0, til...  14.6 us
    ppermute x6, starting transfers between devices, swap(): return lax.ppermute(x, 'tile', [(t, t ^ bit) for t in range(n)])  12.7 us
    all_to_all x2, starting transfers between devices, exchange(): lax.all_to_all(payload, ('tile', 'rec'), split_axis=0, concat_axis=0, til...  9.74 us
    unnamed x27, local copies, waits for them, and re-layouts  8.95 us
    pallas_call x1, Pallas kernels, by_ring(): pl.pallas_call(science_kernel, out_shape=jax.ShapeDtypeStruct((frames, SC...  5.67 us
    pallas_call x4, Pallas kernels, merge(): pl.pallas_call(functools.partial(merge_kernel, frame, bits), in_specs=[sm...  4.65 us
    all_to_all x1, starting transfers between devices, by_ring(): lax.all_to_all(updates, 'tile', split_axis=0, concat_axis=0, tiled=True)  3.33 us
  transfers between devices with their start and end apart: 14, of which 5 were waited for; matrix products, arithmetic and copies ran while one was open for 2% of the time, Pallas kernels for 17%

profile of v8, /device:TPU:0, one launch (start us, length us, event | category | flops | bytes accessed | tf_op | source)
XLA Modules:
  0.0 106.2 jit_solution(8613732704818934977)
XLA Ops:
  7.2 0.0 all-gather.3.cloned.1.call-start
  7.2 0.0 copy-start
  7.2 1.1 %copy-done = bf16[2,48,32,128]{3,2,1,0:T(8,128)(2,1)S(1)} copy-done((bf16[2,48,32,128]{3,2,1,0:T(8,128)(2,1)S(1)}, bf16[2,48,32,128]{3,2,1,0:T(8,128)(2,1)}, u32[]{:S(2)}) %copy-start) | copy-done | bytes 786456
  8.3 0.0 copy-start.5
  8.3 0.7 copy-done.5
  9.1 0.0 copy-start.8
  9.1 0.9 shard_map.103
  10.0 0.0 all-gather.3.cloned.1.call-update
  10.0 3.0 %collective-permute-start.1 = (bf16[4,2,4,32,128]{4,3,2,1,0:T(8,128)(2,1)S(1)}, bf16[4,2,4,32,128]{4,3,2,1,0:T(8,128)(2,1)S(1)}, u32[]{:S(2)}, u32[]{:S(2)}) collective-permute-start(bf16[4,2,4,32,128]{4,3,2,1,0:T(8,128)(2,1)S(1)} %shard_map.103), channel_id=1, source_target_pairs={{0,4},{4,0},{8,12},{12,8},{16,20},{20,16},{24,28},{28,24},{1,5},{5... | collective-permute-start | bytes 786440 | tf_op jit(solution)/shard_map/ppermute | solution.py:507
  13.0 1.1 %copy-done.1 = bf16[2,48,32,128]{3,2,1,0:T(8,128)(2,1)S(1)} copy-done((bf16[2,48,32,128]{3,2,1,0:T(8,128)(2,1)S(1)}, bf16[2,48,32,128]{3,2,1,0:T(8,128)(2,1)}, u32[]{:S(2)}) %copy-start.1) | copy-done | bytes 786456
  14.1 0.7 copy-done.6
  14.9 0.9 shard_map.104.refs_4_
  15.7 0.1 collective-permute-start
  15.8 0.7 copy.13
  16.6 0.0 copy-start.2
  16.6 1.1 %copy-done.2 = bf16[2,48,32,128]{3,2,1,0:T(8,128)(2,1)S(1)} copy-done((bf16[2,48,32,128]{3,2,1,0:T(8,128)(2,1)S(1)}, bf16[2,48,32,128]{3,2,1,0:T(8,128)(2,1)}, u32[]{:S(2)}) %copy-start.2) | copy-done | bytes 786456
  17.7 1.1 %copy-done.4 = bf16[1296,256]{1,0:T(8,128)(2,1)S(1)} copy-done((bf16[1296,256]{1,0:T(8,128)(2,1)S(1)}, bf16[1296,256]{1,0:T(8,128)(2,1)}, u32[]{:S(2)}) %copy-start.4) | copy-done | bytes 663576
  18.8 0.9 copy-done.9
  19.7 0.7 copy-done.11
  20.4 0.4 shard_map.105
  20.8 0.0 collective-permute-done.1.received
  20.8 0.0 copy-start.7
  20.8 0.7 copy-done.7
  21.5 1.2 %shard_map.106 = (bf16[2,2,4,32,128]{4,3,2,1,0:T(8,128)(2,1)S(1)}, bf16[2,2,4,32,128]{4,3,2,1,0:T(8,128)(2,1)S(1)}) custom-call(s32[2,2,1024]{2,1,0:T(2,128)S(1)} %bitcast.13, s32[2,2,1024]{2,1,0:T(2,128)S(1)} %copy-done.7, bf16[2,48,32,128]{3,2,1,0:T(8,128)(2,1)S(1)} %get-tuple-element.31.mine, bf16[4,2,4,32,128]{4,3,2,1,0:T(8,128)(2,1)S(1)} %collective-permute-done.1.received), custom_call_target="tpu_custom_call" | custom-call | tf_op jit(solution)/shard_map/pallas_call | solution.py:524
  22.7 2.2 %collective-permute-start.2 = (bf16[2,2,4,32,128]{4,3,2,1,0:T(8,128)(2,1)S(1)}, bf16[2,2,4,32,128]{4,3,2,1,0:T(8,128)(2,1)S(1)}, u32[]{:S(2)}, u32[]{:S(2)}) collective-permute-start(bf16[2,2,4,32,128]{4,3,2,1,0:T(8,128)(2,1)S(1)} %get-tuple-element.35), channel_id=1, source_target_pairs={{0,8},{4,12},{8,0},{12,4},{16,24},{20,28},{24,16},{28,20},{1,9},{5... | collective-permute-start | bytes 393224 | tf_op jit(solution)/shard_map/ppermute | solution.py:507
  24.8 6.6 %collective-permute-done.2.received = bf16[2,2,4,32,128]{4,3,2,1,0:T(8,128)(2,1)S(1)} collective-permute-done((bf16[2,2,4,32,128]{4,3,2,1,0:T(8,128)(2,1)S(1)}, bf16[2,2,4,32,128]{4,3,2,1,0:T(8,128)(2,1)S(1)}, u32[]{:S(2)}, u32[]{:S(2)}) %collective-permute-start.2) | collective-permute-done | bytes 131104 | tf_op jit(solution)/shard_map/ppermute | solution.py:507
  31.5 1.1 %shard_map.107 = (bf16[1,2,4,32,128]{4,3,2,1,0:T(8,128)(2,1)S(1)}, bf16[1,2,4,32,128]{4,3,2,1,0:T(8,128)(2,1)S(1)}, f32[8,128]{1,0:T(8,128)S(1)}) custom-call(s32[2,2,1024]{2,1,0:T(2,128)S(1)} %bitcast.14, s32[2,2,1024]{2,1,0:T(2,128)S(1)} %copy-done.7, bf16[2,2,4,32,128]{4,3,2,1,0:T(8,128)(2,1)S(1)} %get-tuple-element.34.mine, ...), custom_call_target="tpu_custom_call" | custom-call | tf_op jit(solution)/shard_map/pallas_call | solution.py:524
  32.6 3.0 %collective-permute-start.5 = (bf16[1,2,4,32,128]{4,3,2,1,0:T(8,128)(2,1)S(1)}, bf16[1,2,4,32,128]{4,3,2,1,0:T(8,128)(2,1)S(1)}, u32[]{:S(2)}, u32[]{:S(2)}) collective-permute-start(bf16[1,2,4,32,128]{4,3,2,1,0:T(8,128)(2,1)S(1)} %get-tuple-element.36), channel_id=1, source_target_pairs={{0,16},{4,20},{8,24},{12,28},{16,0},{20,4},{24,8},{28,12},{1,17},{... | collective-permute-start | bytes 196616 | tf_op jit(solution)/shard_map/ppermute | solution.py:507
  35.6 0.0 collective-permute-start.6
  35.6 1.5 %collective-permute-start.7 = (f32[8,128]{1,0:T(8,128)S(1)}, f32[8,128]{1,0:T(8,128)S(1)}, u32[]{:S(2)}, u32[]{:S(2)}) collective-permute-start(f32[8,128]{1,0:T(8,128)S(1)} %bitcast.21), channel_id=1, source_target_pairs={{0,2},{1,3},{2,0},{3,1},{4,6},{5,7},{6,4},{7,5},{8,10},{9,11},{10,... | collective-permute-start | bytes 12296 | tf_op jit(solution)/shard_map/ppermute | solution.py:537
  37.1 0.4 collective-permute-start.8
  37.5 0.0 collective-permute-done.received
  37.5 1.2 %shard_map.108 = (bf16[2,2,4,32,128]{4,3,2,1,0:T(8,128)(2,1)S(1)}, bf16[2,2,4,32,128]{4,3,2,1,0:T(8,128)(2,1)S(1)}) custom-call(s32[2,2,1024]{2,1,0:T(2,128)S(1)} %bitcast.15, s32[2,2,1024]{2,1,0:T(2,128)S(1)} %copy-done.7, bf16[2,48,32,128]{3,2,1,0:T(8,128)(2,1)S(1)} %get-tuple-element.31.mine, bf16[4,2,4,32,128]{4,3,2,1,0:T(8,128)(2,1)S(1)} %collective-permute-done.received), custom_call_target="tpu_custom_call" | custom-call | tf_op jit(solution)/shard_map/pallas_call | solution.py:524
  38.7 1.6 %collective-permute-start.3 = (bf16[2,2,4,32,128]{4,3,2,1,0:T(8,128)(2,1)S(1)}, bf16[2,2,4,32,128]{4,3,2,1,0:T(8,128)(2,1)S(1)}, u32[]{:S(2)}, u32[]{:S(2)}) collective-permute-start(bf16[2,2,4,32,128]{4,3,2,1,0:T(8,128)(2,1)S(1)} %get-tuple-element.39), channel_id=1, source_target_pairs={{0,8},{4,12},{8,0},{12,4},{16,24},{20,28},{24,16},{28,20},{1,9},{5... | collective-permute-start | bytes 393224 | tf_op jit(solution)/shard_map/ppermute | solution.py:507
  40.3 0.0 collective-permute-done.6.refs_1_
  40.3 0.0 collective-permute-done.7.refs_2_
  40.3 0.0 collective-permute-done.8.refs_3_
  40.4 0.0 collective-permute-done.5.received
  40.4 1.7 %shard_map.110 = (f32[32,4,128]{2,1,0:T(4,128)}, f32[4,32]{1,0:T(4,128)S(1)}, f32[32,128]{1,0:T(8,128)S(1)}) custom-call(bf16[1,2,4,32,128]{4,3,2,1,0:T(8,128)(2,1)S(1)} %get-tuple-element.44.kept, bf16[1,2,4,32,128]{4,3,2,1,0:T(8,128)(2,1)S(1)} %collective-permute-done.5.received, f32[8,128]{1,0:T(8,128)S(1)} %get-tuple-element.45.flags, ...), custom_call_target="tpu_custom_call" | custom-call | bytes 11070000 | tf_op jit(solution)/shard_map/pallas_call | solution.py:576
  42.0 5.9 %all-to-all-start = ((f32[32,4,128]{2,1,0:T(4,128)}), f32[32,4,128]{2,1,0:T(4,128)S(1)}, u32[]{:S(2)}, u32[]{:S(2)}) async-start(f32[32,4,128]{2,1,0:T(4,128)} %get-tuple-element.49), calls=%async_computation | async-start | bytes 131072 | tf_op jit(solution)/shard_map/all_to_all | solution.py:486
  48.0 0.0 collective-permute-done.3.received
  48.0 0.0 copy-done.8
  48.0 1.1 %shard_map.109 = (bf16[1,2,4,32,128]{4,3,2,1,0:T(8,128)(2,1)S(1)}, bf16[1,2,4,32,128]{4,3,2,1,0:T(8,128)(2,1)S(1)}, f32[8,128]{1,0:T(8,128)S(1)}) custom-call(s32[2,2,1024]{2,1,0:T(2,128)S(1)} %bitcast.16, s32[2,2,1024]{2,1,0:T(2,128)S(1)} %copy-done.8, bf16[2,2,4,32,128]{4,3,2,1,0:T(8,128)(2,1)S(1)} %get-tuple-element.38.mine, ...), custom_call_target="tpu_custom_call" | custom-call | tf_op jit(solution)/shard_map/pallas_call | solution.py:524
  49.1 7.1 %all-to-all-done = f32[32,4,128]{2,1,0:T(4,128)S(1)} async-done(((f32[32,4,128]{2,1,0:T(4,128)}), f32[32,4,128]{2,1,0:T(4,128)S(1)}, u32[]{:S(2)}, u32[]{:S(2)}) %all-to-all-start) | async-done | bytes 65568 | tf_op jit(solution)/shard_map/all_to_all | solution.py:486
  56.3 0.0 copy-done.3
  56.3 0.0 copy-done.12
  56.3 1.6 %shard_map.111 = f32[32,8,128]{2,1,0:T(8,128)} custom-call(s32[2,8]{1,0:T(2,128)S(1)} %bitcast.23, f32[8,4,4,128]{3,2,1,0:T(4,128)S(1)} %bitcast.18, bf16[8,2,128,128]{3,2,1,0:T(8,128)(2,1)S(1)} %copy-done.3), custom_call_target="tpu_custom_call" | custom-call | bytes 7380000 | tf_op jit(solution)/shard_map/pallas_call | solution.py:490
  57.9 2.6 %all-to-all-start.1 = ((f32[32,8,128]{2,1,0:T(8,128)}), f32[32,8,128]{2,1,0:T(8,128)S(1)}, u32[]{:S(2)}, u32[]{:S(2)}) async-start(f32[32,8,128]{2,1,0:T(8,128)} %shard_map.111), calls=%async_computation.1 | async-start | bytes 262144 | tf_op jit(solution)/shard_map/all_to_all | solution.py:586
  60.5 2.7 %collective-permute-start.4 = (bf16[1,2,4,32,128]{4,3,2,1,0:T(8,128)(2,1)S(1)}, bf16[1,2,4,32,128]{4,3,2,1,0:T(8,128)(2,1)S(1)}, u32[]{:S(2)}, u32[]{:S(2)}) collective-permute-start(bf16[1,2,4,32,128]{4,3,2,1,0:T(8,128)(2,1)S(1)} %get-tuple-element.41), channel_id=1, source_target_pairs={{0,16},{4,20},{8,24},{12,28},{16,0},{20,4},{24,8},{28,12},{1,17},{... | collective-permute-start | bytes 196616 | tf_op jit(solution)/shard_map/ppermute | solution.py:507
  63.2 9.5 %collective-permute-done.4.received = bf16[1,2,4,32,128]{4,3,2,1,0:T(8,128)(2,1)S(1)} collective-permute-done((bf16[1,2,4,32,128]{4,3,2,1,0:T(8,128)(2,1)S(1)}, bf16[1,2,4,32,128]{4,3,2,1,0:T(8,128)(2,1)S(1)}, u32[]{:S(2)}, u32[]{:S(2)}) %collective-permute-start.4) | collective-permute-done | bytes 65568 | tf_op jit(solution)/shard_map/ppermute | solution.py:507
  72.6 0.0 all-to-all-done.1
  72.6 1.7 %shard_map.112 = (f32[32,4,128]{2,1,0:T(4,128)}, f32[2,4,32]{2,1,0:T(4,128)}, f32[32,128]{1,0:T(8,128)S(1)}, f32[8,128]{1,0:T(8,128)S(1)}) custom-call(bf16[1,2,4,32,128]{4,3,2,1,0:T(8,128)(2,1)S(1)} %get-tuple-element.40.kept, bf16[1,2,4,32,128]{4,3,2,1,0:T(8,128)(2,1)S(1)} %collective-permute-done.4.received, f32[8,128]{1,0:T(8,128)S(1)} %get-tuple-element.42.flags, ...), custom_call_target="tpu_custom_call" | custom-call | bytes 11070000 | tf_op jit(solution)/shard_map/pallas_call | solution.py:589
  74.3 3.8 %all-to-all-start.2 = ((f32[32,4,128]{2,1,0:T(4,128)}), f32[32,4,128]{2,1,0:T(4,128)S(1)}, u32[]{:S(2)}, u32[]{:S(2)}) async-start(f32[32,4,128]{2,1,0:T(4,128)} %get-tuple-element.55), calls=%async_computation.2 | async-start | bytes 131072 | tf_op jit(solution)/shard_map/all_to_all | solution.py:486
  78.2 0.8 constant_dynamic-slice_fusion
  78.9 7.5 %all-to-all-done.2 = f32[32,4,128]{2,1,0:T(4,128)S(1)} async-done(((f32[32,4,128]{2,1,0:T(4,128)}), f32[32,4,128]{2,1,0:T(4,128)S(1)}, u32[]{:S(2)}, u32[]{:S(2)}) %all-to-all-start.2) | async-done | bytes 65568 | tf_op jit(solution)/shard_map/all_to_all | solution.py:486
  86.5 1.6 %shard_map.114 = f32[8,8,128]{2,1,0:T(8,128)} custom-call(s32[2,8]{1,0:T(2,128)S(1)} %bitcast.24, f32[8,4,4,128]{3,2,1,0:T(4,128)S(1)} %bitcast.17, bf16[8,2,128,128]{3,2,1,0:T(8,128)(2,1)S(1)} %copy-done.3), custom_call_target="tpu_custom_call" | custom-call | bytes 7380000 | tf_op jit(solution)/shard_map/pallas_call | solution.py:490
  88.0 3.3 %all-to-all-start.3 = ((f32[8,8,128]{2,1,0:T(8,128)}), f32[8,8,128]{2,1,0:T(8,128)S(1)}, u32[]{:S(2)}, u32[]{:S(2)}) async-start(f32[8,8,128]{2,1,0:T(8,128)} %shard_map.114), calls=%async_computation.3 | async-start | bytes 65536 | tf_op jit(solution)/shard_map/all_to_all | solution.py:599
  91.3 0.1 dynamic-slice_add_fusion
  91.4 0.1 reshape.31.places
  91.5 1.5 %all-gather.3.cloned.1.call-done = bf16[16,48,32,128]{3,2,1,0:T(8,128)(2,1)} async-done(((bf16[2,48,32,128]{3,2,1,0:T(8,128)(2,1)}), bf16[16,48,32,128]{3,2,1,0:T(8,128)(2,1)}) %all-gather.3.cloned.1.call-update) | async-done | bytes 6291472 | tf_op jit(solution)/shard_map/all_gather | solution.py:565
  93.0 0.0 copy-done.10
  93.0 5.7 %shard_map.113 = bf16[2,124,32,128]{3,2,1,0:T(8,128)(2,1)} custom-call(s32[496]{0:T(512)S(1)} %reshape.31.places, f32[32,128]{1,0:T(8,128)S(1)} %get-tuple-element.48.c_base.c_first, f32[32,128]{1,0:T(8,128)S(1)} %get-tuple-element.53.c_second, f32[144,128]{1,0:T(8,128)S(1)} %copy-done.10, bf16[768,32,128]{2,1,0:T(8,128)(2,1)} %bitcast.25), custom_call_target="tpu_custom_call" | custom-call | flops 8126464 | bytes 8323072 | tf_op jit(solution)/shard_map/pallas_call | solution.py:600
  98.7 0.0 all-to-all-done.3
  98.7 0.6 add_bitcast_fusion
  (9 shorter events, 0.0 us)
Async XLA Ops:
  7.2 85.9 %all-gather.3.cloned.1.call-start = ((), (), s32[]{:S(2)}) async-start(), calls=%async_computation.4 | async-start | bytes 7077888 | tf_op jit(solution)/shard_map/all_gather | solution.py:565
  7.2 1.1 %copy-start = (bf16[2,48,32,128]{3,2,1,0:T(8,128)(2,1)S(1)}, bf16[2,48,32,128]{3,2,1,0:T(8,128)(2,1)}, u32[]{:S(2)}) copy-start(bf16[2,48,32,128]{3,2,1,0:T(8,128)(2,1)} %refs_3_.1) | copy-start | bytes 2359300
  8.3 0.7 copy-start.5
  9.1 38.9 %copy-start.8 = (s32[2,2,1024]{2,1,0:T(2,128)S(1)}, s32[2,2,1024]{2,1,0:T(2,128)}, u32[]{:S(2)}) copy-start(s32[2,2,1024]{2,1,0:T(2,128)} %slots.11) | copy-start | bytes 49156
  9.1 47.2 %copy-start.3 = (bf16[8,2,128,128]{3,2,1,0:T(8,128)(2,1)S(1)}, bf16[8,2,128,128]{3,2,1,0:T(8,128)(2,1)}, u32[]{:S(2)}) copy-start(bf16[8,2,128,128]{3,2,1,0:T(8,128)(2,1)} %blocks.3) | copy-start | bytes 1572868
  9.1 47.2 %copy-start.12 = (s32[8,2]{0,1:T(2,128)S(1)}, s32[8,2]{0,1:T(2,128)}, u32[]{:S(2)}) copy-start(s32[8,2]{0,1:T(2,128)} %param.13) | copy-start | bytes 196
  9.1 84.0 %copy-start.10 = (f32[144,128]{1,0:T(8,128)S(1)}, f32[144,128]{1,0:T(8,128)}, u32[]{:S(2)}) copy-start(f32[144,128]{1,0:T(8,128)} %constant.58.clone.refs_0_.mirror) | copy-start | bytes 221188
  10.0 10.8 %collective-permute-start.1 = (bf16[4,2,4,32,128]{4,3,2,1,0:T(8,128)(2,1)S(1)}, bf16[4,2,4,32,128]{4,3,2,1,0:T(8,128)(2,1)S(1)}, u32[]{:S(2)}, u32[]{:S(2)}) collective-permute-start(bf16[4,2,4,32,128]{4,3,2,1,0:T(8,128)(2,1)S(1)} %shard_map.103), channel_id=1, source_target_pairs={{0,4},{4,0},{8,12},{12,8},{16,20},{20,16},{24,28},{28,24},{1,5},{5... | collective-permute-start | bytes 786440 | tf_op jit(solution)/shard_map/ppermute | solution.py:507
  13.0 1.1 %copy-start.1 = (bf16[2,48,32,128]{3,2,1,0:T(8,128)(2,1)S(1)}, bf16[2,48,32,128]{3,2,1,0:T(8,128)(2,1)}, u32[]{:S(2)}) copy-start(bf16[2,48,32,128]{3,2,1,0:T(8,128)(2,1)} %refs_3_.1) | copy-start | bytes 2359300
  14.1 0.7 copy-start.6
  15.7 21.8 %collective-permute-start = (bf16[4,2,4,32,128]{4,3,2,1,0:T(8,128)(2,1)S(1)}, bf16[4,2,4,32,128]{4,3,2,1,0:T(8,128)(2,1)S(1)}, u32[]{:S(2)}, u32[]{:S(2)}) collective-permute-start(bf16[4,2,4,32,128]{4,3,2,1,0:T(8,128)(2,1)S(1)} %shard_map.104.refs_4_), channel_id=1, source_target_pairs={{0,4},{4,0},{8,12},{12,8},{16,20},{20,16},{24,28},{28,24},{1,5},{5... | collective-permute-start | bytes 786440 | tf_op jit(solution)/shard_map/ppermute | solution.py:507
  16.6 1.1 %copy-start.2 = (bf16[2,48,32,128]{3,2,1,0:T(8,128)(2,1)S(1)}, bf16[2,48,32,128]{3,2,1,0:T(8,128)(2,1)}, u32[]{:S(2)}) copy-start(bf16[2,48,32,128]{3,2,1,0:T(8,128)(2,1)} %refs_3_.1) | copy-start | bytes 2359300
  17.7 1.1 %copy-start.4 = (bf16[1296,256]{1,0:T(8,128)(2,1)S(1)}, bf16[1296,256]{1,0:T(8,128)(2,1)}, u32[]{:S(2)}) copy-start(bf16[1296,256]{1,0:T(8,128)(2,1)} %constant.57.clone.refs_1_) | copy-start | bytes 1990660
  18.8 0.9 copy-start.9
  19.7 0.7 copy-start.11
  20.8 0.7 copy-start.7
  22.7 8.8 %collective-permute-start.2 = (bf16[2,2,4,32,128]{4,3,2,1,0:T(8,128)(2,1)S(1)}, bf16[2,2,4,32,128]{4,3,2,1,0:T(8,128)(2,1)S(1)}, u32[]{:S(2)}, u32[]{:S(2)}) collective-permute-start(bf16[2,2,4,32,128]{4,3,2,1,0:T(8,128)(2,1)S(1)} %get-tuple-element.35), channel_id=1, source_target_pairs={{0,8},{4,12},{8,0},{12,4},{16,24},{20,28},{24,16},{28,20},{1,9},{5... | collective-permute-start | bytes 393224 | tf_op jit(solution)/shard_map/ppermute | solution.py:507
  32.6 7.7 %collective-permute-start.5 = (bf16[1,2,4,32,128]{4,3,2,1,0:T(8,128)(2,1)S(1)}, bf16[1,2,4,32,128]{4,3,2,1,0:T(8,128)(2,1)S(1)}, u32[]{:S(2)}, u32[]{:S(2)}) collective-permute-start(bf16[1,2,4,32,128]{4,3,2,1,0:T(8,128)(2,1)S(1)} %get-tuple-element.36), channel_id=1, source_target_pairs={{0,16},{4,20},{8,24},{12,28},{16,0},{20,4},{24,8},{28,12},{1,17},{... | collective-permute-start | bytes 196616 | tf_op jit(solution)/shard_map/ppermute | solution.py:507
  35.6 4.7 %collective-permute-start.6 = (f32[8,128]{1,0:T(8,128)S(1)}, f32[8,128]{1,0:T(8,128)S(1)}, u32[]{:S(2)}, u32[]{:S(2)}) collective-permute-start(f32[8,128]{1,0:T(8,128)S(1)} %bitcast.20), channel_id=1, source_target_pairs={{0,1},{1,0},{2,3},{3,2},{4,5},{5,4},{6,7},{7,6},{8,9},{9,8},{10,11... | collective-permute-start | bytes 12296 | tf_op jit(solution)/shard_map/ppermute | solution.py:537
  35.6 4.7 %collective-permute-start.7 = (f32[8,128]{1,0:T(8,128)S(1)}, f32[8,128]{1,0:T(8,128)S(1)}, u32[]{:S(2)}, u32[]{:S(2)}) collective-permute-start(f32[8,128]{1,0:T(8,128)S(1)} %bitcast.21), channel_id=1, source_target_pairs={{0,2},{1,3},{2,0},{3,1},{4,6},{5,7},{6,4},{7,5},{8,10},{9,11},{10,... | collective-permute-start | bytes 12296 | tf_op jit(solution)/shard_map/ppermute | solution.py:537
  37.1 3.2 %collective-permute-start.8 = (f32[8,128]{1,0:T(8,128)S(1)}, f32[8,128]{1,0:T(8,128)S(1)}, u32[]{:S(2)}, u32[]{:S(2)}) collective-permute-start(f32[8,128]{1,0:T(8,128)S(1)} %bitcast.22), channel_id=1, source_target_pairs={{0,3},{1,2},{2,1},{3,0},{4,7},{5,6},{6,5},{7,4},{8,11},{9,10},{10,... | collective-permute-start | bytes 12296 | tf_op jit(solution)/shard_map/ppermute | solution.py:537
  38.7 9.3 %collective-permute-start.3 = (bf16[2,2,4,32,128]{4,3,2,1,0:T(8,128)(2,1)S(1)}, bf16[2,2,4,32,128]{4,3,2,1,0:T(8,128)(2,1)S(1)}, u32[]{:S(2)}, u32[]{:S(2)}) collective-permute-start(bf16[2,2,4,32,128]{4,3,2,1,0:T(8,128)(2,1)S(1)} %get-tuple-element.39), channel_id=1, source_target_pairs={{0,8},{4,12},{8,0},{12,4},{16,24},{20,28},{24,16},{28,20},{1,9},{5... | collective-permute-start | bytes 393224 | tf_op jit(solution)/shard_map/ppermute | solution.py:507
  42.0 14.2 %all-to-all-start = ((f32[32,4,128]{2,1,0:T(4,128)}), f32[32,4,128]{2,1,0:T(4,128)S(1)}, u32[]{:S(2)}, u32[]{:S(2)}) async-start(f32[32,4,128]{2,1,0:T(4,128)} %get-tuple-element.49), calls=%async_computation | async-start | bytes 131072 | tf_op jit(solution)/shard_map/all_to_all | solution.py:486
  57.9 14.8 %all-to-all-start.1 = ((f32[32,8,128]{2,1,0:T(8,128)}), f32[32,8,128]{2,1,0:T(8,128)S(1)}, u32[]{:S(2)}, u32[]{:S(2)}) async-start(f32[32,8,128]{2,1,0:T(8,128)} %shard_map.111), calls=%async_computation.1 | async-start | bytes 262144 | tf_op jit(solution)/shard_map/all_to_all | solution.py:586
  60.5 12.2 %collective-permute-start.4 = (bf16[1,2,4,32,128]{4,3,2,1,0:T(8,128)(2,1)S(1)}, bf16[1,2,4,32,128]{4,3,2,1,0:T(8,128)(2,1)S(1)}, u32[]{:S(2)}, u32[]{:S(2)}) collective-permute-start(bf16[1,2,4,32,128]{4,3,2,1,0:T(8,128)(2,1)S(1)} %get-tuple-element.41), channel_id=1, source_target_pairs={{0,16},{4,20},{8,24},{12,28},{16,0},{20,4},{24,8},{28,12},{1,17},{... | collective-permute-start | bytes 196616 | tf_op jit(solution)/shard_map/ppermute | solution.py:507
  74.3 12.1 %all-to-all-start.2 = ((f32[32,4,128]{2,1,0:T(4,128)}), f32[32,4,128]{2,1,0:T(4,128)S(1)}, u32[]{:S(2)}, u32[]{:S(2)}) async-start(f32[32,4,128]{2,1,0:T(4,128)} %get-tuple-element.55), calls=%async_computation.2 | async-start | bytes 131072 | tf_op jit(solution)/shard_map/all_to_all | solution.py:486
  88.0 10.7 %all-to-all-start.3 = ((f32[8,8,128]{2,1,0:T(8,128)}), f32[8,8,128]{2,1,0:T(8,128)S(1)}, u32[]{:S(2)}, u32[]{:S(2)}) async-start(f32[8,8,128]{2,1,0:T(8,128)} %shard_map.114), calls=%async_computation.3 | async-start | bytes 65536 | tf_op jit(solution)/shard_map/all_to_all | solution.py:599
Sparse Core Ops, SparseCore 0:
  10.1 82.8 all-gather.2
